TPU v7x, 32 devices: a whole 2x2x4 slice. The times are simulated.
32 devices in a mesh: src: 16 (over z, y, x), ccd: 2 (over core).
Axes of the slice: x: 2, y: 2, z: 4, core: 2. Of those that a mesh axis runs over, the one named last changes fastest.
Arguments:
- design: float32 [5, 262144], P(None, ('src', 'ccd')), may hold values from -6 to 6
- observed: float32 [262144], P(('src', 'ccd')), may hold values from -12 to 12
- weight: float32 [262144], P(('src', 'ccd')), may hold values from 0.25 to 4
- phase_frac: float32 [262144], P(('src', 'ccd')), may hold values from 0 to 1
- axis_factors: float32 [3, 262144], P(None, ('src', 'ccd')), may hold values from -6 to 6
- source_index: int32 [262144], P(('src', 'ccd')), may hold values from 0 to 1023
- knot_index: int32 [262144], P(('src', 'ccd')), may hold values from 0 to 127
- counts: int32 [16, 2, 16], P('src', 'ccd'), may hold values from 1 to 512, as said below
Outputs:
- source_params: float32 [5, 16384], P(None, 'src')
- attitude: float32 [3, 2048], P(None, 'src')
- residual: float32 [262144], P(('src', 'ccd'))
Inputs may be any that keep to these rules, and one draw needn't show every extreme that they name: Slot l of device (p, c) is live when l % 512 < counts[p, c, l // 512]; every device has one full block of 512 live slots, and one time shard receives full blocks from every device.
All inputs are finite; a program needn't handle non-finite values.
Results may differ from a plain program's by a relative error of at most 0.0003.
Values sent between devices are 32-bit elements; how exact they have to be, the bound alone decides.
No kernel may reach another device: no remote copies, remote signals or barrier semaphores. Data moves between devices by JAX's collectives and lax.ppermute only.
A program may use at most 64 MiB of HBM per device.

v0:
```python
import math

import jax
import jax.numpy as jnp
from jax import lax
from jax.sharding import PartitionSpec as P

SRC_DEV = 1024
KNOT_DEV = 128
ITERS = 3


src_ridge = 1.0
att_ridge = 1.0
relax_step = 0.15


def passed_along(block, axis, distance):
    devices = range(lax.axis_size(axis))
    route = [(i - distance, i) for i in devices if i - distance in devices]
    return lax.ppermute(block, axis, route)


def row_moments(design_rows, observed_rows, weight_rows):
    products = []
    for m in range(5):
        for n in range(m, 5):
            products.append(design_rows[m] * design_rows[n] * weight_rows)
    for m in range(5):
        products.append(design_rows[m] * weight_rows * observed_rows)
    return jnp.stack(products)


def solve_small(moments):
    matrix = {}
    position = 0
    for m in range(5):
        for n in range(m, 5):
            matrix[m, n] = moments[position] + (src_ridge if m == n else 0.0)
            position += 1
    factor = {}
    for j in range(5):
        for i in range(j, 5):
            running = matrix[j, i]
            for k in range(j):
                running = running - factor[i, k] * factor[j, k]
            if i == j:
                factor[j, j] = jnp.sqrt(running)
            else:
                factor[i, j] = running / factor[j, j]
    forward = []
    for i in range(5):
        running = moments[15 + i]
        for k in range(i):
            running = running - factor[i, k] * forward[k]
        forward.append(running / factor[i, i])
    solution = [None] * 5
    for i in reversed(range(5)):
        running = forward[i]
        for k in range(i + 1, 5):
            running = running - factor[k, i] * solution[k]
        solution[i] = running / factor[i, i]
    return jnp.stack(solution)


def spline_basis(phase_rows):
    remain = 1.0 - phase_rows
    square = phase_rows * phase_rows
    cube_term = square * phase_rows
    return [
        remain * remain * remain / 6.0,
        (3.0 * cube_term - 6.0 * square + 4.0) / 6.0,
        (-3.0 * cube_term + 3.0 * square + 3.0 * phase_rows + 1.0) / 6.0,
        cube_term / 6.0,
    ]


def spread_knots(row_values, spline_terms, knot_rows, knot_count):
    row_count = knot_rows.shape[0]
    block_rows = math.gcd(row_count, 2048)
    stacked = jnp.concatenate([row_values * factor_row for factor_row in spline_terms], 0)
    blocked = stacked.reshape(12, row_count // block_rows, block_rows).transpose(1, 0, 2)
    knot_blocks = knot_rows.reshape(row_count // block_rows, block_rows)
    columns = lax.iota(jnp.int32, knot_count)

    def add_block(carried, scan_items):
        values_blk, knots_blk = scan_items
        onehot = (knots_blk[:, None] == columns[None, :]).astype(jnp.float32)
        return (carried + jnp.dot(values_blk, onehot, precision=lax.Precision.HIGHEST), None)

    knot_sums, _ = lax.scan(
        add_block, jnp.zeros((12, knot_count), jnp.float32), (blocked, knot_blocks)
    )
    return sum((jnp.pad(knot_sums[3 * j : 3 * j + 3], ((0, 0), (j, 3 - j))) for j in range(4)))


def predict_rows(extended, spline_terms, axis_rows, knot_rows, knot_count):
    row_count = knot_rows.shape[0]
    block_rows = math.gcd(row_count, 2048)
    windows = jnp.concatenate([extended[:, j : j + knot_count] for j in range(4)], 0)
    knot_blocks = knot_rows.reshape(row_count // block_rows, block_rows)
    columns = lax.iota(jnp.int32, knot_count)

    def pick_block(carried, knots_blk):
        onehot = (knots_blk[:, None] == columns[None, :]).astype(jnp.float32)
        return (
            carried,
            lax.dot_general(
                windows, onehot, (((1,), (1,)), ((), ())), precision=lax.Precision.HIGHEST
            ),
        )

    _, picked = lax.scan(pick_block, jnp.zeros((), jnp.int32), knot_blocks)
    picked = picked.transpose(1, 0, 2).reshape(12, row_count)
    running = jnp.zeros_like(spline_terms[0])
    for j in range(4):
        running = running + spline_terms[j] * jnp.sum(axis_rows * picked[3 * j : 3 * j + 3], 0)
    return running


def knot_assemble(partial_sums):
    summed = lax.psum(partial_sums, "ccd")
    spill_cols = passed_along(summed[:, -3:], "src", 1)
    return summed[:, :-3] + jnp.pad(spill_cols, ((0, 0), (0, summed.shape[1] - 6)))


def extend_edge(coefficients):
    edge_cols = passed_along(coefficients[:, :3], "src", -1)
    return jnp.concatenate([coefficients, edge_cols], 1)


def on_device(design, observed, weight, phase_frac, axis_factors, source_index, knot_index, counts):
    row_count = observed.shape[0]
    shards = lax.axis_size("src")
    cap_rows = row_count // shards
    knot_count = KNOT_DEV
    local_row = lax.iota(jnp.int32, row_count)
    bucket = local_row // cap_rows
    slot_pos = (local_row % cap_rows).reshape(shards, cap_rows)
    live_mask = (slot_pos < counts[0, 0][:, None]).astype(jnp.float32).reshape(row_count)
    weight_live = weight * live_mask
    static_rows = jnp.concatenate(
        [weight_live[None], phase_frac[None], axis_factors, knot_index.astype(jnp.float32)[None]], 0
    )
    moments = jax.ops.segment_sum(
        row_moments(design, observed, weight_live).T, source_index, num_segments=SRC_DEV
    ).T
    share_sums = lax.psum_scatter(moments, "ccd", scatter_dimension=1, tiled=True)
    params = lax.all_gather(solve_small(share_sums), "ccd", axis=1, tiled=True)
    fitted = jnp.sum(design * jnp.take(params, source_index, axis=1), 0)
    params, resid_rows = (params, live_mask * (observed - fitted))
    arrived = lax.all_to_all(
        jnp.concatenate([resid_rows[None], static_rows], 0),
        "src",
        split_axis=1,
        concat_axis=1,
        tiled=True,
    )
    resid_in = arrived[0]
    static_in = arrived[1:]
    weight_in = static_in[0]
    spline_in = spline_basis(static_in[1])
    factor_in = static_in[2:5]
    knot_in = static_in[5].astype(jnp.int32)
    rhs_part = spread_knots(weight_in * factor_in * resid_in, spline_in, knot_in, knot_count)
    diag_part = spread_knots(
        weight_in * factor_in * factor_in, [t * t for t in spline_in], knot_in, knot_count
    )
    totals = knot_assemble(jnp.concatenate([rhs_part, diag_part], 0))
    rhs_knots = totals[:3]
    diag_knots = att_ridge + totals[3:]
    coefficients = relax_step * rhs_knots / diag_knots
    for iteration in range(1, ITERS):
        predicted = predict_rows(
            extend_edge(coefficients), spline_in, factor_in, knot_in, knot_count
        )
        back_sums = knot_assemble(
            spread_knots(weight_in * factor_in * predicted, spline_in, knot_in, knot_count)
        )
        normal_prod = att_ridge * coefficients + back_sums
        coefficients = coefficients + relax_step * (rhs_knots - normal_prod) / diag_knots
    whole_coefs = jnp.pad(lax.all_gather(coefficients, "src", axis=1, tiled=True), ((0, 0), (0, 3)))
    global_knot = bucket * knot_count + knot_index
    spline_own = spline_basis(phase_frac)
    predicted = jnp.zeros_like(observed)
    for j in range(4):
        predicted = predicted + spline_own[j] * jnp.sum(
            axis_factors * jnp.take(whole_coefs, global_knot + j, axis=1), 0
        )
    residual = live_mask * (resid_rows - predicted)
    return (params, coefficients, residual)


def solution(mesh):
    in_specs = (
        P(None, ("src", "ccd")),
        P(("src", "ccd")),
        P(("src", "ccd")),
        P(("src", "ccd")),
        P(None, ("src", "ccd")),
        P(("src", "ccd")),
        P(("src", "ccd")),
        P("src", "ccd", None),
    )
    out_specs = (P(None, "src"), P(None, "src"), P(("src", "ccd")))
    return jax.shard_map(
        on_device, mesh=mesh, in_specs=in_specs, out_specs=out_specs, check_vma=False
    )
```

profile of v0, /device:TPU:0, one launch (start us, length us, event | category | flops | bytes accessed | tf_op | source)
XLA Modules:
  0.0 357.8 jit_solution(4224753279794439122)
XLA Ops:
  12.5 2.6 copy.152
  15.1 44.4 %scatter_custom_fusion = f32[1024,20]{1,0:T(8,128)S(1)} fusion(s32[8192]{0:T(1024)S(1)} %copy-done.4, f32[8192,20]{1,0:T(8,128)} %copy.152, f32[]{:T(128)} %constant.121.clone.1), kind=kCustom, calls=%fused_computation.60 | custom fusion | flops 163840 | bytes 82432 | tf_op jit(solution)/shard_map/scatter-add | solution.py:145
  63.2 7.7 %reduce-scatter.2.cloned.1.call-done = f32[20,512]{1,0:T(8,128)} async-done(((f32[20,1024]{1,0:T(8,128)}), f32[20,512]{1,0:T(8,128)}) %reduce-scatter.2.cloned.1.call-update) | async-done | bytes 40976 | tf_op jit(solution)/shard_map/reduce_scatter | solution.py:148
  76.0 27.7 %gather_fusion = f32[8192,5]{1,0:T(8,128)} fusion(f32[5,1024]{0,1:T(8,128)S(1)} %copy.154, s32[8192]{0:T(1024)S(1)} %fusion.61), kind=kCustom, calls=%fused_computation.4 | custom fusion | bytes 360448 | tf_op jit(solution)/shard_map/jit(_take)/gather | solution.py:150
  103.7 5.2 %fusion.24 = f32[8192]{0:T(1024)S(1)} fusion(f32[5,8192]{0,1:T(8,128)} %copy.155, f32[8192,5]{1,0:T(8,128)} %gather_fusion, pred[8192]{0:T(1024)(128)(4,1)S(1)} %compare_and_fusion.4), kind=kLoop, calls=%fused_computation.55 | loop fusion | flops 114688 | bytes 368640 | tf_op jit(solution)/shard_map/reduce_sum | solution.py:150
  109.9 6.7 %all-to-all-start = ((f32[7,16,512]{2,0,1:T(8,128)}), f32[7,16,512]{2,0,1:T(8,128)S(1)}, u32[]{:S(2)}, u32[]{:S(2)}) async-start(f32[7,16,512]{2,0,1:T(8,128)} %concatenate.50), calls=%async_computation.1 | async-start | bytes 524288 | tf_op jit(solution)/shard_map/all_to_all | solution.py:152
  119.3 7.7 %all-to-all-done = f32[7,16,512]{2,0,1:T(8,128)S(1)} async-done(((f32[7,16,512]{2,0,1:T(8,128)}), f32[7,16,512]{2,0,1:T(8,128)S(1)}, u32[]{:S(2)}, u32[]{:S(2)}) %all-to-all-start) | async-done | bytes 229408 | tf_op jit(solution)/shard_map/all_to_all | solution.py:152
  128.2 3.0 while.68
  131.2 3.0 while.69
  136.8 2.7 collective-permute-start
  142.1 4.4 %collective-permute-done.1 = f32[3,3]{1,0:T(4,128)S(1)} collective-permute-done((f32[3,3]{1,0:T(4,128)S(1)}, f32[3,3]{1,0:T(4,128)S(1)}, u32[]{:S(2)}, u32[]{:S(2)}) %collective-permute-start.1) | collective-permute-done | bytes 68 | tf_op jit(solution)/shard_map/ppermute | solution.py:21
  146.8 3.9 %while.66 = (s32[]{:T(128)}, f32[4,12,2048]{2,1,0:T(8,128)S(1)}, s32[4,2048]{1,0:T(4,128)S(1)}, f32[12,128]{1,0:T(8,128)S(1)}, s32[]{:T(128)}) while((s32[]{:T(128)}, f32[4,12,2048]{2,1,0:T(8,128)S(1)}, s32[4,2048]{1,0:T(4,128)S(1)}, f32[12,128]{1,0:T(8,128)S(1)}, s32[]{:T(128)}) %tuple.256), condition=%wide.region_9.10_spmd.clone, body=%wide.region_8.9_spmd.clone.sunk | while | flops 38010880 | bytes 163917 | solution.py:113
  151.8 3.0 while.70
  157.3 4.8 %collective-permute-start.2 = (f32[3,3]{1,0:T(4,128)S(1)}, f32[3,3]{1,0:T(4,128)S(1)}, u32[]{:S(2)}, u32[]{:S(2)}) collective-permute-start(f32[3,3]{1,0:T(4,128)S(1)} %slice.404), channel_id=1, source_target_pairs={{0,2},{2,4},{4,6},{6,8},{8,10},{10,12},{12,14},{14,16},{16,18},{18... | collective-permute-start | bytes 116 | tf_op jit(solution)/shard_map/ppermute | solution.py:21
  164.9 4.3 %collective-permute-done.3 = f32[3,3]{1,0:T(4,128)S(1)} collective-permute-done((f32[3,3]{1,0:T(4,128)S(1)}, f32[3,3]{1,0:T(4,128)S(1)}, u32[]{:S(2)}, u32[]{:S(2)}) %collective-permute-start.3) | collective-permute-done | bytes 68 | tf_op jit(solution)/shard_map/ppermute | solution.py:21
  169.4 3.9 %while.67 = (s32[]{:T(128)}, f32[4,12,2048]{2,1,0:T(8,128)S(1)}, s32[4,2048]{1,0:T(4,128)S(1)}, f32[12,128]{1,0:T(8,128)S(1)}, s32[]{:T(128)}) while((s32[]{:T(128)}, f32[4,12,2048]{2,1,0:T(8,128)S(1)}, s32[4,2048]{1,0:T(4,128)S(1)}, f32[12,128]{1,0:T(8,128)S(1)}, s32[]{:T(128)}) %tuple.258), condition=%wide.region_18.19_spmd.clone, body=%wide.region_17.18_spmd.clone.sunk | while | flops 38010880 | bytes 163917 | solution.py:113
  174.4 3.0 while.71
  179.9 4.8 %collective-permute-start.4 = (f32[3,3]{1,0:T(4,128)S(1)}, f32[3,3]{1,0:T(4,128)S(1)}, u32[]{:S(2)}, u32[]{:S(2)}) collective-permute-start(f32[3,3]{1,0:T(4,128)S(1)} %slice.414), channel_id=1, source_target_pairs={{0,2},{2,4},{4,6},{6,8},{8,10},{10,12},{12,14},{14,16},{16,18},{18... | collective-permute-start | bytes 116 | tf_op jit(solution)/shard_map/ppermute | solution.py:21
  186.0 38.7 %all_gather.7 = f32[3,2048]{1,0:T(4,128)S(1)} all-gather(f32[3,128]{1,0:T(4,128)S(1)} %fusion.77), channel_id=1, replica_groups=mesh['src'=16,'ccd'=2] {'src'}, dimensions={1}, use_global_device_ids=true | all-gather | bytes 26112 | tf_op jit(solution)/shard_map/all_gather | solution.py:182
  225.2 27.7 %gather_fusion.4 = f32[8192,3]{1,0:T(8,128)} fusion(f32[3,2051]{0,1:T(8,128)S(1)} %pad.86.clone, s32[8192]{0:T(1024)S(1)} %get-tuple-element.490), kind=kCustom, calls=%fused_computation.3.clone | custom fusion | bytes 229376 | tf_op jit(solution)/shard_map/jit(_take)/gather | solution.py:188
  252.9 27.7 %gather_fusion.3 = f32[8192,3]{1,0:T(8,128)} fusion(f32[3,2051]{0,1:T(8,128)S(1)} %pad.86.clone, s32[8192]{0:T(1024)S(1)} %get-tuple-element.491), kind=kCustom, calls=%fused_computation.2.clone | custom fusion | bytes 229376 | tf_op jit(solution)/shard_map/jit(_take)/gather | solution.py:188
  280.6 27.7 %gather_fusion.2 = f32[8192,3]{1,0:T(8,128)} fusion(f32[3,2051]{0,1:T(8,128)S(1)} %pad.86.clone, s32[8192]{0:T(1024)S(1)} %get-tuple-element.492), kind=kCustom, calls=%fused_computation.1.clone | custom fusion | bytes 229376 | tf_op jit(solution)/shard_map/jit(_take)/gather | solution.py:188
  308.3 27.7 %gather_fusion.1 = f32[8192,3]{1,0:T(8,128)} fusion(f32[3,2051]{0,1:T(8,128)S(1)} %pad.86.clone, s32[8192]{0:T(1024)S(1)} %get-tuple-element.489), kind=kCustom, calls=%fused_computation.clone | custom fusion | bytes 229376 | tf_op jit(solution)/shard_map/jit(_take)/gather | solution.py:188
  336.0 13.6 %fusion.20 = (f32[8192]{0:T(1024)S(1)}, f32[8192]{0:T(1024)S(1)}, f32[8192]{0:T(1024)S(1)}, f32[8192]{0:T(1024)S(1)}) fusion(f32[3,8192]{0,1:T(8,128)} %copy.170, f32[8192,3]{1,0:T(8,128)} %gather_fusion.4, pred[8192]{0:T(1024)(128)(4,1)S(1)} %get-tuple-element.488, f32[8192,3]{1,0:T(8,128)} %gather_fusion.3, pred[8192]{0:T(1024)(128)(4,1)S(1)} %get-tuple-element.487, ...), kind=kLoop, calls=%fused_computation.47 | loop fusion | flops 262144 | bytes 655360 | tf_op jit(solution)/shard_map/reduce_sum | solution.py:187
  (187 shorter events, 55.9 us)
Async XLA Ops:
  7.2 0.7 copy-start
  7.2 8.0 %copy-start.4 = (s32[8192]{0:T(1024)S(1)}, s32[8192]{0:T(1024)}, u32[]{:S(2)}) copy-start(s32[8192]{0:T(1024)} %param.27) | copy-start | bytes 98308
  7.2 63.7 %reduce-scatter.2.cloned.1.call-start = ((), (), s32[]{:S(2)}) async-start(), calls=%async_computation.2 | async-start | bytes 147456 | tf_op jit(solution)/shard_map/reduce_scatter | solution.py:148
  10.6 49.8 %copy-start.1 = (f32[5,8192]{1,0:T(8,128)S(1)}, f32[5,8192]{1,0:T(8,128)}, u32[]{:S(2)}) copy-start(f32[5,8192]{1,0:T(8,128)} %param.22) | copy-start | bytes 491524
  12.5 50.6 %copy-start.5 = (s32[8192]{0:T(1024)S(1)}, s32[8192]{0:T(1024)}, u32[]{:S(2)}) copy-start(s32[8192]{0:T(1024)} %param.28) | copy-start | bytes 98308
  103.7 5.2 %copy-start.3 = (f32[8192]{0:T(1024)S(1)}, f32[8192]{0:T(1024)}, u32[]{:S(2)}) copy-start(f32[8192]{0:T(1024)} %param.23) | copy-start | bytes 98308
  103.7 5.2 %copy-start.2 = (f32[3,8192]{1,0:T(4,128)S(1)}, f32[3,8192]{1,0:T(4,128)}, u32[]{:S(2)}) copy-start(f32[3,8192]{1,0:T(4,128)} %param.26) | copy-start | bytes 294916
  103.7 5.2 %copy-start.6 = (f32[8192]{0:T(1024)S(1)}, f32[8192]{0:T(1024)}, u32[]{:S(2)}) copy-start(f32[8192]{0:T(1024)} %param.25) | copy-start | bytes 98308
  109.9 17.1 %all-to-all-start = ((f32[7,16,512]{2,0,1:T(8,128)}), f32[7,16,512]{2,0,1:T(8,128)S(1)}, u32[]{:S(2)}, u32[]{:S(2)}) async-start(f32[7,16,512]{2,0,1:T(8,128)} %concatenate.50), calls=%async_computation.1 | async-start | bytes 524288 | tf_op jit(solution)/shard_map/all_to_all | solution.py:152
  136.8 4.0 %collective-permute-start = (f32[6,3]{1,0:T(8,128)S(1)}, f32[6,3]{1,0:T(8,128)S(1)}, u32[]{:S(2)}, u32[]{:S(2)}) collective-permute-start(f32[6,3]{1,0:T(8,128)S(1)} %slice.394), channel_id=1, source_target_pairs={{0,2},{2,4},{4,6},{6,8},{8,10},{10,12},{12,14},{14,16},{16,18},{18... | collective-permute-start | bytes 224 | tf_op jit(solution)/shard_map/ppermute | solution.py:21
  140.8 5.7 %collective-permute-start.1 = (f32[3,3]{1,0:T(4,128)S(1)}, f32[3,3]{1,0:T(4,128)S(1)}, u32[]{:S(2)}, u32[]{:S(2)}) collective-permute-start(f32[3,3]{1,0:T(4,128)S(1)} %bitcast.172), channel_id=1, source_target_pairs={{2,0},{4,2},{6,4},{8,6},{10,8},{12,10},{14,12},{16,14},{18,16},{20... | collective-permute-start | bytes 116 | tf_op jit(solution)/shard_map/ppermute | solution.py:21
  157.3 6.1 %collective-permute-start.2 = (f32[3,3]{1,0:T(4,128)S(1)}, f32[3,3]{1,0:T(4,128)S(1)}, u32[]{:S(2)}, u32[]{:S(2)}) collective-permute-start(f32[3,3]{1,0:T(4,128)S(1)} %slice.404), channel_id=1, source_target_pairs={{0,2},{2,4},{4,6},{6,8},{8,10},{10,12},{12,14},{14,16},{16,18},{18... | collective-permute-start | bytes 116 | tf_op jit(solution)/shard_map/ppermute | solution.py:21
  163.4 5.7 %collective-permute-start.3 = (f32[3,3]{1,0:T(4,128)S(1)}, f32[3,3]{1,0:T(4,128)S(1)}, u32[]{:S(2)}, u32[]{:S(2)}) collective-permute-start(f32[3,3]{1,0:T(4,128)S(1)} %bitcast.171), channel_id=1, source_target_pairs={{2,0},{4,2},{6,4},{8,6},{10,8},{12,10},{14,12},{16,14},{18,16},{20... | collective-permute-start | bytes 116 | tf_op jit(solution)/shard_map/ppermute | solution.py:21
  179.9 6.1 %collective-permute-start.4 = (f32[3,3]{1,0:T(4,128)S(1)}, f32[3,3]{1,0:T(4,128)S(1)}, u32[]{:S(2)}, u32[]{:S(2)}) collective-permute-start(f32[3,3]{1,0:T(4,128)S(1)} %slice.414), channel_id=1, source_target_pairs={{0,2},{2,4},{4,6},{6,8},{8,10},{10,12},{12,14},{14,16},{16,18},{18... | collective-permute-start | bytes 116 | tf_op jit(solution)/shard_map/ppermute | solution.py:21
  186.0 163.7 %copy-start.7 = (f32[3,128]{1,0:T(4,128)}, f32[3,128]{1,0:T(4,128)S(1)}, u32[]{:S(2)}) copy-start(f32[3,128]{1,0:T(4,128)S(1)} %fusion.77) | copy-start | bytes 4612
Sparse Core Ops, SparseCore 0:
  60.6 10.2 reduce-scatter.1
where the time goes:
time: 359 us; the launch traced here: 358 us
  local copies, waits for them, and re-layouts  157 us (44%)
  other arithmetic  70.6 us (20%)
  blocking collectives  48 us (13%)
  waiting for transfers between devices  28 us (8%)
  starting transfers between devices  21.8 us (6%)
  matrix products  16.8 us (5%)
  between operations  14.7 us (4%)
    gather x4, local copies, waits for them, and re-layouts, on_device(): jnp.take(whole_coefs, global_knot + j, axis=1)  111 us
    scatter-add x1, other arithmetic, on_device(): jax.ops.segment_sum(row_moments(design, observed, weight_live).T, source_...  44.4 us
    all_gather x1, blocking collectives, on_device(): lax.all_gather(coefficients, 'src', axis=1, tiled=True)  38.7 us
    gather x1, local copies, waits for them, and re-layouts, on_device(): fitted = jnp.sum(design * jnp.take(params, source_index, axis=1), 0)  27.7 us
    ppermute x5, starting transfers between devices, passed_along(): return lax.ppermute(block, axis, route)  15 us
    reduce_sum x1, other arithmetic, on_device(): jnp.sum(axis_factors * jnp.take(whole_coefs, global_knot + j, axis=1), 0)  13.6 us
    ppermute x5, waiting for transfers between devices, passed_along(): return lax.ppermute(block, axis, route)  12.6 us
    dot_general x16, matrix products, add_block(): jnp.dot(values_blk, onehot, precision=lax.Precision.HIGHEST)  9.38 us
  transfers between devices with their start and end apart: 7, of which 7 were waited for; matrix products, arithmetic and copies ran while one was open for 2% of the time, Pallas kernels for 0%

commit v1 on v0

v1 whole, which is shorter than its diff:
```python
import jax
import jax.numpy as jnp
from jax import lax
from jax.experimental import pallas as pl
from jax.experimental.pallas import tpu as pltpu
from jax.sharding import PartitionSpec as P

SRC_DEV = 1024
KNOT_DEV = 128
ITERS = 3
LANES = 128
SUB = 8
LOW = 256
SIGNALS = 15 + 5
PAIRS = [(x, y) for x in range(3) for y in range(x, 3)]

src_ridge = 1.0
att_ridge = 1.0
relax_step = 0.15

f32 = jnp.float32
bf16 = jnp.bfloat16


def bernstein_products():
    parts = [(1.0, 0.0, 0.0, 0.0), (4.0, 12.0, 6.0, 1.0), (1.0, 6.0, 12.0, 4.0), (0.0, 0.0, 0.0, 1.0)]
    table = {}
    for i in range(4):
        for j in range(i, 4):
            coefs = [0.0] * 7
            for p in range(4):
                for q in range(4):
                    coefs[p + q] += parts[i][p] * parts[j][q] / 36.0
            table[i, j] = coefs
    return table


def split3(value):
    high = value.astype(bf16).astype(f32)
    rest = value - high
    middle = rest.astype(bf16).astype(f32)
    return [high, middle, rest - middle]


def spline_basis(phase_rows):
    remain = 1.0 - phase_rows
    square = phase_rows * phase_rows
    cube_term = square * phase_rows
    return [
        remain * remain * remain / 6.0,
        (3.0 * cube_term - 6.0 * square + 4.0) / 6.0,
        (-3.0 * cube_term + 3.0 * square + 3.0 * phase_rows + 1.0) / 6.0,
        cube_term / 6.0,
    ]


def solve_small(moments):
    matrix = {}
    position = 0
    for m in range(5):
        for n in range(m, 5):
            matrix[m, n] = moments[position] + (src_ridge if m == n else 0.0)
            position += 1
    factor = {}
    inverse = {}
    for j in range(5):
        for i in range(j, 5):
            running = matrix[j, i]
            for k in range(j):
                running = running - factor[i, k] * factor[j, k]
            if i == j:
                factor[j, j] = jnp.sqrt(running)
                inverse[j] = 1.0 / factor[j, j]
            else:
                factor[i, j] = running * inverse[j]
    forward = []
    for i in range(5):
        running = moments[15 + i]
        for k in range(i):
            running = running - factor[i, k] * forward[k]
        forward.append(running * inverse[i])
    solved = [None] * 5
    for i in reversed(range(5)):
        running = forward[i]
        for k in range(i + 1, 5):
            running = running - factor[k, i] * solved[k]
        solved[i] = running * inverse[i]
    return solved


def iota(shape, axis):
    return lax.broadcasted_iota(jnp.int32, shape, axis)


def fill_counts(counts_ref, limit_ref):
    shards = counts_ref.shape[2]
    rep = limit_ref.shape[0] // shards
    for d in range(shards):
        limit_ref[pl.ds(d * rep, rep), :] = jnp.full((rep, LANES), counts_ref[0, 0, d], jnp.int32)


def live_rows(limit_ref, start, rep):
    tile_row = start + iota((SUB, LANES), 0)
    slot = lax.rem(tile_row, rep) * LANES + iota((SUB, LANES), 1)
    return (slot < limit_ref[pl.ds(start, SUB), :]).astype(f32)


def by_tile(wide_ref, tiled_ref):
    rows = wide_ref.shape[0]
    for t in range(tiled_ref.shape[0]):
        tiled_ref[t, 0:rows, :] = wide_ref[:, t * LANES : (t + 1) * LANES]


def onehot(index_row, count):
    hit = iota((count, LANES), 0) == index_row
    return jnp.where(hit, 1.0, 0.0).astype(bf16)


def contract(left, right):
    return lax.dot_general(left, right, (((1,), (1,)), ((), ())), preferred_element_type=f32)


def shift_up(value, n):
    turned = pltpu.roll(value, n, 1)
    before = pltpu.roll(turned, 1, 0)
    before = jnp.where(iota(value.shape, 0) == 0, 0.0, before)
    return jnp.where(iota(value.shape, 1) < n, before, turned)


def shift_down(value, n):
    turned = pltpu.roll(value, LANES - n, 1)
    after = pltpu.roll(turned, value.shape[0] - 1, 0)
    after = jnp.where(iota(value.shape, 0) == value.shape[0] - 1, 0.0, after)
    return jnp.where(iota(value.shape, 1) >= LANES - n, after, turned)


def source_kernel(counts_ref, design_ref, obs_ref, weight_ref, index_ref, out_ref, tiled, limit, pieces, total):
    tiles = obs_ref.shape[0]
    rep = tiles // counts_ref.shape[2]
    fill_counts(counts_ref, limit)
    by_tile(design_ref, tiled)
    total[...] = jnp.zeros_like(total)
    highs = SRC_DEV // LOW

    def group(g, _):
        start = pl.multiple_of(g * SUB, SUB)
        rows = pl.ds(start, SUB)
        w = weight_ref[rows, :] * live_rows(limit, start, rep)
        cols = [tiled[rows, m, :] for m in range(5)]
        cols_w = [c * w for c in cols]
        values = [cols_w[m] * cols[n] for m in range(5) for n in range(m, 5)]
        values += [c * obs_ref[rows, :] for c in cols_w]
        for q, value in enumerate(values):
            for s, part in enumerate(split3(value)):
                pieces[:, s * SIGNALS + q, :] = part
        lefts, rights = [], []
        for i in range(SUB):
            block = pieces[i].astype(bf16)
            index = index_ref[pl.ds(start + i, 1), :]
            high = index // LOW
            masks = [jnp.where(jnp.broadcast_to(high, block.shape) == h, 1.0, 0.0).astype(bf16) for h in range(highs)]
            lefts.append(jnp.concatenate([block * mask for mask in masks], 0))
            rights.append(onehot(index - high * LOW, LOW))
        total[...] += contract(jnp.concatenate(lefts, 1), jnp.concatenate(rights, 1))
        return 0

    lax.fori_loop(0, tiles // SUB, group, 0)
    rows = pieces.shape[1]
    for h in range(highs):
        block = total[h * rows : h * rows + 3 * SIGNALS, :]
        summed = block[0:SIGNALS] + block[SIGNALS : 2 * SIGNALS] + block[2 * SIGNALS : 3 * SIGNALS]
        for half in range(LOW // LANES):
            out_ref[:, h * (LOW // LANES) + half, :] = summed[:, half * LANES : (half + 1) * LANES]


def band_kernel(counts_ref, phase_ref, axis_ref, weight_ref, knot_ref, out_ref, tiled, limit, pieces, moments):
    tiles = phase_ref.shape[0]
    shards = counts_ref.shape[2]
    rep = tiles // shards
    fill_counts(counts_ref, limit)
    by_tile(axis_ref, tiled)
    width = pieces.shape[1]

    def group(g, _):
        start = pl.multiple_of(g * SUB, SUB)
        rows = pl.ds(start, SUB)
        w = weight_ref[rows, :] * live_rows(limit, start, rep)
        u = phase_ref[rows, :]
        r = 1.0 - u
        u2, r2 = u * u, r * r
        u3, r3 = u2 * u, r2 * r
        powers = [r3 * r3, r3 * r2 * u, r2 * r2 * u2, r3 * u3, r2 * u2 * u2, r * u2 * u3, u3 * u3]
        axes = [tiled[rows, x, :] for x in range(3)]
        axes_w = [a * w for a in axes]
        pairs = [axes_w[x] * axes[y] for x, y in PAIRS]
        for p in range(7):
            for n in range(6):
                pieces[:, p * 6 + n, :] = powers[p] * pairs[n]
        per_block = min(rep, SUB)
        for b in range(SUB // per_block):
            lefts, rights = [], []
            for i in range(b * per_block, (b + 1) * per_block):
                lefts.append(jnp.concatenate(split3(pieces[i]), 0).astype(bf16))
                rights.append(onehot(knot_ref[pl.ds(start + i, 1), :], KNOT_DEV))
            got = contract(jnp.concatenate(lefts, 1), jnp.concatenate(rights, 1))
            summed = got[0:width] + got[width : 2 * width] + got[2 * width :]
            where_to = (start + b * per_block) // rep
            if rep <= SUB:
                moments[:, pl.ds(where_to, 1), :] = summed[:, None, :]
            else:
                moments[:, pl.ds(where_to, 1), :] += summed[:, None, :]
        return 0

    if rep > SUB:
        moments[...] = jnp.zeros_like(moments)
    lax.fori_loop(0, tiles // SUB, group, 0)
    table = bernstein_products()
    for n in range(6):
        parts = [moments[p * 6 + n] for p in range(7)]

        def product(i, j):
            return sum(c * part for c, part in zip(table[i, j], parts) if c)

        for delta in range(4):
            running = product(3 - delta, 3)
            for j in reversed(range(3 - delta)):
                running = product(j, j + delta) + shift_up(running, 1)
            out_ref[delta * 6 + n] = running


def resid_kernel(
    counts_ref, mine_ref, other_ref, design_ref, obs_ref, weight_ref, index_ref, phase_ref, axis_ref, knot_ref,
    params_ref, resid_ref, rhs_ref, tiled, tiled_axis, limit, pieces, moments, solved_ref,
):
    tiles = obs_ref.shape[0]
    shards = counts_ref.shape[2]
    rep = tiles // shards
    fill_counts(counts_ref, limit)
    by_tile(design_ref, tiled)
    by_tile(axis_ref, tiled_axis)
    solved = solve_small([mine_ref[q] + other_ref[q] for q in range(SIGNALS)])
    blocks = SRC_DEV // LANES
    for m in range(5):
        solved_ref[m] = solved[m]
        for b in range(blocks):
            params_ref[m : m + 1, b * LANES : (b + 1) * LANES] = solved[m][b : b + 1, :]
    width = pieces.shape[1]

    def group(g, _):
        start = pl.multiple_of(g * SUB, SUB)
        rows = pl.ds(start, SUB)
        live = live_rows(limit, start, rep)
        index = index_ref[rows, :]
        block_of = index // LANES
        lane_of = index - block_of * LANES
        hits = [block_of == b for b in range(blocks)]
        fitted = jnp.zeros((SUB, LANES), f32)
        for m in range(5):
            picked = jnp.zeros((SUB, LANES), f32)
            for b in range(blocks):
                table = jnp.broadcast_to(solved_ref[m, b : b + 1, :], (SUB, LANES))
                picked = jnp.where(hits[b], jnp.take_along_axis(table, lane_of, axis=1), picked)
            fitted = fitted + tiled[rows, m, :] * picked
        resid = live * (obs_ref[rows, :] - fitted)
        resid_ref[rows, :] = resid
        scaled = weight_ref[rows, :] * live * resid
        basis = spline_basis(phase_ref[rows, :])
        for x in range(3):
            along = scaled * tiled_axis[rows, x, :]
            for j in range(4):
                pieces[:, j * 3 + x, :] = along * basis[j]
        per_block = min(rep, SUB)
        for b in range(SUB // per_block):
            lefts, rights = [], []
            for i in range(b * per_block, (b + 1) * per_block):
                lefts.append(jnp.concatenate(split3(pieces[i]), 0).astype(bf16))
                rights.append(onehot(knot_ref[pl.ds(start + i, 1), :], KNOT_DEV))
            got = contract(jnp.concatenate(lefts, 1), jnp.concatenate(rights, 1))
            summed = got[0:width] + got[width : 2 * width] + got[2 * width :]
            where_to = (start + b * per_block) // rep
            if rep <= SUB:
                moments[:, pl.ds(where_to, 1), :] = summed[:, None, :]
            else:
                moments[:, pl.ds(where_to, 1), :] += summed[:, None, :]
        return 0

    if rep > SUB:
        moments[...] = jnp.zeros_like(moments)
    lax.fori_loop(0, tiles // SUB, group, 0)
    for x in range(3):
        running = moments[9 + x]
        for j in reversed(range(3)):
            running = moments[j * 3 + x] + shift_up(running, 1)
        rhs_ref[x] = running


def final_kernel(
    counts_ref, place_ref, sums_ref, resid_ref, phase_ref, axis_ref, knot_ref,
    att_ref, out_ref, tiled_axis, limit, tables, coef_ref,
):
    tiles = phase_ref.shape[0]
    shards = counts_ref.shape[2]
    rep = tiles // shards
    fill_counts(counts_ref, limit)
    by_tile(axis_ref, tiled_axis)
    order = {pair: n for n, pair in enumerate(PAIRS)}

    def band(delta, x, y):
        return sums_ref[3 + delta * 6 + order[min(x, y), max(x, y)]]

    rhs = [sums_ref[x] for x in range(3)]
    scale = [relax_step / (att_ridge + band(0, x, x)) for x in range(3)]
    coefs = [rhs[x] * scale[x] for x in range(3)]
    for _ in range(1, ITERS):
        ahead = {(y, delta): shift_down(coefs[y], delta) for y in range(3) for delta in range(1, 4)}
        fresh = []
        for x in range(3):
            normal = att_ridge * coefs[x]
            for y in range(3):
                normal = normal + band(0, x, y) * coefs[y]
            for delta in range(1, 4):
                for y in range(3):
                    normal = normal + band(delta, x, y) * ahead[y, delta]
                normal = normal + shift_up(sum(band(delta, x, y) * coefs[y] for y in range(3)), delta)
            fresh.append(coefs[x] + scale[x] * (rhs[x] - normal))
        coefs = fresh
    place = place_ref[0]
    for x in range(3):
        coef_ref[x] = coefs[x]
        att_ref[x : x + 1, :] = coef_ref[x, pl.ds(place, 1), :]
        for j in range(4):
            window = coefs[x] if j == 0 else shift_down(coefs[x], j)
            for d in range(shards):
                tables[x * 4 + j, pl.ds(d * rep, rep), :] = jnp.broadcast_to(window[d : d + 1], (rep, LANES))

    def group(g, _):
        start = pl.multiple_of(g * SUB, SUB)
        rows = pl.ds(start, SUB)
        knots = knot_ref[rows, :]
        basis = spline_basis(phase_ref[rows, :])
        predicted = jnp.zeros((SUB, LANES), f32)
        for j in range(4):
            inner = jnp.zeros((SUB, LANES), f32)
            for x in range(3):
                inner = inner + tiled_axis[rows, x, :] * jnp.take_along_axis(tables[x * 4 + j, rows, :], knots, axis=1)
            predicted = predicted + basis[j] * inner
        out_ref[rows, :] = live_rows(limit, start, rep) * (resid_ref[rows, :] - predicted)
        return 0

    lax.fori_loop(0, tiles // SUB, group, 0)


SMEM = pl.BlockSpec(memory_space=pltpu.SMEM)
VMEM = pl.BlockSpec(memory_space=pltpu.VMEM)


def call(kernel, name, scalars, arrays, outs, scratch):
    return pl.pallas_call(
        kernel,
        name=name,
        out_shape=outs,
        in_specs=[SMEM] * len(scalars) + [VMEM] * len(arrays),
        out_specs=jax.tree.map(lambda _: VMEM, outs),
        scratch_shapes=scratch,
    )(*scalars, *arrays)


def swapped(value, axis, bit):
    size = lax.axis_size(axis)
    return lax.ppermute(value, axis, [(i, i ^ bit) for i in range(size)])


def summed_over(value, axis):
    size = lax.axis_size(axis)
    if size & (size - 1):
        return lax.psum(value, axis)
    bit = 1
    while bit < size:
        value = value + swapped(value, axis, bit)
        bit *= 2
    return value


def on_device(design, observed, weight, phase_frac, axis_factors, source_index, knot_index, counts):
    row_count = observed.shape[0]
    tiles = row_count // LANES
    shards = lax.axis_size("src")
    obs, w, phase, index, knots = (
        a.reshape(tiles, LANES) for a in (observed, weight, phase_frac, source_index, knot_index)
    )
    tiled = pltpu.VMEM((tiles, SUB, LANES), f32)
    limit = pltpu.VMEM((tiles, LANES), jnp.int32)
    blocks = SRC_DEV // LANES
    highs = SRC_DEV // LOW
    moments = call(
        source_kernel, "source_sums", [counts], [design, obs, w, index],
        jax.ShapeDtypeStruct((SIGNALS, blocks, LANES), f32),
        [tiled, limit, pltpu.VMEM((SUB, 64, LANES), f32), pltpu.VMEM((highs * 64, LOW), f32)],
    )
    band = call(
        band_kernel, "band_sums", [counts], [phase, axis_factors, w, knots],
        jax.ShapeDtypeStruct((24, shards, KNOT_DEV), f32),
        [tiled, limit, pltpu.VMEM((SUB, 48, LANES), f32), pltpu.VMEM((48, shards, KNOT_DEV), f32)],
    )
    if lax.axis_size("ccd") == 2:
        other = swapped(moments, "ccd", 1)
    else:
        moments = summed_over(moments, "ccd")
        other = jnp.zeros_like(moments)
    params, resid, rhs = call(
        resid_kernel, "residuals", [counts], [moments, other, design, obs, w, index, phase, axis_factors, knots],
        (
            jax.ShapeDtypeStruct((5, SRC_DEV), f32),
            jax.ShapeDtypeStruct((tiles, LANES), f32),
            jax.ShapeDtypeStruct((3, shards, KNOT_DEV), f32),
        ),
        [
            tiled, tiled, limit, pltpu.VMEM((SUB, 16, LANES), f32), pltpu.VMEM((16, shards, KNOT_DEV), f32),
            pltpu.VMEM((5, blocks, LANES), f32),
        ],
    )
    sums = jnp.concatenate([rhs, band], 0)
    sums = summed_over(summed_over(sums, "ccd"), "src")
    place = lax.axis_index("src").reshape(1)
    attitude, residual = call(
        final_kernel, "attitude", [counts, place], [sums, resid, phase, axis_factors, knots],
        (jax.ShapeDtypeStruct((3, KNOT_DEV), f32), jax.ShapeDtypeStruct((tiles, LANES), f32)),
        [tiled, limit, pltpu.VMEM((12, tiles, LANES), f32), pltpu.VMEM((3, shards, KNOT_DEV), f32)],
    )
    return params, attitude, residual.reshape(row_count)


def solution(mesh):
    rows = P(("src", "ccd"))
    wide = P(None, ("src", "ccd"))
    in_specs = (wide, rows, rows, rows, wide, rows, rows, P("src", "ccd", None))
    out_specs = (P(None, "src"), P(None, "src"), rows)
    return jax.shard_map(on_device, mesh=mesh, in_specs=in_specs, out_specs=out_specs, check_vma=False)
```

time: 359 us -> 57.7 us (0.16)
  local copies, waits for them, and re-layouts: 157 us -> 0.62 us
  other arithmetic: 70.6 us -> 1.66 us
  blocking collectives: 48 us -> 0 us
  Pallas kernels: 0 us -> 19.1 us
  matrix products: 16.8 us -> 0 us
  between operations: 14.7 us -> 0.66 us
  starting transfers between devices: 21.8 us -> 9.03 us
    gather x5 -> x0, local copies, waits for them, and re-layouts: 139 us -> none  [the longest x4 111 us: on_device(): jnp.take(whole_coefs, global_knot + j, axis=1)]
    scatter-add x1 -> x0, other arithmetic: 44.4 us -> none  [on_device(): jax.ops.segment_sum(row_moments(design, observed, weight_live).T, source_...]
    all_gather x2 -> x0, blocking collectives: 40.6 us -> none  [the longest x1 38.7 us: on_device(): lax.all_gather(coefficients, 'src', axis=1, tiled=True)]
    pallas_call x0 -> x4, Pallas kernels: none -> 19.1 us  [call(): pl.pallas_call(kernel, name=name, out_shape=outs, in_specs=[SMEM] * len(s...]
    reduce_sum x4 -> x0, other arithmetic: 19 us -> none  [the longest x1 13.6 us: on_device(): jnp.sum(axis_factors * jnp.take(whole_coefs, global_knot + j, axis=1), 0)]
    dot_general x24 -> x0, matrix products: 16.8 us -> none  [the longest x16 9.38 us: add_block(): jnp.dot(values_blk, onehot, precision=lax.Precision.HIGHEST)]
    ppermute x5 -> x6, waiting for transfers between devices: 12.6 us -> 26.3 us  [swapped(): return lax.ppermute(value, axis, [(i, i ^ bit) for i in range(size)])]
    reduce_scatter x1 -> x0, waiting for transfers between devices: 7.71 us -> none  [on_device(): lax.psum_scatter(moments, 'ccd', scatter_dimension=1, tiled=True)]
  transfers between devices with their start and end apart: 7 -> 6, of which waited for: 7 -> 5; matrix products, arithmetic and copies ran while one was open for 2% -> 0% of each run, Pallas kernels for 0% -> 9%
where the time goes in v1:
time: 57.7 us; the launch traced here: 57.4 us
  waiting for transfers between devices  26.3 us (46%)
  Pallas kernels  19.1 us (33%)
  starting transfers between devices  9.03 us (16%)
  other arithmetic  1.66 us (3%)
  between operations  0.66 us (1%)
  local copies, waits for them, and re-layouts  0.62 us (1%)
    ppermute x6, waiting for transfers between devices, swapped(): return lax.ppermute(value, axis, [(i, i ^ bit) for i in range(size)])  26.3 us
    pallas_call x4, Pallas kernels, call(): pl.pallas_call(kernel, name=name, out_shape=outs, in_specs=[SMEM] * len(s...  19.1 us
    ppermute x6, starting transfers between devices, swapped(): return lax.ppermute(value, axis, [(i, i ^ bit) for i in range(size)])  9.03 us
  transfers between devices with their start and end apart: 6, of which 5 were waited for; matrix products, arithmetic and copies ran while one was open for 0% of the time, Pallas kernels for 9%

profile of v1, /device:TPU:0, one launch (start us, length us, event | category | flops | bytes accessed | tf_op | source)
XLA Modules:
  0.0 57.4 jit_solution(861775470765186393)
XLA Ops:
  0.6 6.2 %source_sums.1.mine_ref = f32[20,8,128]{2,1,0:T(8,128)} custom-call(s32[1,1,16]{2,1,0:T(1,128)} %counts_ref.7, f32[5,8192]{1,0:T(8,128)} %design_ref.3, f32[64,128]{1,0:T(8,128)} %bitcast.16, f32[64,128]{1,0:T(8,128)} %bitcast.13, s32[64,128]{1,0:T(8,128)} %bitcast.18), custom_call_target="tpu_custom_call" | custom-call | tf_op jit(solution)/shard_map/source_sums/pallas_call | solution.py:358
  6.8 0.5 collective-permute-start
  7.3 5.3 %band_sums.1 = f32[24,16,128]{2,1,0:T(8,128)} custom-call(s32[1,1,16]{2,1,0:T(1,128)} %counts_ref.7, f32[64,128]{1,0:T(8,128)} %bitcast.7, f32[3,8192]{1,0:T(4,128)} %axis_ref.5, f32[64,128]{1,0:T(8,128)} %bitcast.14, s32[64,128]{1,0:T(8,128)} %bitcast.10), custom_call_target="tpu_custom_call" | custom-call | tf_op jit(solution)/shard_map/band_sums/pallas_call | solution.py:358
  12.6 0.0 copy-start
  12.6 0.0 collective-permute-done.other_ref
  12.6 0.0 copy-start.2
  12.6 0.6 %copy-done.2 = f32[20,8,128]{2,1,0:T(8,128)} copy-done((f32[20,8,128]{2,1,0:T(8,128)}, f32[20,8,128]{2,1,0:T(8,128)S(1)}, u32[]{:S(2)}) %copy-start.2) | copy-done | bytes 81944
  13.2 4.9 %residuals.1 = (f32[5,1024]{1,0:T(8,128)}, f32[64,128]{1,0:T(8,128)}, f32[3,16,128]{2,1,0:T(8,128)}) custom-call(s32[1,1,16]{2,1,0:T(1,128)} %counts_ref.7, f32[20,8,128]{2,1,0:T(8,128)} %source_sums.1.mine_ref, f32[20,8,128]{2,1,0:T(8,128)} %copy-done.2, f32[5,8192]{1,0:T(8,128)} %design_ref.3, f32[64,128]{1,0:T(8,128)} %bitcast.17, f32[64,128]{1,0:T(8,128)} %bitcast.15, ...), custom_call_target="tpu_custom_call" | custom-call | tf_op jit(solution)/shard_map/residuals/pallas_call | solution.py:358
  18.1 0.0 copy-done
  18.1 0.0 copy-start.1
  18.1 0.8 %pad_maximum_fusion = f32[27,16,128]{2,1,0:T(8,128)S(1)} fusion(f32[24,16,128]{2,1,0:T(8,128)S(1)} %copy-done, f32[3,16,128]{2,1,0:T(8,128)} %get-tuple-element.9), kind=kLoop, calls=%fused_computation | loop fusion | flops 55296 | bytes 442368 | tf_op jit(solution)/shard_map/concatenate | solution.py:422
  19.0 0.1 collective-permute-start.1
  19.0 1.5 %collective-permute-done.1 = f32[27,16,128]{2,1,0:T(8,128)S(1)} collective-permute-done((f32[27,16,128]{2,1,0:T(8,128)S(1)}, f32[27,16,128]{2,1,0:T(8,128)S(1)}, u32[]{:S(2)}, u32[]{:S(2)}) %collective-permute-start.1) | collective-permute-done | bytes 221216 | tf_op jit(solution)/shard_map/ppermute | solution.py:370
  20.5 0.0 copy-done.1
  20.5 2.7 %collective-permute-start.2 = (f32[27,16,128]{2,1,0:T(8,128)S(1)}, f32[27,16,128]{2,1,0:T(8,128)S(1)}, u32[]{:S(2)}, u32[]{:S(2)}) collective-permute-start(f32[27,16,128]{2,1,0:T(8,128)S(1)} %fusion), channel_id=1, source_target_pairs={{0,2},{2,0},{4,6},{6,4},{8,10},{10,8},{12,14},{14,12},{16,18},{18,... | collective-permute-start | bytes 663560 | tf_op jit(solution)/shard_map/ppermute | solution.py:370
  23.2 6.0 %collective-permute-done.2 = f32[27,16,128]{2,1,0:T(8,128)S(1)} collective-permute-done((f32[27,16,128]{2,1,0:T(8,128)S(1)}, f32[27,16,128]{2,1,0:T(8,128)S(1)}, u32[]{:S(2)}, u32[]{:S(2)}) %collective-permute-start.2) | collective-permute-done | bytes 221216 | tf_op jit(solution)/shard_map/ppermute | solution.py:370
  29.2 1.8 %collective-permute-start.3 = (f32[27,16,128]{2,1,0:T(8,128)S(1)}, f32[27,16,128]{2,1,0:T(8,128)S(1)}, u32[]{:S(2)}, u32[]{:S(2)}) collective-permute-start(f32[27,16,128]{2,1,0:T(8,128)S(1)} %add.16), channel_id=1, source_target_pairs={{0,4},{2,6},{4,0},{6,2},{8,12},{10,14},{12,8},{14,10},{16,20},{18,... | collective-permute-start | bytes 663560 | tf_op jit(solution)/shard_map/ppermute | solution.py:370
  31.1 5.4 %collective-permute-done.3 = f32[27,16,128]{2,1,0:T(8,128)S(1)} collective-permute-done((f32[27,16,128]{2,1,0:T(8,128)S(1)}, f32[27,16,128]{2,1,0:T(8,128)S(1)}, u32[]{:S(2)}, u32[]{:S(2)}) %collective-permute-start.3) | collective-permute-done | bytes 221216 | tf_op jit(solution)/shard_map/ppermute | solution.py:370
  36.4 1.6 %collective-permute-start.4 = (f32[27,16,128]{2,1,0:T(8,128)S(1)}, f32[27,16,128]{2,1,0:T(8,128)S(1)}, u32[]{:S(2)}, u32[]{:S(2)}) collective-permute-start(f32[27,16,128]{2,1,0:T(8,128)S(1)} %add.17), channel_id=1, source_target_pairs={{0,8},{2,10},{4,12},{6,14},{8,0},{10,2},{12,4},{14,6},{16,24},{18,... | collective-permute-start | bytes 663560 | tf_op jit(solution)/shard_map/ppermute | solution.py:370
  38.1 4.7 %collective-permute-done.4 = f32[27,16,128]{2,1,0:T(8,128)S(1)} collective-permute-done((f32[27,16,128]{2,1,0:T(8,128)S(1)}, f32[27,16,128]{2,1,0:T(8,128)S(1)}, u32[]{:S(2)}, u32[]{:S(2)}) %collective-permute-start.4) | collective-permute-done | bytes 221216 | tf_op jit(solution)/shard_map/ppermute | solution.py:370
  42.8 2.3 %collective-permute-start.5 = (f32[27,16,128]{2,1,0:T(8,128)S(1)}, f32[27,16,128]{2,1,0:T(8,128)S(1)}, u32[]{:S(2)}, u32[]{:S(2)}) collective-permute-start(f32[27,16,128]{2,1,0:T(8,128)S(1)} %add.18), channel_id=1, source_target_pairs={{0,16},{2,18},{4,20},{6,22},{8,24},{10,26},{12,28},{14,30},{16,0},... | collective-permute-start | bytes 663560 | tf_op jit(solution)/shard_map/ppermute | solution.py:370
  45.2 8.8 %collective-permute-done.5 = f32[27,16,128]{2,1,0:T(8,128)S(1)} collective-permute-done((f32[27,16,128]{2,1,0:T(8,128)S(1)}, f32[27,16,128]{2,1,0:T(8,128)S(1)}, u32[]{:S(2)}, u32[]{:S(2)}) %collective-permute-start.5) | collective-permute-done | bytes 221216 | tf_op jit(solution)/shard_map/ppermute | solution.py:370
  53.9 0.7 %add.19.sums_ref = f32[27,16,128]{2,1,0:T(8,128)} add(f32[27,16,128]{2,1,0:T(8,128)S(1)} %add.18, f32[27,16,128]{2,1,0:T(8,128)S(1)} %collective-permute-done.5) | non-fusion elementwise | flops 55296 | bytes 663552 | tf_op jit(solution)/shard_map/add | solution.py:379
  54.7 2.7 %attitude.1 = (f32[3,128]{1,0:T(4,128)}, f32[64,128]{1,0:T(8,128)}) custom-call(s32[1,1,16]{2,1,0:T(1,128)} %counts_ref.7, s32[1]{0:T(128)} %bitcast.5.place_ref, f32[27,16,128]{2,1,0:T(8,128)} %add.19.sums_ref, f32[64,128]{1,0:T(8,128)} %get-tuple-element.10.resid_ref, f32[64,128]{1,0:T(8,128)} %bitcast.9, f32[3,8192]{1,0:T(4,128)} %axis_ref.5, ...), custom_call_target="tpu_custom_call" | custom-call | tf_op jit(solution)/shard_map/attitude/pallas_call | solution.py:358
  (4 shorter events, 0.1 us)
Async XLA Ops:
  6.8 5.8 %collective-permute-start = (f32[20,8,128]{2,1,0:T(8,128)}, f32[20,8,128]{2,1,0:T(8,128)S(1)}, u32[]{:S(2)}, u32[]{:S(2)}) collective-permute-start(f32[20,8,128]{2,1,0:T(8,128)} %source_sums.1.mine_ref), channel_id=1, source_target_pairs={{0,1},{1,0},{2,3},{3,2},{4,5},{5,4},{6,7},{7,6},{8,9},{9,8},{10,11... | collective-permute-start | bytes 245768 | tf_op jit(solution)/shard_map/ppermute | solution.py:370
  12.6 5.5 %copy-start = (f32[24,16,128]{2,1,0:T(8,128)S(1)}, f32[24,16,128]{2,1,0:T(8,128)}, u32[]{:S(2)}) copy-start(f32[24,16,128]{2,1,0:T(8,128)} %band_sums.1) | copy-start | bytes 589828
  12.6 0.6 %copy-start.2 = (f32[20,8,128]{2,1,0:T(8,128)}, f32[20,8,128]{2,1,0:T(8,128)S(1)}, u32[]{:S(2)}) copy-start(f32[20,8,128]{2,1,0:T(8,128)S(1)} %collective-permute-done.other_ref) | copy-start | bytes 245764
  18.1 2.4 %copy-start.1 = (f32[3,16,128]{2,1,0:T(8,128)S(1)}, f32[3,16,128]{2,1,0:T(8,128)}, u32[]{:S(2)}) copy-start(f32[3,16,128]{2,1,0:T(8,128)} %get-tuple-element.9) | copy-start | bytes 73732
  19.0 1.5 %collective-permute-start.1 = (f32[27,16,128]{2,1,0:T(8,128)S(1)}, f32[27,16,128]{2,1,0:T(8,128)S(1)}, u32[]{:S(2)}, u32[]{:S(2)}) collective-permute-start(f32[27,16,128]{2,1,0:T(8,128)S(1)} %pad_maximum_fusion), channel_id=1, source_target_pairs={{0,1},{1,0},{2,3},{3,2},{4,5},{5,4},{6,7},{7,6},{8,9},{9,8},{10,11... | collective-permute-start | bytes 663560 | tf_op jit(solution)/shard_map/ppermute | solution.py:370
  20.5 8.6 %collective-permute-start.2 = (f32[27,16,128]{2,1,0:T(8,128)S(1)}, f32[27,16,128]{2,1,0:T(8,128)S(1)}, u32[]{:S(2)}, u32[]{:S(2)}) collective-permute-start(f32[27,16,128]{2,1,0:T(8,128)S(1)} %fusion), channel_id=1, source_target_pairs={{0,2},{2,0},{4,6},{6,4},{8,10},{10,8},{12,14},{14,12},{16,18},{18,... | collective-permute-start | bytes 663560 | tf_op jit(solution)/shard_map/ppermute | solution.py:370
  29.2 7.2 %collective-permute-start.3 = (f32[27,16,128]{2,1,0:T(8,128)S(1)}, f32[27,16,128]{2,1,0:T(8,128)S(1)}, u32[]{:S(2)}, u32[]{:S(2)}) collective-permute-start(f32[27,16,128]{2,1,0:T(8,128)S(1)} %add.16), channel_id=1, source_target_pairs={{0,4},{2,6},{4,0},{6,2},{8,12},{10,14},{12,8},{14,10},{16,20},{18,... | collective-permute-start | bytes 663560 | tf_op jit(solution)/shard_map/ppermute | solution.py:370
  36.4 6.3 %collective-permute-start.4 = (f32[27,16,128]{2,1,0:T(8,128)S(1)}, f32[27,16,128]{2,1,0:T(8,128)S(1)}, u32[]{:S(2)}, u32[]{:S(2)}) collective-permute-start(f32[27,16,128]{2,1,0:T(8,128)S(1)} %add.17), channel_id=1, source_target_pairs={{0,8},{2,10},{4,12},{6,14},{8,0},{10,2},{12,4},{14,6},{16,24},{18,... | collective-permute-start | bytes 663560 | tf_op jit(solution)/shard_map/ppermute | solution.py:370
  42.8 11.1 %collective-permute-start.5 = (f32[27,16,128]{2,1,0:T(8,128)S(1)}, f32[27,16,128]{2,1,0:T(8,128)S(1)}, u32[]{:S(2)}, u32[]{:S(2)}) collective-permute-start(f32[27,16,128]{2,1,0:T(8,128)S(1)} %add.18), channel_id=1, source_target_pairs={{0,16},{2,18},{4,20},{6,22},{8,24},{10,26},{12,28},{14,30},{16,0},... | collective-permute-start | bytes 663560 | tf_op jit(solution)/shard_map/ppermute | solution.py:370

commit v2 on v1

--- a/solution.py
+++ b/solution.py
@@ -111,9 +111,17 @@
         tiled_ref[t, 0:rows, :] = wide_ref[:, t * LANES : (t + 1) * LANES]
 
 
+def spread_row(index_row, count):
+    packed = jnp.broadcast_to(index_row.astype(f32), (2 * SUB, LANES)).astype(bf16)
+    return jnp.concatenate([packed] * (count // (2 * SUB)), 0)
+
+
+def is_equal(left, right):
+    return jnp.where(left == right, jnp.ones((), bf16), jnp.zeros((), bf16))
+
+
 def onehot(index_row, count):
-    hit = iota((count, LANES), 0) == index_row
-    return jnp.where(hit, 1.0, 0.0).astype(bf16)
+    return is_equal(iota((count, LANES), 0).astype(f32).astype(bf16), spread_row(index_row, count))
 
 
 def contract(left, right):
@@ -158,8 +166,10 @@
             block = pieces[i].astype(bf16)
             index = index_ref[pl.ds(start + i, 1), :]
             high = index // LOW
-            masks = [jnp.where(jnp.broadcast_to(high, block.shape) == h, 1.0, 0.0).astype(bf16) for h in range(highs)]
-            lefts.append(jnp.concatenate([block * mask for mask in masks], 0))
+            packed = spread_row(high, 2 * SUB)
+            masks = [is_equal(packed, jnp.full((), h, bf16)) for h in range(highs)]
+            copies = block.shape[0] // (2 * SUB)
+            lefts.append(jnp.concatenate([block * jnp.concatenate([mask] * copies, 0) for mask in masks], 0))
             rights.append(onehot(index - high * LOW, LOW))
         total[...] += contract(jnp.concatenate(lefts, 1), jnp.concatenate(rights, 1))
         return 0
@@ -228,9 +238,26 @@
             out_ref[delta * 6 + n] = running
 
 
+def pack(value, q, message_ref):
+    quantities = len(PAIRS) * 4 + 3
+    parts = message_ref.shape[0]
+    shards = value.shape[0]
+    owned = shards // parts
+    zero = jnp.zeros((1, LANES), f32)
+    for p in range(parts):
+        for r in range(owned):
+            d = p * owned + r
+            message_ref[p, r * quantities + q : r * quantities + q + 1, :] = value[d : d + 1]
+        start, stop = p * owned, (p + 1) * owned
+        after = value[stop : stop + 1] if stop < shards else zero
+        before = value[start - 1 : start] if start else zero
+        edge = jnp.where(iota((1, LANES), 1) < LANES // 2, after, before)
+        message_ref[p, owned * quantities + q : owned * quantities + q + 1, :] = edge
+
+
 def resid_kernel(
-    counts_ref, mine_ref, other_ref, design_ref, obs_ref, weight_ref, index_ref, phase_ref, axis_ref, knot_ref,
-    params_ref, resid_ref, rhs_ref, tiled, tiled_axis, limit, pieces, moments, solved_ref,
+    counts_ref, mine_ref, other_ref, band_ref, design_ref, obs_ref, weight_ref, index_ref, phase_ref, axis_ref, knot_ref,
+    params_ref, resid_ref, message_ref, tiled, tiled_axis, limit, pieces, moments, solved_ref,
 ):
     tiles = obs_ref.shape[0]
     shards = counts_ref.shape[2]
@@ -291,28 +318,44 @@
         running = moments[9 + x]
         for j in reversed(range(3)):
             running = moments[j * 3 + x] + shift_up(running, 1)
-        rhs_ref[x] = running
-
-
-def final_kernel(
-    counts_ref, place_ref, sums_ref, resid_ref, phase_ref, axis_ref, knot_ref,
-    att_ref, out_ref, tiled_axis, limit, tables, coef_ref,
-):
-    tiles = phase_ref.shape[0]
-    shards = counts_ref.shape[2]
-    rep = tiles // shards
-    fill_counts(counts_ref, limit)
-    by_tile(axis_ref, tiled_axis)
+        pack(running, x, message_ref)
+    for q in range(band_ref.shape[0]):
+        pack(band_ref[q], 3 + q, message_ref)
+
+
+def solve_kernel(place_ref, sums_ref, out_ref):
+    quantities = len(PAIRS) * 4 + 3
+    owned = out_ref.shape[0] // 4
+    ring = -(-(owned + 2) // SUB) * SUB
     order = {pair: n for n, pair in enumerate(PAIRS)}
+    row, lane = iota((ring, LANES), 0), iota((ring, LANES), 1)
+    inside = row < owned
+    after = (row == owned) & (lane < LANES // 2)
+    before = (row == ring - 1) & (lane >= LANES // 2)
+    edge = (place_ref[0] == place_ref[1] - 1).astype(jnp.int32)
+    known = jnp.where(after & (jnp.full((ring, LANES), edge, jnp.int32) == 1), 0.0, 1.0)
+
+    def load(q):
+        rows = jnp.concatenate([sums_ref[pl.ds(r * quantities + q, 1), :] for r in range(owned)], 0)
+        rest = jnp.broadcast_to(sums_ref[pl.ds(owned * quantities + q, 1), :], (ring - owned, LANES))
+        return jnp.where(inside | after | before, jnp.concatenate([rows, rest], 0), 0.0)
+
+    def turn(value, n):
+        turned = pltpu.roll(value, n % LANES, 1)
+        if n > 0:
+            return jnp.where(lane < n, pltpu.roll(turned, 1, 0), turned)
+        return jnp.where(lane >= LANES + n, pltpu.roll(turned, ring - 1, 0), turned)
+
+    loaded = [load(q) for q in range(quantities)]
 
     def band(delta, x, y):
-        return sums_ref[3 + delta * 6 + order[min(x, y), max(x, y)]]
-
-    rhs = [sums_ref[x] for x in range(3)]
-    scale = [relax_step / (att_ridge + band(0, x, x)) for x in range(3)]
+        return loaded[3 + delta * 6 + order[min(x, y), max(x, y)]]
+
+    rhs = loaded[:3]
+    scale = [relax_step / (att_ridge + band(0, x, x)) * known for x in range(3)]
     coefs = [rhs[x] * scale[x] for x in range(3)]
     for _ in range(1, ITERS):
-        ahead = {(y, delta): shift_down(coefs[y], delta) for y in range(3) for delta in range(1, 4)}
+        ahead = {(y, delta): turn(coefs[y], -delta) for y in range(3) for delta in range(1, 4)}
         fresh = []
         for x in range(3):
             normal = att_ridge * coefs[x]
@@ -321,15 +364,30 @@
             for delta in range(1, 4):
                 for y in range(3):
                     normal = normal + band(delta, x, y) * ahead[y, delta]
-                normal = normal + shift_up(sum(band(delta, x, y) * coefs[y] for y in range(3)), delta)
+                normal = normal + turn(sum(band(delta, x, y) * coefs[y] for y in range(3)), delta)
             fresh.append(coefs[x] + scale[x] * (rhs[x] - normal))
         coefs = fresh
+    for x in range(3):
+        for r in range(owned):
+            out_ref[pl.ds(r * 4 + x, 1), :] = coefs[x][r : r + 1]
+
+
+def predict_kernel(
+    counts_ref, place_ref, coef_ref, resid_ref, phase_ref, axis_ref, knot_ref,
+    att_ref, out_ref, tiled_axis, limit, tables, own,
+):
+    tiles = phase_ref.shape[0]
+    shards = counts_ref.shape[2]
+    rep = tiles // shards
+    fill_counts(counts_ref, limit)
+    by_tile(axis_ref, tiled_axis)
     place = place_ref[0]
     for x in range(3):
-        coef_ref[x] = coefs[x]
-        att_ref[x : x + 1, :] = coef_ref[x, pl.ds(place, 1), :]
+        coefs = coef_ref[:, x, :]
+        own[x] = coefs
+        att_ref[x : x + 1, :] = own[x, pl.ds(place, 1), :]
         for j in range(4):
-            window = coefs[x] if j == 0 else shift_down(coefs[x], j)
+            window = coefs if j == 0 else shift_down(coefs, j)
             for d in range(shards):
                 tables[x * 4 + j, pl.ds(d * rep, rep), :] = jnp.broadcast_to(window[d : d + 1], (rep, LANES))
 
@@ -350,6 +408,7 @@
     lax.fori_loop(0, tiles // SUB, group, 0)
 
 
+BOTH = ("src", "ccd")
 SMEM = pl.BlockSpec(memory_space=pltpu.SMEM)
 VMEM = pl.BlockSpec(memory_space=pltpu.VMEM)
 
@@ -362,6 +421,7 @@
         in_specs=[SMEM] * len(scalars) + [VMEM] * len(arrays),
         out_specs=jax.tree.map(lambda _: VMEM, outs),
         scratch_shapes=scratch,
+        compiler_params=pltpu.CompilerParams(vmem_limit_bytes=8 << 20),
     )(*scalars, *arrays)
 
 
@@ -379,6 +439,20 @@
         value = value + swapped(value, axis, bit)
         bit *= 2
     return value
+
+
+def halved(value, mask, keep):
+    pair = value.reshape((2, value.shape[0] // 2) + value.shape[1:])
+    kept = lax.dynamic_index_in_dim(pair, keep, 0, False)
+    sent = lax.dynamic_index_in_dim(pair, 1 - keep, 0, False)
+    return kept + swapped(sent, BOTH, mask)
+
+
+def doubled(value, mask, keep):
+    other = swapped(value, BOTH, mask)
+    first = jnp.where(keep == 0, value, other)
+    second = jnp.where(keep == 0, other, value)
+    return jnp.concatenate([first, second], 0)
 
 
 def on_device(design, observed, weight, phase_frac, axis_factors, source_index, knot_index, counts):
@@ -407,23 +481,47 @@
     else:
         moments = summed_over(moments, "ccd")
         other = jnp.zeros_like(moments)
-    params, resid, rhs = call(
-        resid_kernel, "residuals", [counts], [moments, other, design, obs, w, index, phase, axis_factors, knots],
+    fast = lax.axis_size("ccd") == 2 and shards >= 4 and shards & (shards - 1) == 0
+    parts = 4 if fast else 1
+    owned = shards // parts
+    message_rows = -(-(owned + 1) * 27 // SUB) * SUB
+    params, resid, message = call(
+        resid_kernel, "residuals", [counts],
+        [moments, other, band, design, obs, w, index, phase, axis_factors, knots],
         (
             jax.ShapeDtypeStruct((5, SRC_DEV), f32),
             jax.ShapeDtypeStruct((tiles, LANES), f32),
-            jax.ShapeDtypeStruct((3, shards, KNOT_DEV), f32),
+            jax.ShapeDtypeStruct((parts, message_rows, LANES), f32),
         ),
         [
             tiled, tiled, limit, pltpu.VMEM((SUB, 16, LANES), f32), pltpu.VMEM((16, shards, KNOT_DEV), f32),
             pltpu.VMEM((5, blocks, LANES), f32),
         ],
     )
-    sums = jnp.concatenate([rhs, band], 0)
-    sums = summed_over(summed_over(sums, "ccd"), "src")
-    place = lax.axis_index("src").reshape(1)
+    place = lax.axis_index("src")
+    if fast:
+        upper = lax.axis_index("ccd")
+        for shift in range(shards.bit_length() - 1):
+            upper = upper ^ ((place >> shift) & 1)
+        lower = place & 1
+        sums = halved(halved(message, 1, upper), 3, lower)[0]
+        bit = 2
+        while bit < shards:
+            sums = sums + swapped(sums, BOTH, 2 * bit + 1)
+            bit *= 2
+        part = 2 * upper + lower
+    else:
+        sums = summed_over(summed_over(message[0], "ccd"), "src")
+        part = jnp.zeros_like(place)
+    coefs = call(
+        solve_kernel, "attitude", [jnp.stack([part, jnp.full_like(part, parts)])], [sums],
+        jax.ShapeDtypeStruct((owned * 4, LANES), f32), [],
+    )
+    if fast:
+        coefs = doubled(doubled(coefs, 3, lower), 1, upper)
     attitude, residual = call(
-        final_kernel, "attitude", [counts, place], [sums, resid, phase, axis_factors, knots],
+        predict_kernel, "predict", [counts, place.reshape(1)],
+        [coefs.reshape(shards, 4, LANES), resid, phase, axis_factors, knots],
         (jax.ShapeDtypeStruct((3, KNOT_DEV), f32), jax.ShapeDtypeStruct((tiles, LANES), f32)),
         [tiled, limit, pltpu.VMEM((12, tiles, LANES), f32), pltpu.VMEM((3, shards, KNOT_DEV), f32)],
     )

time: 57.7 us -> 47.2 us (0.82)
  waiting for transfers between devices: 26.3 us -> 16.5 us
  Pallas kernels: 19.1 us -> 15.7 us
  local copies, waits for them, and re-layouts: 0.62 us -> 3.93 us
  other arithmetic: 1.66 us -> 0.15 us
  starting transfers between devices: 9.03 us -> 9.83 us
    ppermute x6 -> x8, waiting for transfers between devices: 26.3 us -> 16.5 us  [swapped(): return lax.ppermute(value, axis, [(i, i ^ bit) for i in range(size)])]
    pallas_call x4 -> x5, Pallas kernels: 19.1 us -> 15.7 us  [call(): pl.pallas_call(kernel, name=name, out_shape=outs, in_specs=[SMEM] * len(s...]
    unnamed x6 -> x24, local copies, waits for them, and re-layouts: 0.62 us -> 3.9 us
    concatenate x1 -> x2, other arithmetic: 0.82 us -> 0.01 us  [doubled(): return jnp.concatenate([first, second], 0)]
    ppermute x6 -> x8, starting transfers between devices: 9.03 us -> 9.83 us  [swapped(): return lax.ppermute(value, axis, [(i, i ^ bit) for i in range(size)])]
    add x5 -> x4, other arithmetic: 0.84 us -> 0.05 us  [the longest x3 0.03 us: on_device(): sums = sums + swapped(sums, BOTH, 2 * bit + 1)]
  transfers between devices with their start and end apart: 6 -> 8, of which waited for: 5 -> 7; matrix products, arithmetic and copies ran while one was open for 0% -> 0% of each run, Pallas kernels for 9% -> 9%
where the time goes in v2:
time: 47.2 us; the launch traced here: 46.8 us
  waiting for transfers between devices  16.5 us (35%)
  Pallas kernels  15.7 us (33%)
  starting transfers between devices  9.83 us (21%)
  local copies, waits for them, and re-layouts  3.93 us (8%)
  between operations  0.77 us (2%)
    ppermute x8, waiting for transfers between devices, swapped(): return lax.ppermute(value, axis, [(i, i ^ bit) for i in range(size)])  16.5 us
    pallas_call x5, Pallas kernels, call(): pl.pallas_call(kernel, name=name, out_shape=outs, in_specs=[SMEM] * len(s...  15.7 us
    ppermute x8, starting transfers between devices, swapped(): return lax.ppermute(value, axis, [(i, i ^ bit) for i in range(size)])  9.83 us
    unnamed x24, local copies, waits for them, and re-layouts  3.9 us
  transfers between devices with their start and end apart: 8, of which 7 were waited for; matrix products, arithmetic and copies ran while one was open for 0% of the time, Pallas kernels for 9%

profile of v2, /device:TPU:0, one launch (start us, length us, event | category | flops | bytes accessed | tf_op | source)
XLA Modules:
  0.0 46.8 jit_solution(1588326571545339709)
XLA Ops:
  0.6 0.6 %copy-done.11 = s32[1,1,16]{2,1,0:T(1,128)S(1)} copy-done((s32[1,1,16]{2,1,0:T(1,128)S(1)}, s32[1,1,16]{2,1,0:T(1,128)}, u32[]{:S(2)}) %copy-start.11) | copy-done | bytes 88
  1.3 0.9 %copy-done.1 = f32[5,8192]{1,0:T(8,128)S(1)} copy-done((f32[5,8192]{1,0:T(8,128)S(1)}, f32[5,8192]{1,0:T(8,128)}, u32[]{:S(2)}) %copy-start.1) | copy-done | bytes 163864
  2.2 0.8 %copy-done.3 = f32[8192]{0:T(1024)S(1)} copy-done((f32[8192]{0:T(1024)S(1)}, f32[8192]{0:T(1024)}, u32[]{:S(2)}) %copy-start.3) | copy-done | bytes 32792
  3.0 0.8 %copy-done.7 = f32[8192]{0:T(1024)S(1)} copy-done((f32[8192]{0:T(1024)S(1)}, f32[8192]{0:T(1024)}, u32[]{:S(2)}) %copy-start.7) | copy-done | bytes 32792
  3.8 0.8 %copy-done.9 = s32[8192]{0:T(1024)S(1)} copy-done((s32[8192]{0:T(1024)S(1)}, s32[8192]{0:T(1024)}, u32[]{:S(2)}) %copy-start.9) | copy-done | bytes 32792
  4.5 4.9 %source_sums.1.mine_ref = f32[20,8,128]{2,1,0:T(8,128)S(1)} custom-call(s32[1,1,16]{2,1,0:T(1,128)S(1)} %copy-done.11, f32[5,8192]{1,0:T(8,128)S(1)} %copy-done.1, f32[64,128]{1,0:T(8,128)S(1)} %bitcast.27, f32[64,128]{1,0:T(8,128)S(1)} %bitcast.16, s32[64,128]{1,0:T(8,128)S(1)} %bitcast.29), custom_call_target="tpu_custom_call" | custom-call | tf_op jit(solution)/shard_map/source_sums/pallas_call | solution.py:417
  9.5 0.5 %collective-permute-start = (f32[20,8,128]{2,1,0:T(8,128)S(1)}, f32[20,8,128]{2,1,0:T(8,128)S(1)}, u32[]{:S(2)}, u32[]{:S(2)}) collective-permute-start(f32[20,8,128]{2,1,0:T(8,128)S(1)} %source_sums.1.mine_ref), channel_id=1, source_target_pairs={{0,1},{1,0},{2,3},{3,2},{4,5},{5,4},{6,7},{7,6},{8,9},{9,8},{10,11... | collective-permute-start | bytes 245768 | tf_op jit(solution)/shard_map/ppermute | solution.py:430
  10.1 4.1 %band_sums.1.band_ref = f32[24,16,128]{2,1,0:T(8,128)S(1)} custom-call(s32[1,1,16]{2,1,0:T(1,128)S(1)} %copy-done.11, f32[64,128]{1,0:T(8,128)S(1)} %bitcast.19, f32[3,8192]{1,0:T(4,128)S(1)} %copy-done, f32[64,128]{1,0:T(8,128)S(1)} %bitcast.17, s32[64,128]{1,0:T(8,128)S(1)} %bitcast.22), custom_call_target="tpu_custom_call" | custom-call | tf_op jit(solution)/shard_map/band_sums/pallas_call | solution.py:417
  14.2 3.9 %residuals.1 = (f32[5,1024]{1,0:T(8,128)}, f32[64,128]{1,0:T(8,128)S(1)}, f32[4,136,128]{2,1,0:T(8,128)S(1)}) custom-call(s32[1,1,16]{2,1,0:T(1,128)S(1)} %copy-done.11, f32[20,8,128]{2,1,0:T(8,128)S(1)} %source_sums.1.mine_ref, f32[20,8,128]{2,1,0:T(8,128)S(1)} %collective-permute-done.other_ref, f32[24,16,128]{2,1,0:T(8,128)S(1)} %band_sums.1.band_ref, ...), custom_call_target="tpu_custom_call" | custom-call | tf_op jit(solution)/shard_map/residuals/pallas_call | solution.py:417
  18.2 1.3 %collective-permute-done.1 = f32[2,136,128]{2,1,0:T(8,128)S(1)} collective-permute-done((f32[2,136,128]{2,1,0:T(8,128)S(1)}, f32[2,136,128]{2,1,0:T(8,128)S(1)}, u32[]{:S(2)}, u32[]{:S(2)}) %collective-permute-start.1) | collective-permute-done | bytes 139296 | tf_op jit(solution)/shard_map/ppermute | solution.py:430
  19.6 2.7 %collective-permute-start.2 = (f32[1,136,128]{2,1,0:T(8,128)S(1)}, f32[1,136,128]{2,1,0:T(8,128)S(1)}, u32[]{:S(2)}, u32[]{:S(2)}) collective-permute-start(f32[1,136,128]{2,1,0:T(8,128)S(1)} %constant_dynamic-slice_fusion), channel_id=1, source_target_pairs={{0,3},{1,2},{2,1},{3,0},{4,7},{5,6},{6,5},{7,4},{8,11},{9,10},{10,... | collective-permute-start | bytes 208904 | tf_op jit(solution)/shard_map/ppermute | solution.py:430
  22.2 2.4 %collective-permute-done.2 = f32[1,136,128]{2,1,0:T(8,128)S(1)} collective-permute-done((f32[1,136,128]{2,1,0:T(8,128)S(1)}, f32[1,136,128]{2,1,0:T(8,128)S(1)}, u32[]{:S(2)}, u32[]{:S(2)}) %collective-permute-start.2) | collective-permute-done | bytes 69664 | tf_op jit(solution)/shard_map/ppermute | solution.py:430
  24.6 1.6 %collective-permute-start.3 = (f32[136,128]{1,0:T(8,128)S(1)}, f32[136,128]{1,0:T(8,128)S(1)}, u32[]{:S(2)}, u32[]{:S(2)}) collective-permute-start(f32[136,128]{1,0:T(8,128)S(1)} %add_bitcast_fusion), channel_id=1, source_target_pairs={{0,5},{1,4},{2,7},{3,6},{4,1},{5,0},{6,3},{7,2},{8,13},{9,12},{10,... | collective-permute-start | bytes 208904 | tf_op jit(solution)/shard_map/ppermute | solution.py:430
  26.3 2.6 %collective-permute-done.3 = f32[136,128]{1,0:T(8,128)S(1)} collective-permute-done((f32[136,128]{1,0:T(8,128)S(1)}, f32[136,128]{1,0:T(8,128)S(1)}, u32[]{:S(2)}, u32[]{:S(2)}) %collective-permute-start.3) | collective-permute-done | bytes 69664 | tf_op jit(solution)/shard_map/ppermute | solution.py:430
  28.9 1.5 %collective-permute-start.4 = (f32[136,128]{1,0:T(8,128)S(1)}, f32[136,128]{1,0:T(8,128)S(1)}, u32[]{:S(2)}, u32[]{:S(2)}) collective-permute-start(f32[136,128]{1,0:T(8,128)S(1)} %add.41), channel_id=1, source_target_pairs={{0,9},{1,8},{2,11},{3,10},{4,13},{5,12},{6,15},{7,14},{8,1},{9,0},... | collective-permute-start | bytes 208904 | tf_op jit(solution)/shard_map/ppermute | solution.py:430
  30.3 2.7 %collective-permute-done.4 = f32[136,128]{1,0:T(8,128)S(1)} collective-permute-done((f32[136,128]{1,0:T(8,128)S(1)}, f32[136,128]{1,0:T(8,128)S(1)}, u32[]{:S(2)}, u32[]{:S(2)}) %collective-permute-start.4) | collective-permute-done | bytes 69664 | tf_op jit(solution)/shard_map/ppermute | solution.py:430
  33.1 2.3 %collective-permute-start.5 = (f32[136,128]{1,0:T(8,128)S(1)}, f32[136,128]{1,0:T(8,128)S(1)}, u32[]{:S(2)}, u32[]{:S(2)}) collective-permute-start(f32[136,128]{1,0:T(8,128)S(1)} %add.42), channel_id=1, source_target_pairs={{0,17},{1,16},{2,19},{3,18},{4,21},{5,20},{6,23},{7,22},{8,25},{9,... | collective-permute-start | bytes 208904 | tf_op jit(solution)/shard_map/ppermute | solution.py:430
  35.5 4.2 %collective-permute-done.5 = f32[136,128]{1,0:T(8,128)S(1)} collective-permute-done((f32[136,128]{1,0:T(8,128)S(1)}, f32[136,128]{1,0:T(8,128)S(1)}, u32[]{:S(2)}, u32[]{:S(2)}) %collective-permute-start.5) | collective-permute-done | bytes 69664 | tf_op jit(solution)/shard_map/ppermute | solution.py:430
  39.7 0.7 %attitude.1 = f32[16,128]{1,0:T(8,128)S(1)} custom-call(s32[2]{0:T(128)S(1)} %pad_add_fusion.place_ref, f32[136,128]{1,0:T(8,128)S(1)} %add.43.sums_ref), custom_call_target="tpu_custom_call" | custom-call | tf_op jit(solution)/shard_map/attitude/pallas_call | solution.py:417
  40.4 1.0 %collective-permute-start.6 = (f32[16,128]{1,0:T(8,128)S(1)}, f32[16,128]{1,0:T(8,128)S(1)}, u32[]{:S(2)}, u32[]{:S(2)}) collective-permute-start(f32[16,128]{1,0:T(8,128)S(1)} %attitude.1), channel_id=1, source_target_pairs={{0,3},{1,2},{2,1},{3,0},{4,7},{5,6},{6,5},{7,4},{8,11},{9,10},{10,... | collective-permute-start | bytes 24584 | tf_op jit(solution)/shard_map/ppermute | solution.py:430
  41.4 2.2 %collective-permute-done.6 = f32[16,128]{1,0:T(8,128)S(1)} collective-permute-done((f32[16,128]{1,0:T(8,128)S(1)}, f32[16,128]{1,0:T(8,128)S(1)}, u32[]{:S(2)}, u32[]{:S(2)}) %collective-permute-start.6) | collective-permute-done | bytes 8224 | tf_op jit(solution)/shard_map/ppermute | solution.py:430
  43.6 0.2 collective-permute-start.7
  43.8 1.0 %collective-permute-done.7 = f32[32,128]{1,0:T(8,128)S(1)} collective-permute-done((f32[32,128]{1,0:T(8,128)S(1)}, f32[32,128]{1,0:T(8,128)S(1)}, u32[]{:S(2)}, u32[]{:S(2)}) %collective-permute-start.7) | collective-permute-done | bytes 16416 | tf_op jit(solution)/shard_map/ppermute | solution.py:430
  44.8 2.0 %predict.1 = (f32[3,128]{1,0:T(4,128)}, f32[64,128]{1,0:T(8,128)}) custom-call(s32[1,1,16]{2,1,0:T(1,128)S(1)} %copy-done.11, s32[1]{0:T(128)} %bitcast.5.place_ref, f32[16,4,128]{2,1,0:T(4,128)S(1)} %bitcast.31, f32[64,128]{1,0:T(8,128)S(1)} %get-tuple-element.10.resid_ref, f32[64,128]{1,0:T(8,128)S(1)} %bitcast.21, f32[3,8192]{1,0:T(4,128)S(1)} %copy-done, ...), custom_call_target="tpu_custom_call" | custom-call | tf_op jit(solution)/shard_map/predict/pallas_call | solution.py:417
  (33 shorter events, 0.4 us)
Async XLA Ops:
  0.6 0.7 %copy-start.11 = (s32[1,1,16]{2,1,0:T(1,128)S(1)}, s32[1,1,16]{2,1,0:T(1,128)}, u32[]{:S(2)}) copy-start(s32[1,1,16]{2,1,0:T(1,128)} %counts_ref.7) | copy-start | bytes 196
  1.3 0.9 %copy-start.1 = (f32[5,8192]{1,0:T(8,128)S(1)}, f32[5,8192]{1,0:T(8,128)}, u32[]{:S(2)}) copy-start(f32[5,8192]{1,0:T(8,128)} %design_ref.3) | copy-start | bytes 491524
  2.2 0.8 %copy-start.3 = (f32[8192]{0:T(1024)S(1)}, f32[8192]{0:T(1024)}, u32[]{:S(2)}) copy-start(f32[8192]{0:T(1024)} %param.10) | copy-start | bytes 98308
  3.0 0.8 %copy-start.7 = (f32[8192]{0:T(1024)S(1)}, f32[8192]{0:T(1024)}, u32[]{:S(2)}) copy-start(f32[8192]{0:T(1024)} %param.9) | copy-start | bytes 98308
  3.8 0.8 %copy-start.9 = (s32[8192]{0:T(1024)S(1)}, s32[8192]{0:T(1024)}, u32[]{:S(2)}) copy-start(s32[8192]{0:T(1024)} %param.13) | copy-start | bytes 98308
  4.5 5.5 %copy-start = (f32[3,8192]{1,0:T(4,128)S(1)}, f32[3,8192]{1,0:T(4,128)}, u32[]{:S(2)}) copy-start(f32[3,8192]{1,0:T(4,128)} %axis_ref.5) | copy-start | bytes 294916
  4.5 5.5 %copy-start.4 = (f32[8192]{0:T(1024)S(1)}, f32[8192]{0:T(1024)}, u32[]{:S(2)}) copy-start(f32[8192]{0:T(1024)} %param.10) | copy-start | bytes 98308
  4.5 5.5 %copy-start.5 = (f32[8192]{0:T(1024)S(1)}, f32[8192]{0:T(1024)}, u32[]{:S(2)}) copy-start(f32[8192]{0:T(1024)} %param.11) | copy-start | bytes 98308
  4.5 5.5 %copy-start.6 = (s32[8192]{0:T(1024)S(1)}, s32[8192]{0:T(1024)}, u32[]{:S(2)}) copy-start(s32[8192]{0:T(1024)} %param.14) | copy-start | bytes 98308
  9.5 4.7 %copy-start.2 = (f32[5,8192]{1,0:T(8,128)S(1)}, f32[5,8192]{1,0:T(8,128)}, u32[]{:S(2)}) copy-start(f32[5,8192]{1,0:T(8,128)} %design_ref.3) | copy-start | bytes 491524
  9.5 4.7 %collective-permute-start = (f32[20,8,128]{2,1,0:T(8,128)S(1)}, f32[20,8,128]{2,1,0:T(8,128)S(1)}, u32[]{:S(2)}, u32[]{:S(2)}) collective-permute-start(f32[20,8,128]{2,1,0:T(8,128)S(1)} %source_sums.1.mine_ref), channel_id=1, source_target_pairs={{0,1},{1,0},{2,3},{3,2},{4,5},{5,4},{6,7},{7,6},{8,9},{9,8},{10,11... | collective-permute-start | bytes 245768 | tf_op jit(solution)/shard_map/ppermute | solution.py:430
  10.0 4.2 %copy-start.8 = (f32[8192]{0:T(1024)S(1)}, f32[8192]{0:T(1024)}, u32[]{:S(2)}) copy-start(f32[8192]{0:T(1024)} %param.9) | copy-start | bytes 98308
  10.0 4.2 %copy-start.10 = (s32[8192]{0:T(1024)S(1)}, s32[8192]{0:T(1024)}, u32[]{:S(2)}) copy-start(s32[8192]{0:T(1024)} %param.13) | copy-start | bytes 98308
  18.1 1.4 %collective-permute-start.1 = (f32[2,136,128]{2,1,0:T(8,128)S(1)}, f32[2,136,128]{2,1,0:T(8,128)S(1)}, u32[]{:S(2)}, u32[]{:S(2)}) collective-permute-start(f32[2,136,128]{2,1,0:T(8,128)S(1)} %dynamic-slice_bitcast_fusion), channel_id=1, source_target_pairs={{0,1},{1,0},{2,3},{3,2},{4,5},{5,4},{6,7},{7,6},{8,9},{9,8},{10,11... | collective-permute-start | bytes 417800 | tf_op jit(solution)/shard_map/ppermute | solution.py:430
  19.6 5.1 %collective-permute-start.2 = (f32[1,136,128]{2,1,0:T(8,128)S(1)}, f32[1,136,128]{2,1,0:T(8,128)S(1)}, u32[]{:S(2)}, u32[]{:S(2)}) collective-permute-start(f32[1,136,128]{2,1,0:T(8,128)S(1)} %constant_dynamic-slice_fusion), channel_id=1, source_target_pairs={{0,3},{1,2},{2,1},{3,0},{4,7},{5,6},{6,5},{7,4},{8,11},{9,10},{10,... | collective-permute-start | bytes 208904 | tf_op jit(solution)/shard_map/ppermute | solution.py:430
  24.6 4.2 %collective-permute-start.3 = (f32[136,128]{1,0:T(8,128)S(1)}, f32[136,128]{1,0:T(8,128)S(1)}, u32[]{:S(2)}, u32[]{:S(2)}) collective-permute-start(f32[136,128]{1,0:T(8,128)S(1)} %add_bitcast_fusion), channel_id=1, source_target_pairs={{0,5},{1,4},{2,7},{3,6},{4,1},{5,0},{6,3},{7,2},{8,13},{9,12},{10,... | collective-permute-start | bytes 208904 | tf_op jit(solution)/shard_map/ppermute | solution.py:430
  28.9 4.2 %collective-permute-start.4 = (f32[136,128]{1,0:T(8,128)S(1)}, f32[136,128]{1,0:T(8,128)S(1)}, u32[]{:S(2)}, u32[]{:S(2)}) collective-permute-start(f32[136,128]{1,0:T(8,128)S(1)} %add.41), channel_id=1, source_target_pairs={{0,9},{1,8},{2,11},{3,10},{4,13},{5,12},{6,15},{7,14},{8,1},{9,0},... | collective-permute-start | bytes 208904 | tf_op jit(solution)/shard_map/ppermute | solution.py:430
  33.1 6.6 %collective-permute-start.5 = (f32[136,128]{1,0:T(8,128)S(1)}, f32[136,128]{1,0:T(8,128)S(1)}, u32[]{:S(2)}, u32[]{:S(2)}) collective-permute-start(f32[136,128]{1,0:T(8,128)S(1)} %add.42), channel_id=1, source_target_pairs={{0,17},{1,16},{2,19},{3,18},{4,21},{5,20},{6,23},{7,22},{8,25},{9,... | collective-permute-start | bytes 208904 | tf_op jit(solution)/shard_map/ppermute | solution.py:430
  40.4 3.1 %collective-permute-start.6 = (f32[16,128]{1,0:T(8,128)S(1)}, f32[16,128]{1,0:T(8,128)S(1)}, u32[]{:S(2)}, u32[]{:S(2)}) collective-permute-start(f32[16,128]{1,0:T(8,128)S(1)} %attitude.1), channel_id=1, source_target_pairs={{0,3},{1,2},{2,1},{3,0},{4,7},{5,6},{6,5},{7,4},{8,11},{9,10},{10,... | collective-permute-start | bytes 24584 | tf_op jit(solution)/shard_map/ppermute | solution.py:430
  43.6 1.2 %collective-permute-start.7 = (f32[32,128]{1,0:T(8,128)S(1)}, f32[32,128]{1,0:T(8,128)S(1)}, u32[]{:S(2)}, u32[]{:S(2)}) collective-permute-start(f32[32,128]{1,0:T(8,128)S(1)} %pad_maximum_fusion.1), channel_id=1, source_target_pairs={{0,1},{1,0},{2,3},{3,2},{4,5},{5,4},{6,7},{7,6},{8,9},{9,8},{10,11... | collective-permute-start | bytes 49160 | tf_op jit(solution)/shard_map/ppermute | solution.py:430

commit v3 on v2

v3 whole, which is shorter than its diff:
```python
import jax
import jax.numpy as jnp
from jax import lax
from jax.experimental import pallas as pl
from jax.experimental.pallas import tpu as pltpu
from jax.sharding import PartitionSpec as P

SRC_DEV = 1024
KNOT_DEV = 128
ITERS = 3
LANES = 128
SUB = 8
LOW = 256
STEPS = 16
CUBICS = [(1.0, 0.0, 0.0, 0.0), (4.0, 12.0, 6.0, 1.0), (1.0, 6.0, 12.0, 4.0), (0.0, 0.0, 0.0, 1.0)]
SIGNALS = 15 + 5
PAIRS = [(x, y) for x in range(3) for y in range(x, 3)]

src_ridge = 1.0
att_ridge = 1.0
relax_step = 0.15

f32 = jnp.float32
bf16 = jnp.bfloat16


def bernstein_products():
    table = {}
    for i in range(4):
        for j in range(i, 4):
            coefs = [0.0] * 7
            for p in range(4):
                for q in range(4):
                    coefs[p + q] += CUBICS[i][p] * CUBICS[j][q] / 36.0
            table[i, j] = coefs
    return table


def split3(value):
    high = value.astype(bf16).astype(f32)
    rest = value - high
    middle = rest.astype(bf16).astype(f32)
    return [high, middle, rest - middle]


def spline_basis(phase_rows):
    remain = 1.0 - phase_rows
    square = phase_rows * phase_rows
    cube_term = square * phase_rows
    return [
        remain * remain * remain / 6.0,
        (3.0 * cube_term - 6.0 * square + 4.0) / 6.0,
        (-3.0 * cube_term + 3.0 * square + 3.0 * phase_rows + 1.0) / 6.0,
        cube_term / 6.0,
    ]


def solve_small(moments):
    matrix = {}
    position = 0
    for m in range(5):
        for n in range(m, 5):
            matrix[m, n] = moments[position] + (src_ridge if m == n else 0.0)
            position += 1
    factor = {}
    inverse = {}
    for j in range(5):
        for i in range(j, 5):
            running = matrix[j, i]
            for k in range(j):
                running = running - factor[i, k] * factor[j, k]
            if i == j:
                factor[j, j] = jnp.sqrt(running)
                inverse[j] = 1.0 / factor[j, j]
            else:
                factor[i, j] = running * inverse[j]
    forward = []
    for i in range(5):
        running = moments[15 + i]
        for k in range(i):
            running = running - factor[i, k] * forward[k]
        forward.append(running * inverse[i])
    solved = [None] * 5
    for i in reversed(range(5)):
        running = forward[i]
        for k in range(i + 1, 5):
            running = running - factor[k, i] * solved[k]
        solved[i] = running * inverse[i]
    return solved


def iota(shape, axis):
    return lax.broadcasted_iota(jnp.int32, shape, axis)


def spread_row(index_row, count):
    packed = jnp.broadcast_to(index_row, (2 * SUB, LANES)).astype(bf16)
    return jnp.concatenate([packed] * (count // (2 * SUB)), 0)


def is_equal(left, right):
    return jnp.where(left == right, jnp.ones((), bf16), jnp.zeros((), bf16))


def onehot(index_row, count):
    return is_equal(iota((count, LANES), 0).astype(f32).astype(bf16), spread_row(index_row, count))


def by_tile(wide_ref, tiled_ref):
    rows = wide_ref.shape[0]
    for t in range(tiled_ref.shape[0]):
        tiled_ref[t, 0:rows, :] = wide_ref[:, t * LANES : (t + 1) * LANES]


def tile_of(wide_ref, t):
    block = wide_ref[:, pl.ds(pl.multiple_of(t * LANES, LANES), LANES)]
    return jnp.concatenate([block, jnp.zeros((SUB - block.shape[0], LANES), f32)], 0)


def row_of(ref, t):
    return jnp.broadcast_to(ref[pl.ds(t, 1), :], (SUB, LANES))


def per_sublane(values, kind):
    row = iota((SUB, LANES), 0)
    out = jnp.full((SUB, LANES), values[0], kind)
    for s in range(1, SUB):
        if values[s] != values[0]:
            out = jnp.where(row == s, jnp.full((SUB, LANES), values[s], kind), out)
    return out


def pick_rows(value, pattern):
    return jnp.take_along_axis(value, pattern, axis=0)


def patterns(values):
    values = list(values) + [0] * (-len(values) % SUB)
    return [per_sublane(values[i : i + SUB], jnp.int32) for i in range(0, len(values), SUB)]


def stacked_parts(values):
    value = jnp.concatenate(values, 0)
    rows = 3 * value.shape[0]
    parts = split3(value)
    if rows % (2 * SUB):
        parts.append(jnp.zeros((SUB, LANES), f32))
    return jnp.concatenate(parts, 0).astype(bf16)


def sum_parts(value, rows):
    return value[0:rows] + value[rows : 2 * rows] + value[2 * rows : 3 * rows]


def add_blocks(moments_ref, start, steps, rep, rows, left_of, knot_ref):
    per_block = min(rep, steps)
    for b in range(steps // per_block):
        lefts, rights = [], []
        for i in range(b * per_block, (b + 1) * per_block):
            lefts.append(left_of(start + i))
            rights.append(onehot(knot_ref[pl.ds(start + i, 1), :].astype(f32), KNOT_DEV))
        got = contract(jnp.concatenate(lefts, 1), jnp.concatenate(rights, 1))
        summed = sum_parts(got, rows)[:, None, :]
        where_to = pl.ds((start + b * per_block) // rep, 1)
        if rep <= steps:
            moments_ref[:, where_to, :] = summed
        else:
            moments_ref[:, where_to, :] += summed


def contract(left, right):
    return lax.dot_general(left, right, (((1,), (1,)), ((), ())), preferred_element_type=f32)


def shift_up(value, n):
    turned = pltpu.roll(value, n, 1)
    before = pltpu.roll(turned, 1, 0)
    before = jnp.where(iota(value.shape, 0) == 0, 0.0, before)
    return jnp.where(iota(value.shape, 1) < n, before, turned)


def shift_down(value, n):
    turned = pltpu.roll(value, LANES - n, 1)
    after = pltpu.roll(turned, value.shape[0] - 1, 0)
    after = jnp.where(iota(value.shape, 0) == value.shape[0] - 1, 0.0, after)
    return jnp.where(iota(value.shape, 1) >= LANES - n, after, turned)


def source_kernel(
    counts_hbm, design_hbm, obs_hbm, weight_hbm, index_hbm, out_ref, live_ref,
    counts_ref, design_ref, obs_ref, weight_ref, index_ref, sems, low_ref, high_ref, total,
):
    tiles = obs_ref.shape[0]
    shards = counts_ref.shape[2]
    rep = tiles // shards
    copies = [
        pltpu.make_async_copy(src, dst, sems.at[i])
        for i, (src, dst) in enumerate(
            [(counts_hbm, counts_ref), (weight_hbm, weight_ref), (index_hbm, index_ref), (obs_hbm, obs_ref),
             (design_hbm, design_ref)]
        )
    ]
    for copy in copies:
        copy.start()
    total[...] = jnp.zeros_like(total)
    highs = SRC_DEV // LOW
    pairs = [(m, n) for m in range(5) for n in range(m, 5)] + [(m, 5) for m in range(5)]
    lefts_of = patterns([m for m, _ in pairs])
    rights_of = patterns([n for _, n in pairs])
    rows = SUB * len(lefts_of)
    is_observed = iota((SUB, LANES), 0) == 5
    copies[0].wait()
    slots = iota((rep, LANES), 0) * LANES + iota((rep, LANES), 1)
    for d in range(shards):
        live_ref[pl.ds(d * rep, rep), :] = (slots < counts_ref[0, 0, d]).astype(f32)
    copies[1].wait()
    copies[2].wait()
    for g in range(tiles // SUB):
        at = pl.ds(g * SUB, SUB)
        weight_ref[at, :] = weight_ref[at, :] * live_ref[at, :]
        high = index_ref[at, :] // LOW
        high_ref[at, :] = high.astype(f32)
        low_ref[at, :] = (index_ref[at, :] - high * LOW).astype(f32)
    copies[3].wait()
    copies[4].wait()

    def group(g, _):
        start = g * STEPS
        lefts, rights = [], []
        for i in range(STEPS):
            t = start + i
            values = jnp.where(is_observed, row_of(obs_ref, t), tile_of(design_ref, t))
            scaled = values * row_of(weight_ref, t)
            block = stacked_parts([pick_rows(scaled, m) * pick_rows(values, n) for m, n in zip(lefts_of, rights_of)])
            packed = spread_row(high_ref[pl.ds(t, 1), :], 2 * SUB)
            masks = [is_equal(packed, jnp.full((), h, bf16)) for h in range(highs)]
            repeats = block.shape[0] // (2 * SUB)
            lefts.append(jnp.concatenate([block * jnp.concatenate([mask] * repeats, 0) for mask in masks], 0))
            rights.append(onehot(low_ref[pl.ds(t, 1), :], LOW))
        total[...] += contract(jnp.concatenate(lefts, 1), jnp.concatenate(rights, 1))
        return 0

    lax.fori_loop(0, tiles // STEPS, group, 0)
    height = total.shape[0] // highs
    for h in range(highs):
        summed = sum_parts(total[h * height : (h + 1) * height, :], rows)
        for half in range(LOW // LANES):
            out_ref[:, h * (LOW // LANES) + half, :] = summed[0:SIGNALS, half * LANES : (half + 1) * LANES]


def band_kernel(live_ref, phase_ref, axis_ref, weight_ref, knot_ref, out_ref, scaled_ref, moments):
    tiles, shards = phase_ref.shape[0], moments.shape[1]
    rep = tiles // shards
    scaled_ref[...] = weight_ref[...] * live_ref[...]
    rows = moments.shape[0]
    power = iota((SUB, LANES), 0)
    other = jnp.maximum(6 - power, 0)
    lefts_of = patterns([PAIRS[q % 6][0] for q in range(24)])
    rights_of = patterns([PAIRS[q % 6][1] for q in range(24)])
    powers_of = patterns([q // 6 for q in range(rows)])

    def left_of(t):
        u = row_of(phase_ref, t)
        r = 1.0 - u
        powers = jnp.ones((SUB, LANES), f32)
        for base, exponent in ((u, power), (r, other)):
            squared = base * base
            for bit, factor in ((1, base), (2, squared), (4, squared * squared)):
                powers = powers * jnp.where((exponent & bit) != 0, factor, 1.0)
        axes = tile_of(axis_ref, t)
        scaled = axes * row_of(scaled_ref, t)
        products = [pick_rows(scaled, x) * pick_rows(axes, y) for x, y in zip(lefts_of, rights_of)]
        return stacked_parts([products[i % 3] * pick_rows(powers, p) for i, p in enumerate(powers_of)])

    def group(g, _):
        add_blocks(moments, g * STEPS, STEPS, rep, rows, left_of, knot_ref)
        return 0

    if rep > STEPS:
        moments[...] = jnp.zeros_like(moments)
    lax.fori_loop(0, tiles // STEPS, group, 0)
    table = bernstein_products()
    for n in range(6):
        parts = [moments[p * 6 + n] for p in range(7)]

        def product(i, j):
            return sum(c * part for c, part in zip(table[i, j], parts) if c)

        for delta in range(4):
            running = product(3 - delta, 3)
            for j in reversed(range(3 - delta)):
                running = product(j, j + delta) + shift_up(running, 1)
            out_ref[delta * 6 + n] = running


def pack(value, q, message_ref):
    quantities = len(PAIRS) * 4 + 3
    parts = message_ref.shape[0]
    shards = value.shape[0]
    owned = shards // parts
    zero = jnp.zeros((1, LANES), f32)
    for p in range(parts):
        for r in range(owned):
            d = p * owned + r
            message_ref[p, r * quantities + q : r * quantities + q + 1, :] = value[d : d + 1]
        start, stop = p * owned, (p + 1) * owned
        after = value[stop : stop + 1] if stop < shards else zero
        before = value[start - 1 : start] if start else zero
        edge = jnp.where(iota((1, LANES), 1) < LANES // 2, after, before)
        message_ref[p, owned * quantities + q : owned * quantities + q + 1, :] = edge


def resid_kernel(
    mine_ref, other_ref, band_ref, live_ref, design_ref, obs_ref, weight_ref, index_ref, phase_ref, axis_ref, knot_ref,
    params_ref, resid_ref, message_ref, tiled, scaled_ref, moments, solved_ref,
):
    tiles, shards = obs_ref.shape[0], moments.shape[1]
    rep = tiles // shards
    by_tile(design_ref, tiled)
    solved = solve_small([mine_ref[q] + other_ref[q] for q in range(SIGNALS)])
    blocks = SRC_DEV // LANES
    for m in range(5):
        solved_ref[m] = solved[m]
        for b in range(blocks):
            params_ref[m : m + 1, b * LANES : (b + 1) * LANES] = solved[m][b : b + 1, :]
    rows = moments.shape[0]
    axes_of = patterns([q % 3 for q in range(rows)])
    weights_of = [
        [per_sublane([CUBICS[min(q // 3, 3)][c] / 6.0 for q in range(i, i + SUB)], f32) for c in range(4)]
        for i in range(0, rows, SUB)
    ]

    def left_of(t):
        u = row_of(phase_ref, t)
        r = 1.0 - u
        u2, r2 = u * u, r * r
        cubes = [r2 * r, r2 * u, r * u2, u2 * u]
        axes = tile_of(axis_ref, t)
        scaled = axes * row_of(scaled_ref, t)
        return stacked_parts(
            [pick_rows(scaled, x) * sum(c * m for c, m in zip(w, cubes)) for x, w in zip(axes_of, weights_of)]
        )

    def group(g, _):
        for part in range(STEPS // SUB):
            at = pl.ds(pl.multiple_of(g * STEPS + part * SUB, SUB), SUB)
            live = live_ref[at, :]
            index = index_ref[at, :]
            block_of = index // LANES
            lane_of = index - block_of * LANES
            hits = [block_of == b for b in range(blocks)]
            fitted = jnp.zeros((SUB, LANES), f32)
            for m in range(5):
                picked = jnp.zeros((SUB, LANES), f32)
                for b in range(blocks):
                    table = jnp.broadcast_to(solved_ref[m, b : b + 1, :], (SUB, LANES))
                    picked = jnp.where(hits[b], jnp.take_along_axis(table, lane_of, axis=1), picked)
                fitted = fitted + tiled[at, m, :] * picked
            resid = live * (obs_ref[at, :] - fitted)
            resid_ref[at, :] = resid
            scaled_ref[at, :] = weight_ref[at, :] * live * resid
        add_blocks(moments, g * STEPS, STEPS, rep, rows, left_of, knot_ref)
        return 0

    if rep > STEPS:
        moments[...] = jnp.zeros_like(moments)
    lax.fori_loop(0, tiles // STEPS, group, 0)
    for x in range(3):
        running = moments[9 + x]
        for j in reversed(range(3)):
            running = moments[j * 3 + x] + shift_up(running, 1)
        pack(running, x, message_ref)
    for q in range(band_ref.shape[0]):
        pack(band_ref[q], 3 + q, message_ref)


def solve_kernel(place_ref, sums_ref, out_ref):
    quantities = len(PAIRS) * 4 + 3
    owned = out_ref.shape[0] // 4
    ring = -(-(owned + 2) // SUB) * SUB
    order = {pair: n for n, pair in enumerate(PAIRS)}
    row, lane = iota((ring, LANES), 0), iota((ring, LANES), 1)
    inside = row < owned
    after = (row == owned) & (lane < LANES // 2)
    before = (row == ring - 1) & (lane >= LANES // 2)
    edge = (place_ref[0] == place_ref[1] - 1).astype(jnp.int32)
    known = jnp.where(after & (jnp.full((ring, LANES), edge, jnp.int32) == 1), 0.0, 1.0)

    def load(q):
        rows = jnp.concatenate([sums_ref[pl.ds(r * quantities + q, 1), :] for r in range(owned)], 0)
        rest = jnp.broadcast_to(sums_ref[pl.ds(owned * quantities + q, 1), :], (ring - owned, LANES))
        return jnp.where(inside | after | before, jnp.concatenate([rows, rest], 0), 0.0)

    def turn(value, n):
        turned = pltpu.roll(value, n % LANES, 1)
        if n > 0:
            return jnp.where(lane < n, pltpu.roll(turned, 1, 0), turned)
        return jnp.where(lane >= LANES + n, pltpu.roll(turned, ring - 1, 0), turned)

    loaded = [load(q) for q in range(quantities)]

    def band(delta, x, y):
        return loaded[3 + delta * 6 + order[min(x, y), max(x, y)]]

    rhs = loaded[:3]
    scale = [relax_step / (att_ridge + band(0, x, x)) * known for x in range(3)]
    coefs = [rhs[x] * scale[x] for x in range(3)]
    for _ in range(1, ITERS):
        ahead = {(y, delta): turn(coefs[y], -delta) for y in range(3) for delta in range(1, 4)}
        fresh = []
        for x in range(3):
            normal = att_ridge * coefs[x]
            for y in range(3):
                normal = normal + band(0, x, y) * coefs[y]
            for delta in range(1, 4):
                for y in range(3):
                    normal = normal + band(delta, x, y) * ahead[y, delta]
                normal = normal + turn(sum(band(delta, x, y) * coefs[y] for y in range(3)), delta)
            fresh.append(coefs[x] + scale[x] * (rhs[x] - normal))
        coefs = fresh
    for x in range(3):
        for r in range(owned):
            out_ref[pl.ds(r * 4 + x, 1), :] = coefs[x][r : r + 1]


def predict_kernel(
    place_ref, coef_ref, live_ref, resid_ref, phase_ref, axis_ref, knot_ref, att_ref, out_ref, tiled, windows,
):
    tiles, shards = phase_ref.shape[0], coef_ref.shape[0]
    rep = tiles // shards
    by_tile(axis_ref, tiled)
    for x in range(3):
        coefs = coef_ref[:, x, :]
        for j in range(4):
            windows[x * 4 + j] = coefs if j == 0 else shift_down(coefs, j)
        att_ref[x : x + 1, :] = windows[x * 4, pl.ds(place_ref[0], 1), :]
    row = iota((SUB, LANES), 0)

    def group(g, _):
        start = pl.multiple_of(g * SUB, SUB)
        at = pl.ds(start, SUB)
        knots = knot_ref[at, :]
        basis = spline_basis(phase_ref[at, :])
        first = start // rep
        predicted = jnp.zeros((SUB, LANES), f32)
        for j in range(4):
            inner = jnp.zeros((SUB, LANES), f32)
            for x in range(3):
                table = jnp.broadcast_to(windows[x * 4 + j, pl.ds(first, 1), :], (SUB, LANES))
                for k in range(1, SUB // rep):
                    later = jnp.broadcast_to(windows[x * 4 + j, pl.ds(first + k, 1), :], (SUB, LANES))
                    table = jnp.where(row >= k * rep, later, table)
                inner = inner + tiled[at, x, :] * jnp.take_along_axis(table, knots, axis=1)
            predicted = predicted + basis[j] * inner
        out_ref[at, :] = live_ref[at, :] * (resid_ref[at, :] - predicted)
        return 0

    lax.fori_loop(0, tiles // SUB, group, 0)


BOTH = ("src", "ccd")
SMEM = pl.BlockSpec(memory_space=pltpu.SMEM)
VMEM = pl.BlockSpec(memory_space=pltpu.VMEM)
HBM = pl.BlockSpec(memory_space=pltpu.HBM)


def call(kernel, name, scalars, arrays, outs, scratch, space=VMEM):
    return pl.pallas_call(
        kernel,
        name=name,
        out_shape=outs,
        in_specs=[SMEM] * len(scalars) + [space] * len(arrays),
        out_specs=jax.tree.map(lambda _: VMEM, outs),
        scratch_shapes=scratch,
        compiler_params=pltpu.CompilerParams(vmem_limit_bytes=8 << 20),
    )(*scalars, *arrays)


def swapped(value, axis, bit):
    size = lax.axis_size(axis)
    return lax.ppermute(value, axis, [(i, i ^ bit) for i in range(size)])


def summed_over(value, axis):
    size = lax.axis_size(axis)
    if size & (size - 1):
        return lax.psum(value, axis)
    bit = 1
    while bit < size:
        value = value + swapped(value, axis, bit)
        bit *= 2
    return value


def halved(value, mask, keep):
    pair = value.reshape((2, value.shape[0] // 2) + value.shape[1:])
    kept = lax.dynamic_index_in_dim(pair, keep, 0, False)
    sent = lax.dynamic_index_in_dim(pair, 1 - keep, 0, False)
    return kept + swapped(sent, BOTH, mask)


def doubled(value, mask, keep):
    other = swapped(value, BOTH, mask)
    first = jnp.where(keep == 0, value, other)
    second = jnp.where(keep == 0, other, value)
    return jnp.concatenate([first, second], 0)


def on_device(design, observed, weight, phase_frac, axis_factors, source_index, knot_index, counts):
    row_count = observed.shape[0]
    tiles = row_count // LANES
    shards = lax.axis_size("src")
    obs, w, phase, index, knots = (
        a.reshape(tiles, LANES) for a in (observed, weight, phase_frac, source_index, knot_index)
    )
    tiled = pltpu.VMEM((tiles, SUB, LANES), f32)
    dense = pltpu.VMEM((tiles, LANES), f32)
    blocks = SRC_DEV // LANES
    moments, live = call(
        source_kernel, "source_sums", [], [counts, design, obs, w, index],
        (jax.ShapeDtypeStruct((SIGNALS, blocks, LANES), f32), jax.ShapeDtypeStruct((tiles, LANES), f32)),
        [
            pltpu.SMEM(counts.shape, jnp.int32), pltpu.VMEM(design.shape, f32), dense, dense,
            pltpu.VMEM((tiles, LANES), jnp.int32), pltpu.SemaphoreType.DMA((5,)), dense, dense,
            pltpu.VMEM((SRC_DEV // LOW * 80, LOW), f32),
        ],
        HBM,
    )
    band = call(
        band_kernel, "band_sums", [], [live, phase, axis_factors, w, knots],
        jax.ShapeDtypeStruct((24, shards, KNOT_DEV), f32),
        [dense, pltpu.VMEM((48, shards, KNOT_DEV), f32)],
    )
    if lax.axis_size("ccd") == 2:
        other = swapped(moments, "ccd", 1)
    else:
        moments = summed_over(moments, "ccd")
        other = jnp.zeros_like(moments)
    fast = lax.axis_size("ccd") == 2 and shards >= 4 and shards & (shards - 1) == 0
    parts = 4 if fast else 1
    owned = shards // parts
    message_rows = -(-(owned + 1) * 27 // SUB) * SUB
    params, resid, message = call(
        resid_kernel, "residuals", [],
        [moments, other, band, live, design, obs, w, index, phase, axis_factors, knots],
        (
            jax.ShapeDtypeStruct((5, SRC_DEV), f32),
            jax.ShapeDtypeStruct((tiles, LANES), f32),
            jax.ShapeDtypeStruct((parts, message_rows, LANES), f32),
        ),
        [tiled, dense, pltpu.VMEM((16, shards, KNOT_DEV), f32), pltpu.VMEM((5, blocks, LANES), f32)],
    )
    place = lax.axis_index("src")
    if fast:
        upper = lax.axis_index("ccd")
        for shift in range(shards.bit_length() - 1):
            upper = upper ^ ((place >> shift) & 1)
        lower = place & 1
        sums = halved(halved(message, 1, upper), 3, lower)[0]
        bit = 2
        while bit < shards:
            sums = sums + swapped(sums, BOTH, 2 * bit + 1)
            bit *= 2
        part = 2 * upper + lower
    else:
        sums = summed_over(summed_over(message[0], "ccd"), "src")
        part = jnp.zeros_like(place)
    coefs = call(
        solve_kernel, "attitude", [jnp.stack([part, jnp.full_like(part, parts)])], [sums],
        jax.ShapeDtypeStruct((owned * 4, LANES), f32), [],
    )
    if fast:
        coefs = doubled(doubled(coefs, 3, lower), 1, upper)
    attitude, residual = call(
        predict_kernel, "predict", [place.reshape(1)],
        [coefs.reshape(shards, 4, LANES), live, resid, phase, axis_factors, knots],
        (jax.ShapeDtypeStruct((3, KNOT_DEV), f32), jax.ShapeDtypeStruct((tiles, LANES), f32)),
        [tiled, pltpu.VMEM((12, shards, KNOT_DEV), f32)],
    )
    return params, attitude, residual.reshape(row_count)


def solution(mesh):
    rows = P(("src", "ccd"))
    wide = P(None, ("src", "ccd"))
    in_specs = (wide, rows, rows, rows, wide, rows, rows, P("src", "ccd", None))
    out_specs = (P(None, "src"), P(None, "src"), rows)
    return jax.shard_map(on_device, mesh=mesh, in_specs=in_specs, out_specs=out_specs, check_vma=False)
```

time: 47.2 us -> 40.7 us (0.86)
  Pallas kernels: 15.7 us -> 9.13 us
    pallas_call x5, Pallas kernels: 15.7 us -> 9.13 us  [call(): pl.pallas_call(kernel, name=name, out_shape=outs, in_specs=[SMEM] * len(s...]
  transfers between devices with their start and end apart: 8 -> 8, of which waited for: 7 -> 7; matrix products, arithmetic and copies ran while one was open for 0% -> 0% of each run, Pallas kernels for 9% -> 5%
where the time goes in v3:
time: 40.7 us; the launch traced here: 40.3 us
  waiting for transfers between devices  16.5 us (41%)
  starting transfers between devices  9.8 us (24%)
  Pallas kernels  9.13 us (22%)
  local copies, waits for them, and re-layouts  3.93 us (10%)
  between operations  0.77 us (2%)
    ppermute x8, waiting for transfers between devices, swapped(): return lax.ppermute(value, axis, [(i, i ^ bit) for i in range(size)])  16.5 us
    ppermute x8, starting transfers between devices, swapped(): return lax.ppermute(value, axis, [(i, i ^ bit) for i in range(size)])  9.8 us
    pallas_call x5, Pallas kernels, call(): pl.pallas_call(kernel, name=name, out_shape=outs, in_specs=[SMEM] * len(s...  9.13 us
    unnamed x24, local copies, waits for them, and re-layouts  3.9 us
  transfers between devices with their start and end apart: 8, of which 7 were waited for; matrix products, arithmetic and copies ran while one was open for 0% of the time, Pallas kernels for 5%

profile of v3, /device:TPU:0, one launch (start us, length us, event | category | flops | bytes accessed | tf_op | source)
XLA Modules:
  0.0 40.3 jit_solution(2472202185570437550)
XLA Ops:
  0.6 0.6 %copy-done.11 = s32[1,1,16]{2,1,0:T(1,128)S(1)} copy-done((s32[1,1,16]{2,1,0:T(1,128)S(1)}, s32[1,1,16]{2,1,0:T(1,128)}, u32[]{:S(2)}) %copy-start.11) | copy-done | bytes 88
  1.3 0.9 %copy-done.1 = f32[5,8192]{1,0:T(8,128)S(1)} copy-done((f32[5,8192]{1,0:T(8,128)S(1)}, f32[5,8192]{1,0:T(8,128)}, u32[]{:S(2)}) %copy-start.1) | copy-done | bytes 163864
  2.2 0.8 %copy-done.5 = f32[8192]{0:T(1024)S(1)} copy-done((f32[8192]{0:T(1024)S(1)}, f32[8192]{0:T(1024)}, u32[]{:S(2)}) %copy-start.5) | copy-done | bytes 32792
  3.0 0.8 %copy-done.7 = f32[8192]{0:T(1024)S(1)} copy-done((f32[8192]{0:T(1024)S(1)}, f32[8192]{0:T(1024)}, u32[]{:S(2)}) %copy-start.7) | copy-done | bytes 32792
  3.8 0.8 %copy-done.9 = s32[8192]{0:T(1024)S(1)} copy-done((s32[8192]{0:T(1024)S(1)}, s32[8192]{0:T(1024)}, u32[]{:S(2)}) %copy-start.9) | copy-done | bytes 32792
  4.5 2.8 %source_sums.1 = (f32[20,8,128]{2,1,0:T(8,128)S(1)}, f32[64,128]{1,0:T(8,128)S(1)}) custom-call(s32[1,1,16]{2,1,0:T(1,128)S(1)} %copy-done.11, f32[5,8192]{1,0:T(8,128)S(1)} %copy-done.1, f32[64,128]{1,0:T(8,128)S(1)} %bitcast.28, f32[64,128]{1,0:T(8,128)S(1)} %bitcast.22, s32[64,128]{1,0:T(8,128)S(1)} %bitcast.30), custom_call_target="tpu_custom_call" | custom-call | tf_op jit(solution)/shard_map/source_sums/pallas_call | solution.py:468
  7.4 0.6 %collective-permute-start = (f32[20,8,128]{2,1,0:T(8,128)S(1)}, f32[20,8,128]{2,1,0:T(8,128)S(1)}, u32[]{:S(2)}, u32[]{:S(2)}) collective-permute-start(f32[20,8,128]{2,1,0:T(8,128)S(1)} %get-tuple-element.10.mine_ref), channel_id=1, source_target_pairs={{0,1},{1,0},{2,3},{3,2},{4,5},{5,4},{6,7},{7,6},{8,9},{9,8},{10,11... | collective-permute-start | bytes 245768 | tf_op jit(solution)/shard_map/ppermute | solution.py:481
  8.0 1.9 %band_sums.1.band_ref = f32[24,16,128]{2,1,0:T(8,128)S(1)} custom-call(f32[64,128]{1,0:T(8,128)S(1)} %get-tuple-element.11.live_ref, f32[64,128]{1,0:T(8,128)S(1)} %bitcast.16, f32[3,8192]{1,0:T(4,128)S(1)} %copy-done, f32[64,128]{1,0:T(8,128)S(1)} %bitcast.23, s32[64,128]{1,0:T(8,128)S(1)} %bitcast.19), custom_call_target="tpu_custom_call" | custom-call | tf_op jit(solution)/shard_map/band_sums/pallas_call | solution.py:468
  9.9 2.2 %residuals.1 = (f32[5,1024]{1,0:T(8,128)}, f32[64,128]{1,0:T(8,128)S(1)}, f32[4,136,128]{2,1,0:T(8,128)S(1)}) custom-call(f32[20,8,128]{2,1,0:T(8,128)S(1)} %get-tuple-element.10.mine_ref, f32[20,8,128]{2,1,0:T(8,128)S(1)} %collective-permute-done.other_ref, f32[24,16,128]{2,1,0:T(8,128)S(1)} %band_sums.1.band_ref, ...), custom_call_target="tpu_custom_call" | custom-call | tf_op jit(solution)/shard_map/residuals/pallas_call | solution.py:468
  12.2 1.3 %collective-permute-done.1 = f32[2,136,128]{2,1,0:T(8,128)S(1)} collective-permute-done((f32[2,136,128]{2,1,0:T(8,128)S(1)}, f32[2,136,128]{2,1,0:T(8,128)S(1)}, u32[]{:S(2)}, u32[]{:S(2)}) %collective-permute-start.1) | collective-permute-done | bytes 139296 | tf_op jit(solution)/shard_map/ppermute | solution.py:481
  13.6 2.7 %collective-permute-start.2 = (f32[1,136,128]{2,1,0:T(8,128)S(1)}, f32[1,136,128]{2,1,0:T(8,128)S(1)}, u32[]{:S(2)}, u32[]{:S(2)}) collective-permute-start(f32[1,136,128]{2,1,0:T(8,128)S(1)} %constant_dynamic-slice_fusion), channel_id=1, source_target_pairs={{0,3},{1,2},{2,1},{3,0},{4,7},{5,6},{6,5},{7,4},{8,11},{9,10},{10,... | collective-permute-start | bytes 208904 | tf_op jit(solution)/shard_map/ppermute | solution.py:481
  16.3 2.4 %collective-permute-done.2 = f32[1,136,128]{2,1,0:T(8,128)S(1)} collective-permute-done((f32[1,136,128]{2,1,0:T(8,128)S(1)}, f32[1,136,128]{2,1,0:T(8,128)S(1)}, u32[]{:S(2)}, u32[]{:S(2)}) %collective-permute-start.2) | collective-permute-done | bytes 69664 | tf_op jit(solution)/shard_map/ppermute | solution.py:481
  18.7 1.6 %collective-permute-start.3 = (f32[136,128]{1,0:T(8,128)S(1)}, f32[136,128]{1,0:T(8,128)S(1)}, u32[]{:S(2)}, u32[]{:S(2)}) collective-permute-start(f32[136,128]{1,0:T(8,128)S(1)} %add_bitcast_fusion), channel_id=1, source_target_pairs={{0,5},{1,4},{2,7},{3,6},{4,1},{5,0},{6,3},{7,2},{8,13},{9,12},{10,... | collective-permute-start | bytes 208904 | tf_op jit(solution)/shard_map/ppermute | solution.py:481
  20.3 2.6 %collective-permute-done.3 = f32[136,128]{1,0:T(8,128)S(1)} collective-permute-done((f32[136,128]{1,0:T(8,128)S(1)}, f32[136,128]{1,0:T(8,128)S(1)}, u32[]{:S(2)}, u32[]{:S(2)}) %collective-permute-start.3) | collective-permute-done | bytes 69664 | tf_op jit(solution)/shard_map/ppermute | solution.py:481
  22.9 1.4 %collective-permute-start.4 = (f32[136,128]{1,0:T(8,128)S(1)}, f32[136,128]{1,0:T(8,128)S(1)}, u32[]{:S(2)}, u32[]{:S(2)}) collective-permute-start(f32[136,128]{1,0:T(8,128)S(1)} %add.41), channel_id=1, source_target_pairs={{0,9},{1,8},{2,11},{3,10},{4,13},{5,12},{6,15},{7,14},{8,1},{9,0},... | collective-permute-start | bytes 208904 | tf_op jit(solution)/shard_map/ppermute | solution.py:481
  24.4 2.8 %collective-permute-done.4 = f32[136,128]{1,0:T(8,128)S(1)} collective-permute-done((f32[136,128]{1,0:T(8,128)S(1)}, f32[136,128]{1,0:T(8,128)S(1)}, u32[]{:S(2)}, u32[]{:S(2)}) %collective-permute-start.4) | collective-permute-done | bytes 69664 | tf_op jit(solution)/shard_map/ppermute | solution.py:481
  27.1 2.3 %collective-permute-start.5 = (f32[136,128]{1,0:T(8,128)S(1)}, f32[136,128]{1,0:T(8,128)S(1)}, u32[]{:S(2)}, u32[]{:S(2)}) collective-permute-start(f32[136,128]{1,0:T(8,128)S(1)} %add.42), channel_id=1, source_target_pairs={{0,17},{1,16},{2,19},{3,18},{4,21},{5,20},{6,23},{7,22},{8,25},{9,... | collective-permute-start | bytes 208904 | tf_op jit(solution)/shard_map/ppermute | solution.py:481
  29.5 4.3 %collective-permute-done.5 = f32[136,128]{1,0:T(8,128)S(1)} collective-permute-done((f32[136,128]{1,0:T(8,128)S(1)}, f32[136,128]{1,0:T(8,128)S(1)}, u32[]{:S(2)}, u32[]{:S(2)}) %collective-permute-start.5) | collective-permute-done | bytes 69664 | tf_op jit(solution)/shard_map/ppermute | solution.py:481
  33.7 0.7 %attitude.1 = f32[16,128]{1,0:T(8,128)S(1)} custom-call(s32[2]{0:T(128)S(1)} %pad_add_fusion.place_ref, f32[136,128]{1,0:T(8,128)S(1)} %add.43.sums_ref), custom_call_target="tpu_custom_call" | custom-call | tf_op jit(solution)/shard_map/attitude/pallas_call | solution.py:468
  34.5 1.0 %collective-permute-start.6 = (f32[16,128]{1,0:T(8,128)S(1)}, f32[16,128]{1,0:T(8,128)S(1)}, u32[]{:S(2)}, u32[]{:S(2)}) collective-permute-start(f32[16,128]{1,0:T(8,128)S(1)} %attitude.1), channel_id=1, source_target_pairs={{0,3},{1,2},{2,1},{3,0},{4,7},{5,6},{6,5},{7,4},{8,11},{9,10},{10,... | collective-permute-start | bytes 24584 | tf_op jit(solution)/shard_map/ppermute | solution.py:481
  35.5 2.2 %collective-permute-done.6 = f32[16,128]{1,0:T(8,128)S(1)} collective-permute-done((f32[16,128]{1,0:T(8,128)S(1)}, f32[16,128]{1,0:T(8,128)S(1)}, u32[]{:S(2)}, u32[]{:S(2)}) %collective-permute-start.6) | collective-permute-done | bytes 8224 | tf_op jit(solution)/shard_map/ppermute | solution.py:481
  37.7 0.2 collective-permute-start.7
  37.8 1.0 %collective-permute-done.7 = f32[32,128]{1,0:T(8,128)S(1)} collective-permute-done((f32[32,128]{1,0:T(8,128)S(1)}, f32[32,128]{1,0:T(8,128)S(1)}, u32[]{:S(2)}, u32[]{:S(2)}) %collective-permute-start.7) | collective-permute-done | bytes 16416 | tf_op jit(solution)/shard_map/ppermute | solution.py:481
  38.8 1.5 %predict.1 = (f32[3,128]{1,0:T(4,128)}, f32[64,128]{1,0:T(8,128)}) custom-call(s32[1]{0:T(128)} %bitcast.5.place_ref, f32[16,4,128]{2,1,0:T(4,128)S(1)} %bitcast.27, f32[64,128]{1,0:T(8,128)S(1)} %get-tuple-element.11.live_ref, f32[64,128]{1,0:T(8,128)S(1)} %get-tuple-element.14.resid_ref, f32[64,128]{1,0:T(8,128)S(1)} %bitcast.18, f32[3,8192]{1,0:T(4,128)S(1)} %copy-done, ...), custom_call_target="tpu_custom_call" | custom-call | tf_op jit(solution)/shard_map/predict/pallas_call | solution.py:468
  (33 shorter events, 0.3 us)
Async XLA Ops:
  0.6 0.7 %copy-start.11 = (s32[1,1,16]{2,1,0:T(1,128)S(1)}, s32[1,1,16]{2,1,0:T(1,128)}, u32[]{:S(2)}) copy-start(s32[1,1,16]{2,1,0:T(1,128)} %counts_hbm.1) | copy-start | bytes 196
  1.3 0.9 %copy-start.1 = (f32[5,8192]{1,0:T(8,128)S(1)}, f32[5,8192]{1,0:T(8,128)}, u32[]{:S(2)}) copy-start(f32[5,8192]{1,0:T(8,128)} %design_ref.1) | copy-start | bytes 491524
  2.2 0.8 %copy-start.5 = (f32[8192]{0:T(1024)S(1)}, f32[8192]{0:T(1024)}, u32[]{:S(2)}) copy-start(f32[8192]{0:T(1024)} %param.10) | copy-start | bytes 98308
  3.0 0.8 %copy-start.7 = (f32[8192]{0:T(1024)S(1)}, f32[8192]{0:T(1024)}, u32[]{:S(2)}) copy-start(f32[8192]{0:T(1024)} %param.9) | copy-start | bytes 98308
  3.8 0.8 %copy-start.9 = (s32[8192]{0:T(1024)S(1)}, s32[8192]{0:T(1024)}, u32[]{:S(2)}) copy-start(s32[8192]{0:T(1024)} %param.13) | copy-start | bytes 98308
  4.5 3.4 %copy-start = (f32[3,8192]{1,0:T(4,128)S(1)}, f32[3,8192]{1,0:T(4,128)}, u32[]{:S(2)}) copy-start(f32[3,8192]{1,0:T(4,128)} %axis_ref.5) | copy-start | bytes 294916
  4.5 3.4 %copy-start.3 = (f32[8192]{0:T(1024)S(1)}, f32[8192]{0:T(1024)}, u32[]{:S(2)}) copy-start(f32[8192]{0:T(1024)} %param.11) | copy-start | bytes 98308
  4.5 3.4 %copy-start.4 = (s32[8192]{0:T(1024)S(1)}, s32[8192]{0:T(1024)}, u32[]{:S(2)}) copy-start(s32[8192]{0:T(1024)} %param.14) | copy-start | bytes 98308
  4.5 3.4 %copy-start.6 = (f32[8192]{0:T(1024)S(1)}, f32[8192]{0:T(1024)}, u32[]{:S(2)}) copy-start(f32[8192]{0:T(1024)} %param.10) | copy-start | bytes 98308
  7.4 2.5 %copy-start.2 = (f32[5,8192]{1,0:T(8,128)S(1)}, f32[5,8192]{1,0:T(8,128)}, u32[]{:S(2)}) copy-start(f32[5,8192]{1,0:T(8,128)} %design_ref.1) | copy-start | bytes 491524
  7.4 2.5 %collective-permute-start = (f32[20,8,128]{2,1,0:T(8,128)S(1)}, f32[20,8,128]{2,1,0:T(8,128)S(1)}, u32[]{:S(2)}, u32[]{:S(2)}) collective-permute-start(f32[20,8,128]{2,1,0:T(8,128)S(1)} %get-tuple-element.10.mine_ref), channel_id=1, source_target_pairs={{0,1},{1,0},{2,3},{3,2},{4,5},{5,4},{6,7},{7,6},{8,9},{9,8},{10,11... | collective-permute-start | bytes 245768 | tf_op jit(solution)/shard_map/ppermute | solution.py:481
  8.0 1.9 %copy-start.8 = (f32[8192]{0:T(1024)S(1)}, f32[8192]{0:T(1024)}, u32[]{:S(2)}) copy-start(f32[8192]{0:T(1024)} %param.9) | copy-start | bytes 98308
  8.0 1.9 %copy-start.10 = (s32[8192]{0:T(1024)S(1)}, s32[8192]{0:T(1024)}, u32[]{:S(2)}) copy-start(s32[8192]{0:T(1024)} %param.13) | copy-start | bytes 98308
  12.1 1.4 %collective-permute-start.1 = (f32[2,136,128]{2,1,0:T(8,128)S(1)}, f32[2,136,128]{2,1,0:T(8,128)S(1)}, u32[]{:S(2)}, u32[]{:S(2)}) collective-permute-start(f32[2,136,128]{2,1,0:T(8,128)S(1)} %dynamic-slice_bitcast_fusion), channel_id=1, source_target_pairs={{0,1},{1,0},{2,3},{3,2},{4,5},{5,4},{6,7},{7,6},{8,9},{9,8},{10,11... | collective-permute-start | bytes 417800 | tf_op jit(solution)/shard_map/ppermute | solution.py:481
  13.6 5.1 %collective-permute-start.2 = (f32[1,136,128]{2,1,0:T(8,128)S(1)}, f32[1,136,128]{2,1,0:T(8,128)S(1)}, u32[]{:S(2)}, u32[]{:S(2)}) collective-permute-start(f32[1,136,128]{2,1,0:T(8,128)S(1)} %constant_dynamic-slice_fusion), channel_id=1, source_target_pairs={{0,3},{1,2},{2,1},{3,0},{4,7},{5,6},{6,5},{7,4},{8,11},{9,10},{10,... | collective-permute-start | bytes 208904 | tf_op jit(solution)/shard_map/ppermute | solution.py:481
  18.7 4.2 %collective-permute-start.3 = (f32[136,128]{1,0:T(8,128)S(1)}, f32[136,128]{1,0:T(8,128)S(1)}, u32[]{:S(2)}, u32[]{:S(2)}) collective-permute-start(f32[136,128]{1,0:T(8,128)S(1)} %add_bitcast_fusion), channel_id=1, source_target_pairs={{0,5},{1,4},{2,7},{3,6},{4,1},{5,0},{6,3},{7,2},{8,13},{9,12},{10,... | collective-permute-start | bytes 208904 | tf_op jit(solution)/shard_map/ppermute | solution.py:481
  22.9 4.2 %collective-permute-start.4 = (f32[136,128]{1,0:T(8,128)S(1)}, f32[136,128]{1,0:T(8,128)S(1)}, u32[]{:S(2)}, u32[]{:S(2)}) collective-permute-start(f32[136,128]{1,0:T(8,128)S(1)} %add.41), channel_id=1, source_target_pairs={{0,9},{1,8},{2,11},{3,10},{4,13},{5,12},{6,15},{7,14},{8,1},{9,0},... | collective-permute-start | bytes 208904 | tf_op jit(solution)/shard_map/ppermute | solution.py:481
  27.1 6.6 %collective-permute-start.5 = (f32[136,128]{1,0:T(8,128)S(1)}, f32[136,128]{1,0:T(8,128)S(1)}, u32[]{:S(2)}, u32[]{:S(2)}) collective-permute-start(f32[136,128]{1,0:T(8,128)S(1)} %add.42), channel_id=1, source_target_pairs={{0,17},{1,16},{2,19},{3,18},{4,21},{5,20},{6,23},{7,22},{8,25},{9,... | collective-permute-start | bytes 208904 | tf_op jit(solution)/shard_map/ppermute | solution.py:481
  34.5 3.1 %collective-permute-start.6 = (f32[16,128]{1,0:T(8,128)S(1)}, f32[16,128]{1,0:T(8,128)S(1)}, u32[]{:S(2)}, u32[]{:S(2)}) collective-permute-start(f32[16,128]{1,0:T(8,128)S(1)} %attitude.1), channel_id=1, source_target_pairs={{0,3},{1,2},{2,1},{3,0},{4,7},{5,6},{6,5},{7,4},{8,11},{9,10},{10,... | collective-permute-start | bytes 24584 | tf_op jit(solution)/shard_map/ppermute | solution.py:481
  37.7 1.2 %collective-permute-start.7 = (f32[32,128]{1,0:T(8,128)S(1)}, f32[32,128]{1,0:T(8,128)S(1)}, u32[]{:S(2)}, u32[]{:S(2)}) collective-permute-start(f32[32,128]{1,0:T(8,128)S(1)} %pad_maximum_fusion.1), channel_id=1, source_target_pairs={{0,1},{1,0},{2,3},{3,2},{4,5},{5,4},{6,7},{7,6},{8,9},{9,8},{10,11... | collective-permute-start | bytes 49160 | tf_op jit(solution)/shard_map/ppermute | solution.py:481

commit v4 on v3

--- a/solution.py
+++ b/solution.py
@@ -1,3 +1,5 @@
+import math
+
 import jax
 import jax.numpy as jnp
 from jax import lax
@@ -11,7 +13,9 @@
 LANES = 128
 SUB = 8
 LOW = 256
-STEPS = 16
+QUANTITIES = 3 + 4 * 6
+REACH = 3 * (ITERS - 1)
+PER_ROW = LANES // (2 * REACH)
 CUBICS = [(1.0, 0.0, 0.0, 0.0), (4.0, 12.0, 6.0, 1.0), (1.0, 6.0, 12.0, 4.0), (0.0, 0.0, 0.0, 1.0)]
 SIGNALS = 15 + 5
 PAIRS = [(x, y) for x in range(3) for y in range(x, 3)]
@@ -93,6 +97,19 @@
     return lax.broadcasted_iota(jnp.int32, shape, axis)
 
 
+def over_steps(tiles, body):
+    steps = math.gcd(tiles, 64)
+    if steps == tiles:
+        body(0, steps)
+        return
+
+    def one(g, _):
+        body(pl.multiple_of(g * steps, steps), steps)
+        return 0
+
+    lax.fori_loop(0, tiles // steps, one, 0)
+
+
 def spread_row(index_row, count):
     packed = jnp.broadcast_to(index_row, (2 * SUB, LANES)).astype(bf16)
     return jnp.concatenate([packed] * (count // (2 * SUB)), 0)
@@ -113,7 +130,8 @@
 
 
 def tile_of(wide_ref, t):
-    block = wide_ref[:, pl.ds(pl.multiple_of(t * LANES, LANES), LANES)]
+    start = t * LANES if isinstance(t, int) else pl.multiple_of(t * LANES, LANES)
+    block = wide_ref[:, pl.ds(start, LANES)]
     return jnp.concatenate([block, jnp.zeros((SUB - block.shape[0], LANES), f32)], 0)
 
 
@@ -202,12 +220,14 @@
     ]
     for copy in copies:
         copy.start()
-    total[...] = jnp.zeros_like(total)
+    if math.gcd(tiles, 64) != tiles:
+        total[...] = jnp.zeros_like(total)
     highs = SRC_DEV // LOW
     pairs = [(m, n) for m in range(5) for n in range(m, 5)] + [(m, 5) for m in range(5)]
+    pairs += pairs[2 * SUB :]
     lefts_of = patterns([m for m, _ in pairs])
     rights_of = patterns([n for _, n in pairs])
-    rows = SUB * len(lefts_of)
+    first_half = iota((SUB, LANES), 0) < SUB // 2
     is_observed = iota((SUB, LANES), 0) == 5
     copies[0].wait()
     slots = iota((rep, LANES), 0) * LANES + iota((rep, LANES), 1)
@@ -224,28 +244,39 @@
     copies[3].wait()
     copies[4].wait()
 
-    def group(g, _):
-        start = g * STEPS
+    def group(start, steps):
         lefts, rights = [], []
-        for i in range(STEPS):
+        for i in range(steps):
             t = start + i
             values = jnp.where(is_observed, row_of(obs_ref, t), tile_of(design_ref, t))
             scaled = values * row_of(weight_ref, t)
-            block = stacked_parts([pick_rows(scaled, m) * pick_rows(values, n) for m, n in zip(lefts_of, rights_of)])
+            products = [pick_rows(scaled, m) * pick_rows(values, n) for m, n in zip(lefts_of, rights_of)]
+            high, middle, low = split3(products[2])
+            parts = split3(jnp.concatenate(products[:2], 0)) + [jnp.where(first_half, high, middle), low]
+            block = jnp.concatenate(parts, 0).astype(bf16)
             packed = spread_row(high_ref[pl.ds(t, 1), :], 2 * SUB)
             masks = [is_equal(packed, jnp.full((), h, bf16)) for h in range(highs)]
             repeats = block.shape[0] // (2 * SUB)
             lefts.append(jnp.concatenate([block * jnp.concatenate([mask] * repeats, 0) for mask in masks], 0))
             rights.append(onehot(low_ref[pl.ds(t, 1), :], LOW))
-        total[...] += contract(jnp.concatenate(lefts, 1), jnp.concatenate(rights, 1))
-        return 0
-
-    lax.fori_loop(0, tiles // STEPS, group, 0)
+        got = contract(jnp.concatenate(lefts, 1), jnp.concatenate(rights, 1))
+        if steps == tiles:
+            total[...] = got
+        else:
+            total[...] += got
+
+    over_steps(tiles, group)
     height = total.shape[0] // highs
+    wide, half_tile = 2 * SUB, SUB // 2
     for h in range(highs):
-        summed = sum_parts(total[h * height : (h + 1) * height, :], rows)
+        block = total[h * height : (h + 1) * height, :]
+        tail = block[3 * wide :]
+        summed = sum_parts(block, wide)
+        rest = tail[0:half_tile] + tail[half_tile : 2 * half_tile] + tail[2 * half_tile : 3 * half_tile]
         for half in range(LOW // LANES):
-            out_ref[:, h * (LOW // LANES) + half, :] = summed[0:SIGNALS, half * LANES : (half + 1) * LANES]
+            cols = slice(half * LANES, (half + 1) * LANES)
+            out_ref[0:wide, h * (LOW // LANES) + half, :] = summed[:, cols]
+            out_ref[wide:SIGNALS, h * (LOW // LANES) + half, :] = rest[:, cols]
 
 
 def band_kernel(live_ref, phase_ref, axis_ref, weight_ref, knot_ref, out_ref, scaled_ref, moments):
@@ -272,13 +303,12 @@
         products = [pick_rows(scaled, x) * pick_rows(axes, y) for x, y in zip(lefts_of, rights_of)]
         return stacked_parts([products[i % 3] * pick_rows(powers, p) for i, p in enumerate(powers_of)])
 
-    def group(g, _):
-        add_blocks(moments, g * STEPS, STEPS, rep, rows, left_of, knot_ref)
-        return 0
-
-    if rep > STEPS:
+    def group(start, steps):
+        add_blocks(moments, start, steps, rep, rows, left_of, knot_ref)
+
+    if rep > math.gcd(tiles, 64):
         moments[...] = jnp.zeros_like(moments)
-    lax.fori_loop(0, tiles // STEPS, group, 0)
+    over_steps(tiles, group)
     table = bernstein_products()
     for n in range(6):
         parts = [moments[p * 6 + n] for p in range(7)]
@@ -293,26 +323,33 @@
             out_ref[delta * 6 + n] = running
 
 
-def pack(value, q, message_ref):
-    quantities = len(PAIRS) * 4 + 3
+def halo_rows():
+    return -(-QUANTITIES // PER_ROW)
+
+
+def pack(source_ref, index, q, message_ref, packed):
     parts = message_ref.shape[0]
-    shards = value.shape[0]
-    owned = shards // parts
-    zero = jnp.zeros((1, LANES), f32)
+    owned = source_ref.shape[1] // parts
     for p in range(parts):
-        for r in range(owned):
-            d = p * owned + r
-            message_ref[p, r * quantities + q : r * quantities + q + 1, :] = value[d : d + 1]
-        start, stop = p * owned, (p + 1) * owned
-        after = value[stop : stop + 1] if stop < shards else zero
-        before = value[start - 1 : start] if start else zero
-        edge = jnp.where(iota((1, LANES), 1) < LANES // 2, after, before)
-        message_ref[p, owned * quantities + q : owned * quantities + q + 1, :] = edge
+        message_ref[p, q * owned : (q + 1) * owned, :] = source_ref[index, p * owned : (p + 1) * owned, :]
+    if parts == 1:
+        return packed
+    row, lane = iota((SUB, LANES), 0), iota((SUB, LANES), 1)
+    blank = jnp.zeros((SUB - parts + 1, LANES), f32)
+    after = jnp.concatenate([source_ref[index, pl.ds(owned, parts - 1, stride=owned), :], blank], 0)
+    before = jnp.concatenate([source_ref[index, pl.ds(owned - 1, parts - 1, stride=owned), :], blank], 0)
+    before = pltpu.roll(before, 1, 0)
+    edge = jnp.where(lane < LANES // 2, after, jnp.where(row == 0, 0.0, before))
+    place, slot = q // PER_ROW, q % PER_ROW
+    width = 2 * REACH
+    edge = pltpu.roll(edge, (REACH + width * slot) % LANES, 1)
+    mine = (lane >= width * slot) & (lane < width * (slot + 1))
+    return [jnp.where(mine, edge, row_) if i == place else row_ for i, row_ in enumerate(packed)]
 
 
 def resid_kernel(
     mine_ref, other_ref, band_ref, live_ref, design_ref, obs_ref, weight_ref, index_ref, phase_ref, axis_ref, knot_ref,
-    params_ref, resid_ref, message_ref, tiled, scaled_ref, moments, solved_ref,
+    params_ref, resid_ref, message_ref, tiled, scaled_ref, moments, solved_ref, rhs_ref,
 ):
     tiles, shards = obs_ref.shape[0], moments.shape[1]
     rep = tiles // shards
@@ -341,9 +378,9 @@
             [pick_rows(scaled, x) * sum(c * m for c, m in zip(w, cubes)) for x, w in zip(axes_of, weights_of)]
         )
 
-    def group(g, _):
-        for part in range(STEPS // SUB):
-            at = pl.ds(pl.multiple_of(g * STEPS + part * SUB, SUB), SUB)
+    def group(start, steps):
+        for part in range(steps // SUB):
+            at = pl.ds(start + part * SUB, SUB)
             live = live_ref[at, :]
             index = index_ref[at, :]
             block_of = index // LANES
@@ -359,36 +396,43 @@
             resid = live * (obs_ref[at, :] - fitted)
             resid_ref[at, :] = resid
             scaled_ref[at, :] = weight_ref[at, :] * live * resid
-        add_blocks(moments, g * STEPS, STEPS, rep, rows, left_of, knot_ref)
-        return 0
-
-    if rep > STEPS:
+        add_blocks(moments, start, steps, rep, rows, left_of, knot_ref)
+
+    if rep > math.gcd(tiles, 64):
         moments[...] = jnp.zeros_like(moments)
-    lax.fori_loop(0, tiles // STEPS, group, 0)
+    over_steps(tiles, group)
+    parts = message_ref.shape[0]
+    packed = [jnp.zeros((SUB, LANES), f32)] * halo_rows()
     for x in range(3):
         running = moments[9 + x]
         for j in reversed(range(3)):
             running = moments[j * 3 + x] + shift_up(running, 1)
-        pack(running, x, message_ref)
+        rhs_ref[x] = running
+        packed = pack(rhs_ref, x, x, message_ref, packed)
     for q in range(band_ref.shape[0]):
-        pack(band_ref[q], 3 + q, message_ref)
+        packed = pack(band_ref, q, 3 + q, message_ref, packed)
+    first = QUANTITIES * (shards // parts)
+    for p in range(parts):
+        for i, row in enumerate(packed):
+            message_ref[p, first + i : first + i + 1, :] = row[p : p + 1]
 
 
 def solve_kernel(place_ref, sums_ref, out_ref):
-    quantities = len(PAIRS) * 4 + 3
     owned = out_ref.shape[0] // 4
     ring = -(-(owned + 2) // SUB) * SUB
     order = {pair: n for n, pair in enumerate(PAIRS)}
     row, lane = iota((ring, LANES), 0), iota((ring, LANES), 1)
     inside = row < owned
-    after = (row == owned) & (lane < LANES // 2)
-    before = (row == ring - 1) & (lane >= LANES // 2)
+    after = (row == owned) & (lane < REACH)
+    before = (row == ring - 1) & (lane >= LANES - REACH)
     edge = (place_ref[0] == place_ref[1] - 1).astype(jnp.int32)
     known = jnp.where(after & (jnp.full((ring, LANES), edge, jnp.int32) == 1), 0.0, 1.0)
 
     def load(q):
-        rows = jnp.concatenate([sums_ref[pl.ds(r * quantities + q, 1), :] for r in range(owned)], 0)
-        rest = jnp.broadcast_to(sums_ref[pl.ds(owned * quantities + q, 1), :], (ring - owned, LANES))
+        rows = sums_ref[q * owned : (q + 1) * owned, :]
+        rest = sums_ref[pl.ds(QUANTITIES * owned + q // PER_ROW, 1), :]
+        rest = jnp.broadcast_to(rest, (ring - owned, LANES))
+        rest = pltpu.roll(rest, (-(REACH + 2 * REACH * (q % PER_ROW))) % LANES, 1)
         return jnp.where(inside | after | before, jnp.concatenate([rows, rest], 0), 0.0)
 
     def turn(value, n):
@@ -397,7 +441,7 @@
             return jnp.where(lane < n, pltpu.roll(turned, 1, 0), turned)
         return jnp.where(lane >= LANES + n, pltpu.roll(turned, ring - 1, 0), turned)
 
-    loaded = [load(q) for q in range(quantities)]
+    loaded = [load(q) for q in range(QUANTITIES)]
 
     def band(delta, x, y):
         return loaded[3 + delta * 6 + order[min(x, y), max(x, y)]]
@@ -423,12 +467,24 @@
             out_ref[pl.ds(r * 4 + x, 1), :] = coefs[x][r : r + 1]
 
 
-def predict_kernel(
-    place_ref, coef_ref, live_ref, resid_ref, phase_ref, axis_ref, knot_ref, att_ref, out_ref, tiled, windows,
-):
-    tiles, shards = phase_ref.shape[0], coef_ref.shape[0]
+def prepare_kernel(_, live_ref, phase_ref, axis_ref, out_ref, tiled):
+    by_tile(axis_ref, tiled)
+
+    def group(start, steps):
+        for part in range(steps // SUB):
+            at = pl.ds(start + part * SUB, SUB)
+            basis = [b * live_ref[at, :] for b in spline_basis(phase_ref[at, :])]
+            for x in range(3):
+                along = tiled[at, x, :]
+                for j in range(4):
+                    out_ref[x * 4 + j, at, :] = along * basis[j]
+
+    over_steps(phase_ref.shape[0], group)
+
+
+def predict_kernel(place_ref, coef_ref, factor_ref, resid_ref, knot_ref, att_ref, out_ref, windows):
+    tiles, shards = resid_ref.shape[0], coef_ref.shape[0]
     rep = tiles // shards
-    by_tile(axis_ref, tiled)
     for x in range(3):
         coefs = coef_ref[:, x, :]
         for j in range(4):
@@ -436,26 +492,21 @@
         att_ref[x : x + 1, :] = windows[x * 4, pl.ds(place_ref[0], 1), :]
     row = iota((SUB, LANES), 0)
 
-    def group(g, _):
-        start = pl.multiple_of(g * SUB, SUB)
-        at = pl.ds(start, SUB)
-        knots = knot_ref[at, :]
-        basis = spline_basis(phase_ref[at, :])
-        first = start // rep
-        predicted = jnp.zeros((SUB, LANES), f32)
-        for j in range(4):
-            inner = jnp.zeros((SUB, LANES), f32)
-            for x in range(3):
-                table = jnp.broadcast_to(windows[x * 4 + j, pl.ds(first, 1), :], (SUB, LANES))
+    def group(start, steps):
+        for part in range(steps // SUB):
+            at = pl.ds(start + part * SUB, SUB)
+            knots = knot_ref[at, :]
+            first = (start + part * SUB) // rep
+            left = resid_ref[at, :]
+            for q in range(12):
+                table = jnp.broadcast_to(windows[q, pl.ds(first, 1), :], (SUB, LANES))
                 for k in range(1, SUB // rep):
-                    later = jnp.broadcast_to(windows[x * 4 + j, pl.ds(first + k, 1), :], (SUB, LANES))
+                    later = jnp.broadcast_to(windows[q, pl.ds(first + k, 1), :], (SUB, LANES))
                     table = jnp.where(row >= k * rep, later, table)
-                inner = inner + tiled[at, x, :] * jnp.take_along_axis(table, knots, axis=1)
-            predicted = predicted + basis[j] * inner
-        out_ref[at, :] = live_ref[at, :] * (resid_ref[at, :] - predicted)
-        return 0
-
-    lax.fori_loop(0, tiles // SUB, group, 0)
+                left = left - factor_ref[q, at, :] * jnp.take_along_axis(table, knots, axis=1)
+            out_ref[at, :] = left
+
+    over_steps(tiles, group)
 
 
 BOTH = ("src", "ccd")
@@ -517,12 +568,13 @@
     dense = pltpu.VMEM((tiles, LANES), f32)
     blocks = SRC_DEV // LANES
     moments, live = call(
-        source_kernel, "source_sums", [], [counts, design, obs, w, index],
+        source_kernel, "source_sums", [],
+        [pltpu.with_memory_space_constraint(a, pltpu.HBM) for a in (counts, design, obs, w, index)],
         (jax.ShapeDtypeStruct((SIGNALS, blocks, LANES), f32), jax.ShapeDtypeStruct((tiles, LANES), f32)),
         [
             pltpu.SMEM(counts.shape, jnp.int32), pltpu.VMEM(design.shape, f32), dense, dense,
             pltpu.VMEM((tiles, LANES), jnp.int32), pltpu.SemaphoreType.DMA((5,)), dense, dense,
-            pltpu.VMEM((SRC_DEV // LOW * 80, LOW), f32),
+            pltpu.VMEM((SRC_DEV // LOW * 64, LOW), f32),
         ],
         HBM,
     )
@@ -539,7 +591,7 @@
     fast = lax.axis_size("ccd") == 2 and shards >= 4 and shards & (shards - 1) == 0
     parts = 4 if fast else 1
     owned = shards // parts
-    message_rows = -(-(owned + 1) * 27 // SUB) * SUB
+    message_rows = -(-(QUANTITIES * owned + halo_rows()) // SUB) * SUB
     params, resid, message = call(
         resid_kernel, "residuals", [],
         [moments, other, band, live, design, obs, w, index, phase, axis_factors, knots],
@@ -548,7 +600,12 @@
             jax.ShapeDtypeStruct((tiles, LANES), f32),
             jax.ShapeDtypeStruct((parts, message_rows, LANES), f32),
         ),
-        [tiled, dense, pltpu.VMEM((16, shards, KNOT_DEV), f32), pltpu.VMEM((5, blocks, LANES), f32)],
+        [tiled, dense, pltpu.VMEM((16, shards, KNOT_DEV), f32), pltpu.VMEM((5, blocks, LANES), f32),
+         pltpu.VMEM((3, shards, KNOT_DEV), f32)],
+    )
+    factors = call(
+        prepare_kernel, "prepare", [], [message, live, phase, axis_factors],
+        jax.ShapeDtypeStruct((12, tiles, LANES), f32), [tiled],
     )
     place = lax.axis_index("src")
     if fast:
@@ -572,10 +629,9 @@
     if fast:
         coefs = doubled(doubled(coefs, 3, lower), 1, upper)
     attitude, residual = call(
-        predict_kernel, "predict", [place.reshape(1)],
-        [coefs.reshape(shards, 4, LANES), live, resid, phase, axis_factors, knots],
+        predict_kernel, "predict", [place.reshape(1)], [coefs.reshape(shards, 4, LANES), factors, resid, knots],
         (jax.ShapeDtypeStruct((3, KNOT_DEV), f32), jax.ShapeDtypeStruct((tiles, LANES), f32)),
-        [tiled, pltpu.VMEM((12, shards, KNOT_DEV), f32)],
+        [pltpu.VMEM((12, shards, KNOT_DEV), f32)],
     )
     return params, attitude, residual.reshape(row_count)
 

time: 40.7 us -> 34.1 us (0.84)
  local copies, waits for them, and re-layouts: 3.93 us -> 0.06 us
  waiting for transfers between devices: 16.5 us -> 15 us
  Pallas kernels: 9.13 us -> 8.09 us
    unnamed x24 -> x14, local copies, waits for them, and re-layouts: 3.9 us -> 0.04 us
    ppermute x8, waiting for transfers between devices: 16.5 us -> 15 us  [swapped(): return lax.ppermute(value, axis, [(i, i ^ bit) for i in range(size)])]
    pallas_call x5 -> x6, Pallas kernels: 9.13 us -> 8.09 us  [call(): pl.pallas_call(kernel, name=name, out_shape=outs, in_specs=[SMEM] * len(s...]
where the time goes in v4:
time: 34.1 us; the launch traced here: 33.9 us
  waiting for transfers between devices  15 us (44%)
  starting transfers between devices  9.83 us (29%)
  Pallas kernels  8.09 us (24%)
  between operations  0.79 us (2%)
    ppermute x8, waiting for transfers between devices, swapped(): return lax.ppermute(value, axis, [(i, i ^ bit) for i in range(size)])  15 us
    ppermute x8, starting transfers between devices, swapped(): return lax.ppermute(value, axis, [(i, i ^ bit) for i in range(size)])  9.83 us
    pallas_call x6, Pallas kernels, call(): pl.pallas_call(kernel, name=name, out_shape=outs, in_specs=[SMEM] * len(s...  8.09 us
  transfers between devices with their start and end apart: 8, of which 7 were waited for; matrix products, arithmetic and copies ran while one was open for 0% of the time, Pallas kernels for 5%

profile of v4, /device:TPU:0, one launch (start us, length us, event | category | flops | bytes accessed | tf_op | source)
XLA Modules:
  0.0 33.9 jit_solution(8821435572184009745)
XLA Ops:
  0.7 2.8 %source_sums.1 = (f32[20,8,128]{2,1,0:T(8,128)S(1)}, f32[64,128]{1,0:T(8,128)S(1)}) custom-call(s32[1,1,16]{2,1,0:T(1,128)} %counts_hbm.1, f32[5,8192]{1,0:T(8,128)} %design_ref.1, f32[64,128]{1,0:T(8,128)} %bitcast.28, f32[64,128]{1,0:T(8,128)} %bitcast.24, s32[64,128]{1,0:T(8,128)} %bitcast.30), custom_call_target="tpu_custom_call" | custom-call | tf_op jit(solution)/shard_map/source_sums/pallas_call | solution.py:519
  3.5 0.0 copy-start.1
  3.5 0.6 %collective-permute-start = (f32[20,8,128]{2,1,0:T(8,128)S(1)}, f32[20,8,128]{2,1,0:T(8,128)S(1)}, u32[]{:S(2)}, u32[]{:S(2)}) collective-permute-start(f32[20,8,128]{2,1,0:T(8,128)S(1)} %get-tuple-element.10.mine_ref), channel_id=1, source_target_pairs={{0,1},{1,0},{2,3},{3,2},{4,5},{5,4},{6,7},{7,6},{8,9},{9,8},{10,11... | collective-permute-start | bytes 245768 | tf_op jit(solution)/shard_map/ppermute | solution.py:532
  4.1 0.0 copy-start.5
  4.1 1.5 %band_sums.1.band_ref = f32[24,16,128]{2,1,0:T(8,128)S(1)} custom-call(f32[64,128]{1,0:T(8,128)S(1)} %get-tuple-element.11.live_ref, f32[64,128]{1,0:T(8,128)S(1)} %bitcast.18, f32[3,8192]{1,0:T(4,128)S(1)} %copy-done, f32[64,128]{1,0:T(8,128)S(1)} %bitcast.25, s32[64,128]{1,0:T(8,128)S(1)} %bitcast.21), custom_call_target="tpu_custom_call" | custom-call | tf_op jit(solution)/shard_map/band_sums/pallas_call | solution.py:519
  5.6 1.9 %residuals.1 = (f32[5,1024]{1,0:T(8,128)}, f32[64,128]{1,0:T(8,128)S(1)}, f32[4,112,128]{2,1,0:T(8,128)S(1)}) custom-call(f32[20,8,128]{2,1,0:T(8,128)S(1)} %get-tuple-element.10.mine_ref, f32[20,8,128]{2,1,0:T(8,128)S(1)} %collective-permute-done.other_ref, f32[24,16,128]{2,1,0:T(8,128)S(1)} %band_sums.1.band_ref, ...), custom_call_target="tpu_custom_call" | custom-call | tf_op jit(solution)/shard_map/residuals/pallas_call | solution.py:519
  7.6 0.1 collective-permute-start.1
  7.7 1.3 %collective-permute-done.1 = f32[2,112,128]{2,1,0:T(8,128)S(1)} collective-permute-done((f32[2,112,128]{2,1,0:T(8,128)S(1)}, f32[2,112,128]{2,1,0:T(8,128)S(1)}, u32[]{:S(2)}, u32[]{:S(2)}) %collective-permute-start.1) | collective-permute-done | bytes 114720 | tf_op jit(solution)/shard_map/ppermute | solution.py:532
  9.0 2.6 %collective-permute-start.2 = (f32[1,112,128]{2,1,0:T(8,128)S(1)}, f32[1,112,128]{2,1,0:T(8,128)S(1)}, u32[]{:S(2)}, u32[]{:S(2)}) collective-permute-start(f32[1,112,128]{2,1,0:T(8,128)S(1)} %constant_dynamic-slice_fusion), channel_id=1, source_target_pairs={{0,3},{1,2},{2,1},{3,0},{4,7},{5,6},{6,5},{7,4},{8,11},{9,10},{10,... | collective-permute-start | bytes 172040 | tf_op jit(solution)/shard_map/ppermute | solution.py:532
  11.7 2.1 %collective-permute-done.2 = f32[1,112,128]{2,1,0:T(8,128)S(1)} collective-permute-done((f32[1,112,128]{2,1,0:T(8,128)S(1)}, f32[1,112,128]{2,1,0:T(8,128)S(1)}, u32[]{:S(2)}, u32[]{:S(2)}) %collective-permute-start.2) | collective-permute-done | bytes 57376 | tf_op jit(solution)/shard_map/ppermute | solution.py:532
  13.8 1.6 %collective-permute-start.3 = (f32[112,128]{1,0:T(8,128)S(1)}, f32[112,128]{1,0:T(8,128)S(1)}, u32[]{:S(2)}, u32[]{:S(2)}) collective-permute-start(f32[112,128]{1,0:T(8,128)S(1)} %add_bitcast_fusion), channel_id=1, source_target_pairs={{0,5},{1,4},{2,7},{3,6},{4,1},{5,0},{6,3},{7,2},{8,13},{9,12},{10,... | collective-permute-start | bytes 172040 | tf_op jit(solution)/shard_map/ppermute | solution.py:532
  15.5 2.3 %collective-permute-done.3 = f32[112,128]{1,0:T(8,128)S(1)} collective-permute-done((f32[112,128]{1,0:T(8,128)S(1)}, f32[112,128]{1,0:T(8,128)S(1)}, u32[]{:S(2)}, u32[]{:S(2)}) %collective-permute-start.3) | collective-permute-done | bytes 57376 | tf_op jit(solution)/shard_map/ppermute | solution.py:532
  17.8 1.5 %collective-permute-start.4 = (f32[112,128]{1,0:T(8,128)S(1)}, f32[112,128]{1,0:T(8,128)S(1)}, u32[]{:S(2)}, u32[]{:S(2)}) collective-permute-start(f32[112,128]{1,0:T(8,128)S(1)} %add.41), channel_id=1, source_target_pairs={{0,9},{1,8},{2,11},{3,10},{4,13},{5,12},{6,15},{7,14},{8,1},{9,0},... | collective-permute-start | bytes 172040 | tf_op jit(solution)/shard_map/ppermute | solution.py:532
  19.3 2.5 %collective-permute-done.4 = f32[112,128]{1,0:T(8,128)S(1)} collective-permute-done((f32[112,128]{1,0:T(8,128)S(1)}, f32[112,128]{1,0:T(8,128)S(1)}, u32[]{:S(2)}, u32[]{:S(2)}) %collective-permute-start.4) | collective-permute-done | bytes 57376 | tf_op jit(solution)/shard_map/ppermute | solution.py:532
  21.7 2.3 %collective-permute-start.5 = (f32[112,128]{1,0:T(8,128)S(1)}, f32[112,128]{1,0:T(8,128)S(1)}, u32[]{:S(2)}, u32[]{:S(2)}) collective-permute-start(f32[112,128]{1,0:T(8,128)S(1)} %add.42), channel_id=1, source_target_pairs={{0,17},{1,16},{2,19},{3,18},{4,21},{5,20},{6,23},{7,22},{8,25},{9,... | collective-permute-start | bytes 172040 | tf_op jit(solution)/shard_map/ppermute | solution.py:532
  24.0 0.1 pad_add_fusion.place_ref
  24.1 3.7 %collective-permute-done.5 = f32[112,128]{1,0:T(8,128)S(1)} collective-permute-done((f32[112,128]{1,0:T(8,128)S(1)}, f32[112,128]{1,0:T(8,128)S(1)}, u32[]{:S(2)}, u32[]{:S(2)}) %collective-permute-start.5) | collective-permute-done | bytes 57376 | tf_op jit(solution)/shard_map/ppermute | solution.py:532
  27.8 0.8 %attitude.1 = f32[16,128]{1,0:T(8,128)S(1)} custom-call(s32[2]{0:T(128)S(1)} %pad_add_fusion.place_ref, f32[112,128]{1,0:T(8,128)S(1)} %add.43.sums_ref), custom_call_target="tpu_custom_call" | custom-call | tf_op jit(solution)/shard_map/attitude/pallas_call | solution.py:519
  28.6 1.0 %collective-permute-start.6 = (f32[16,128]{1,0:T(8,128)S(1)}, f32[16,128]{1,0:T(8,128)S(1)}, u32[]{:S(2)}, u32[]{:S(2)}) collective-permute-start(f32[16,128]{1,0:T(8,128)S(1)} %attitude.1), channel_id=1, source_target_pairs={{0,3},{1,2},{2,1},{3,0},{4,7},{5,6},{6,5},{7,4},{8,11},{9,10},{10,... | collective-permute-start | bytes 24584 | tf_op jit(solution)/shard_map/ppermute | solution.py:532
  29.6 2.2 %collective-permute-done.6 = f32[16,128]{1,0:T(8,128)S(1)} collective-permute-done((f32[16,128]{1,0:T(8,128)S(1)}, f32[16,128]{1,0:T(8,128)S(1)}, u32[]{:S(2)}, u32[]{:S(2)}) %collective-permute-start.6) | collective-permute-done | bytes 8224 | tf_op jit(solution)/shard_map/ppermute | solution.py:532
  31.8 0.2 collective-permute-start.7
  31.9 0.1 prepare.1.factor_ref
  32.1 0.9 %collective-permute-done.7 = f32[32,128]{1,0:T(8,128)S(1)} collective-permute-done((f32[32,128]{1,0:T(8,128)S(1)}, f32[32,128]{1,0:T(8,128)S(1)}, u32[]{:S(2)}, u32[]{:S(2)}) %collective-permute-start.7) | collective-permute-done | bytes 16416 | tf_op jit(solution)/shard_map/ppermute | solution.py:532
  33.0 0.9 %predict.1 = (f32[3,128]{1,0:T(4,128)}, f32[64,128]{1,0:T(8,128)}) custom-call(s32[1]{0:T(128)} %bitcast.5.place_ref, f32[16,4,128]{2,1,0:T(4,128)S(1)} %bitcast.27, f32[12,64,128]{2,1,0:T(8,128)S(1)} %prepare.1.factor_ref, f32[64,128]{1,0:T(8,128)S(1)} %get-tuple-element.14.resid_ref, s32[64,128]{1,0:T(8,128)S(1)} %bitcast.23), custom_call_target="tpu_custom_call" | custom-call | tf_op jit(solution)/shard_map/predict/pallas_call | solution.py:519
  (24 shorter events, 0.1 us)
Async XLA Ops:
  0.6 3.4 %copy-start = (f32[3,8192]{1,0:T(4,128)S(1)}, f32[3,8192]{1,0:T(4,128)}, u32[]{:S(2)}) copy-start(f32[3,8192]{1,0:T(4,128)} %axis_ref.5) | copy-start | bytes 294916
  0.6 3.4 %copy-start.2 = (f32[8192]{0:T(1024)S(1)}, f32[8192]{0:T(1024)}, u32[]{:S(2)}) copy-start(f32[8192]{0:T(1024)} %param.11) | copy-start | bytes 98308
  0.7 3.4 %copy-start.3 = (s32[8192]{0:T(1024)S(1)}, s32[8192]{0:T(1024)}, u32[]{:S(2)}) copy-start(s32[8192]{0:T(1024)} %param.14) | copy-start | bytes 98308
  0.7 3.4 %copy-start.4 = (f32[8192]{0:T(1024)S(1)}, f32[8192]{0:T(1024)}, u32[]{:S(2)}) copy-start(f32[8192]{0:T(1024)} %param.10) | copy-start | bytes 98308
  3.5 2.1 %copy-start.1 = (f32[5,8192]{1,0:T(8,128)S(1)}, f32[5,8192]{1,0:T(8,128)}, u32[]{:S(2)}) copy-start(f32[5,8192]{1,0:T(8,128)} %design_ref.1) | copy-start | bytes 491524
  3.5 2.1 %collective-permute-start = (f32[20,8,128]{2,1,0:T(8,128)S(1)}, f32[20,8,128]{2,1,0:T(8,128)S(1)}, u32[]{:S(2)}, u32[]{:S(2)}) collective-permute-start(f32[20,8,128]{2,1,0:T(8,128)S(1)} %get-tuple-element.10.mine_ref), channel_id=1, source_target_pairs={{0,1},{1,0},{2,3},{3,2},{4,5},{5,4},{6,7},{7,6},{8,9},{9,8},{10,11... | collective-permute-start | bytes 245768 | tf_op jit(solution)/shard_map/ppermute | solution.py:532
  4.1 1.5 %copy-start.5 = (f32[8192]{0:T(1024)S(1)}, f32[8192]{0:T(1024)}, u32[]{:S(2)}) copy-start(f32[8192]{0:T(1024)} %param.9) | copy-start | bytes 98308
  4.1 1.5 %copy-start.6 = (s32[8192]{0:T(1024)S(1)}, s32[8192]{0:T(1024)}, u32[]{:S(2)}) copy-start(s32[8192]{0:T(1024)} %param.13) | copy-start | bytes 98308
  7.6 1.4 %collective-permute-start.1 = (f32[2,112,128]{2,1,0:T(8,128)S(1)}, f32[2,112,128]{2,1,0:T(8,128)S(1)}, u32[]{:S(2)}, u32[]{:S(2)}) collective-permute-start(f32[2,112,128]{2,1,0:T(8,128)S(1)} %dynamic-slice_bitcast_fusion), channel_id=1, source_target_pairs={{0,1},{1,0},{2,3},{3,2},{4,5},{5,4},{6,7},{7,6},{8,9},{9,8},{10,11... | collective-permute-start | bytes 344072 | tf_op jit(solution)/shard_map/ppermute | solution.py:532
  9.0 4.8 %collective-permute-start.2 = (f32[1,112,128]{2,1,0:T(8,128)S(1)}, f32[1,112,128]{2,1,0:T(8,128)S(1)}, u32[]{:S(2)}, u32[]{:S(2)}) collective-permute-start(f32[1,112,128]{2,1,0:T(8,128)S(1)} %constant_dynamic-slice_fusion), channel_id=1, source_target_pairs={{0,3},{1,2},{2,1},{3,0},{4,7},{5,6},{6,5},{7,4},{8,11},{9,10},{10,... | collective-permute-start | bytes 172040 | tf_op jit(solution)/shard_map/ppermute | solution.py:532
  13.8 3.9 %collective-permute-start.3 = (f32[112,128]{1,0:T(8,128)S(1)}, f32[112,128]{1,0:T(8,128)S(1)}, u32[]{:S(2)}, u32[]{:S(2)}) collective-permute-start(f32[112,128]{1,0:T(8,128)S(1)} %add_bitcast_fusion), channel_id=1, source_target_pairs={{0,5},{1,4},{2,7},{3,6},{4,1},{5,0},{6,3},{7,2},{8,13},{9,12},{10,... | collective-permute-start | bytes 172040 | tf_op jit(solution)/shard_map/ppermute | solution.py:532
  17.8 3.9 %collective-permute-start.4 = (f32[112,128]{1,0:T(8,128)S(1)}, f32[112,128]{1,0:T(8,128)S(1)}, u32[]{:S(2)}, u32[]{:S(2)}) collective-permute-start(f32[112,128]{1,0:T(8,128)S(1)} %add.41), channel_id=1, source_target_pairs={{0,9},{1,8},{2,11},{3,10},{4,13},{5,12},{6,15},{7,14},{8,1},{9,0},... | collective-permute-start | bytes 172040 | tf_op jit(solution)/shard_map/ppermute | solution.py:532
  21.7 6.1 %collective-permute-start.5 = (f32[112,128]{1,0:T(8,128)S(1)}, f32[112,128]{1,0:T(8,128)S(1)}, u32[]{:S(2)}, u32[]{:S(2)}) collective-permute-start(f32[112,128]{1,0:T(8,128)S(1)} %add.42), channel_id=1, source_target_pairs={{0,17},{1,16},{2,19},{3,18},{4,21},{5,20},{6,23},{7,22},{8,25},{9,... | collective-permute-start | bytes 172040 | tf_op jit(solution)/shard_map/ppermute | solution.py:532
  28.6 3.1 %collective-permute-start.6 = (f32[16,128]{1,0:T(8,128)S(1)}, f32[16,128]{1,0:T(8,128)S(1)}, u32[]{:S(2)}, u32[]{:S(2)}) collective-permute-start(f32[16,128]{1,0:T(8,128)S(1)} %attitude.1), channel_id=1, source_target_pairs={{0,3},{1,2},{2,1},{3,0},{4,7},{5,6},{6,5},{7,4},{8,11},{9,10},{10,... | collective-permute-start | bytes 24584 | tf_op jit(solution)/shard_map/ppermute | solution.py:532
  31.8 1.2 %collective-permute-start.7 = (f32[32,128]{1,0:T(8,128)S(1)}, f32[32,128]{1,0:T(8,128)S(1)}, u32[]{:S(2)}, u32[]{:S(2)}) collective-permute-start(f32[32,128]{1,0:T(8,128)S(1)} %pad_maximum_fusion.1), channel_id=1, source_target_pairs={{0,1},{1,0},{2,3},{3,2},{4,5},{5,4},{6,7},{7,6},{8,9},{9,8},{10,11... | collective-permute-start | bytes 49160 | tf_op jit(solution)/shard_map/ppermute | solution.py:532

commit v5 on v4

--- a/solution.py
+++ b/solution.py
@@ -15,7 +15,7 @@
 LOW = 256
 QUANTITIES = 3 + 4 * 6
 REACH = 3 * (ITERS - 1)
-PER_ROW = LANES // (2 * REACH)
+WINDOW = 2 * REACH
 CUBICS = [(1.0, 0.0, 0.0, 0.0), (4.0, 12.0, 6.0, 1.0), (1.0, 6.0, 12.0, 4.0), (0.0, 0.0, 0.0, 1.0)]
 SIGNALS = 15 + 5
 PAIRS = [(x, y) for x in range(3) for y in range(x, 3)]
@@ -38,6 +38,11 @@
                     coefs[p + q] += CUBICS[i][p] * CUBICS[j][q] / 36.0
             table[i, j] = coefs
     return table
+
+
+def split2(value):
+    high = value.astype(bf16).astype(f32)
+    return [high, value - high]
 
 
 def split3(value):
@@ -125,14 +130,24 @@
 
 def by_tile(wide_ref, tiled_ref):
     rows = wide_ref.shape[0]
-    for t in range(tiled_ref.shape[0]):
-        tiled_ref[t, 0:rows, :] = wide_ref[:, t * LANES : (t + 1) * LANES]
-
-
-def tile_of(wide_ref, t):
-    start = t * LANES if isinstance(t, int) else pl.multiple_of(t * LANES, LANES)
-    block = wide_ref[:, pl.ds(start, LANES)]
-    return jnp.concatenate([block, jnp.zeros((SUB - block.shape[0], LANES), f32)], 0)
+    for t in range(tiled_ref.shape[0] // SUB):
+        tiled_ref[t * SUB : t * SUB + rows, :] = wide_ref[:, t * LANES : (t + 1) * LANES]
+
+
+def by_group(tiles):
+    return range(0, tiles, SUB)
+
+
+def across(start, row):
+    return pl.ds(start * SUB + row, SUB, stride=SUB)
+
+
+def tile_of(tiled_ref, t):
+    return tiled_ref[pl.ds(t * SUB, SUB), :]
+
+
+def low_bits(index, size):
+    return index >> (size.bit_length() - 1), index & (size - 1)
 
 
 def row_of(ref, t):
@@ -157,20 +172,18 @@
     return [per_sublane(values[i : i + SUB], jnp.int32) for i in range(0, len(values), SUB)]
 
 
-def stacked_parts(values):
-    value = jnp.concatenate(values, 0)
-    rows = 3 * value.shape[0]
-    parts = split3(value)
-    if rows % (2 * SUB):
+def stacked_parts(values, split):
+    parts = split(jnp.concatenate(values, 0))
+    if len(parts) * parts[0].shape[0] % (2 * SUB):
         parts.append(jnp.zeros((SUB, LANES), f32))
     return jnp.concatenate(parts, 0).astype(bf16)
 
 
-def sum_parts(value, rows):
-    return value[0:rows] + value[rows : 2 * rows] + value[2 * rows : 3 * rows]
-
-
-def add_blocks(moments_ref, start, steps, rep, rows, left_of, knot_ref):
+def sum_parts(value, rows, count):
+    return sum(value[i * rows : (i + 1) * rows] for i in range(count))
+
+
+def add_blocks(moments_ref, start, steps, rep, rows, count, left_of, knot_ref):
     per_block = min(rep, steps)
     for b in range(steps // per_block):
         lefts, rights = [], []
@@ -178,12 +191,13 @@
             lefts.append(left_of(start + i))
             rights.append(onehot(knot_ref[pl.ds(start + i, 1), :].astype(f32), KNOT_DEV))
         got = contract(jnp.concatenate(lefts, 1), jnp.concatenate(rights, 1))
-        summed = sum_parts(got, rows)[:, None, :]
-        where_to = pl.ds((start + b * per_block) // rep, 1)
+        summed = sum_parts(got, rows, count)
+        where_to = (start + b * per_block) // rep
+        where_to = pl.ds(where_to * rows, rows)
         if rep <= steps:
-            moments_ref[:, where_to, :] = summed
+            moments_ref[where_to, :] = summed
         else:
-            moments_ref[:, where_to, :] += summed
+            moments_ref[where_to, :] += summed
 
 
 def contract(left, right):
@@ -206,7 +220,7 @@
 
 def source_kernel(
     counts_hbm, design_hbm, obs_hbm, weight_hbm, index_hbm, out_ref, live_ref,
-    counts_ref, design_ref, obs_ref, weight_ref, index_ref, sems, low_ref, high_ref, total,
+    counts_ref, design_ref, obs_ref, weight_ref, index_ref, sems, low_ref, high_ref, total, tiled,
 ):
     tiles = obs_ref.shape[0]
     shards = counts_ref.shape[2]
@@ -228,27 +242,29 @@
     lefts_of = patterns([m for m, _ in pairs])
     rights_of = patterns([n for _, n in pairs])
     first_half = iota((SUB, LANES), 0) < SUB // 2
-    is_observed = iota((SUB, LANES), 0) == 5
     copies[0].wait()
     slots = iota((rep, LANES), 0) * LANES + iota((rep, LANES), 1)
     for d in range(shards):
         live_ref[pl.ds(d * rep, rep), :] = (slots < counts_ref[0, 0, d]).astype(f32)
     copies[1].wait()
     copies[2].wait()
-    for g in range(tiles // SUB):
-        at = pl.ds(g * SUB, SUB)
+    for start in by_group(tiles):
+        at = pl.ds(start, SUB)
         weight_ref[at, :] = weight_ref[at, :] * live_ref[at, :]
-        high = index_ref[at, :] // LOW
+        high, low = low_bits(index_ref[at, :], LOW)
         high_ref[at, :] = high.astype(f32)
-        low_ref[at, :] = (index_ref[at, :] - high * LOW).astype(f32)
+        low_ref[at, :] = low.astype(f32)
     copies[3].wait()
     copies[4].wait()
+    by_tile(design_ref, tiled)
+    for start in by_group(tiles):
+        tiled[across(start, 5), :] = obs_ref[pl.ds(start, SUB), :]
 
     def group(start, steps):
         lefts, rights = [], []
         for i in range(steps):
             t = start + i
-            values = jnp.where(is_observed, row_of(obs_ref, t), tile_of(design_ref, t))
+            values = tile_of(tiled, t)
             scaled = values * row_of(weight_ref, t)
             products = [pick_rows(scaled, m) * pick_rows(values, n) for m, n in zip(lefts_of, rights_of)]
             high, middle, low = split3(products[2])
@@ -271,7 +287,7 @@
     for h in range(highs):
         block = total[h * height : (h + 1) * height, :]
         tail = block[3 * wide :]
-        summed = sum_parts(block, wide)
+        summed = sum_parts(block, wide, 3)
         rest = tail[0:half_tile] + tail[half_tile : 2 * half_tile] + tail[2 * half_tile : 3 * half_tile]
         for half in range(LOW // LANES):
             cols = slice(half * LANES, (half + 1) * LANES)
@@ -279,39 +295,41 @@
             out_ref[wide:SIGNALS, h * (LOW // LANES) + half, :] = rest[:, cols]
 
 
-def band_kernel(live_ref, phase_ref, axis_ref, weight_ref, knot_ref, out_ref, scaled_ref, moments):
-    tiles, shards = phase_ref.shape[0], moments.shape[1]
+def band_kernel(live_ref, phase_ref, axis_ref, weight_ref, knot_ref, out_ref, tiled, powers_ref, moments):
+    tiles, shards = phase_ref.shape[0], out_ref.shape[0] // 24
     rep = tiles // shards
-    scaled_ref[...] = weight_ref[...] * live_ref[...]
-    rows = moments.shape[0]
-    power = iota((SUB, LANES), 0)
-    other = jnp.maximum(6 - power, 0)
+    by_tile(axis_ref, tiled)
+    rows = moments.shape[0] // shards
     lefts_of = patterns([PAIRS[q % 6][0] for q in range(24)])
     rights_of = patterns([PAIRS[q % 6][1] for q in range(24)])
-    powers_of = patterns([q // 6 for q in range(rows)])
+    powers_of = patterns([q // 6 if q < 42 else 0 for q in range(rows)])
+    for start in by_group(tiles):
+        at = pl.ds(start, SUB)
+        u = phase_ref[at, :]
+        r = 1.0 - u
+        u2, r2 = u * u, r * r
+        u3, r3 = u2 * u, r2 * r
+        w = weight_ref[at, :] * live_ref[at, :]
+        u3w, r3w = u3 * w, r3 * w
+        powers = [r3w * r3, r3w * (r2 * u), r3w * (r * u2), r3w * u3, u3w * (r2 * u), u3w * (r * u2), u3w * u3]
+        for p in range(7):
+            powers_ref[across(start, p), :] = powers[p]
 
     def left_of(t):
-        u = row_of(phase_ref, t)
-        r = 1.0 - u
-        powers = jnp.ones((SUB, LANES), f32)
-        for base, exponent in ((u, power), (r, other)):
-            squared = base * base
-            for bit, factor in ((1, base), (2, squared), (4, squared * squared)):
-                powers = powers * jnp.where((exponent & bit) != 0, factor, 1.0)
-        axes = tile_of(axis_ref, t)
-        scaled = axes * row_of(scaled_ref, t)
-        products = [pick_rows(scaled, x) * pick_rows(axes, y) for x, y in zip(lefts_of, rights_of)]
-        return stacked_parts([products[i % 3] * pick_rows(powers, p) for i, p in enumerate(powers_of)])
+        axes = tile_of(tiled, t)
+        powers = tile_of(powers_ref, t)
+        products = [pick_rows(axes, x) * pick_rows(axes, y) for x, y in zip(lefts_of, rights_of)]
+        return stacked_parts([products[i % 3] * pick_rows(powers, p) for i, p in enumerate(powers_of)], split2)
 
     def group(start, steps):
-        add_blocks(moments, start, steps, rep, rows, left_of, knot_ref)
+        add_blocks(moments, start, steps, rep, rows, 2, left_of, knot_ref)
 
     if rep > math.gcd(tiles, 64):
         moments[...] = jnp.zeros_like(moments)
     over_steps(tiles, group)
     table = bernstein_products()
     for n in range(6):
-        parts = [moments[p * 6 + n] for p in range(7)]
+        parts = [moments[pl.ds(p * 6 + n, shards, stride=rows), :] for p in range(7)]
 
         def product(i, j):
             return sum(c * part for c, part in zip(table[i, j], parts) if c)
@@ -320,104 +338,100 @@
             running = product(3 - delta, 3)
             for j in reversed(range(3 - delta)):
                 running = product(j, j + delta) + shift_up(running, 1)
-            out_ref[delta * 6 + n] = running
+            to = (delta * 6 + n) * shards
+            out_ref[to : to + shards, :] = running
 
 
 def halo_rows():
-    return -(-QUANTITIES // PER_ROW)
-
-
-def pack(source_ref, index, q, message_ref, packed):
-    parts = message_ref.shape[0]
-    owned = source_ref.shape[1] // parts
-    for p in range(parts):
-        message_ref[p, q * owned : (q + 1) * owned, :] = source_ref[index, p * owned : (p + 1) * owned, :]
-    if parts == 1:
-        return packed
-    row, lane = iota((SUB, LANES), 0), iota((SUB, LANES), 1)
-    blank = jnp.zeros((SUB - parts + 1, LANES), f32)
-    after = jnp.concatenate([source_ref[index, pl.ds(owned, parts - 1, stride=owned), :], blank], 0)
-    before = jnp.concatenate([source_ref[index, pl.ds(owned - 1, parts - 1, stride=owned), :], blank], 0)
-    before = pltpu.roll(before, 1, 0)
-    edge = jnp.where(lane < LANES // 2, after, jnp.where(row == 0, 0.0, before))
-    place, slot = q // PER_ROW, q % PER_ROW
-    width = 2 * REACH
-    edge = pltpu.roll(edge, (REACH + width * slot) % LANES, 1)
-    mine = (lane >= width * slot) & (lane < width * (slot + 1))
-    return [jnp.where(mine, edge, row_) if i == place else row_ for i, row_ in enumerate(packed)]
+    return 1 + (QUANTITIES - 3) // SUB
+
+
+def slots_of(value, shift):
+    return pltpu.roll(value, shift, 1, stride=WINDOW, stride_axis=0)
+
+
+def pack(source_ref, first, count, row, message_ref):
+    parts, shards = message_ref.shape[0], source_ref.shape[0] // count
+    owned = shards // parts
+    lane, slot = iota((SUB, LANES), 1), iota((SUB, LANES), 0)
+    mine = (lane >= WINDOW * slot) & (lane < WINDOW * (slot + 1)) & (slot < count)
+    zero = jnp.zeros((SUB, LANES), f32)
+    for base in range(0, count, SUB):
+        for q in range(base, min(base + SUB, count)):
+            for p in range(parts):
+                at = q * shards + p * owned
+                to = (first + q) * owned
+                message_ref[p, to : to + owned, :] = source_ref[at : at + owned, :]
+        for p in range(parts):
+            taken = min(count, SUB)
+
+            def edge(r):
+                got = source_ref[pl.ds(base * shards + r, taken, stride=shards), :]
+                return got if taken == SUB else jnp.concatenate([got, zero[taken:]], 0)
+
+            after = edge((p + 1) * owned) if p < parts - 1 else zero
+            before = edge(p * owned - 1) if p else zero
+            packed = slots_of(jnp.where(lane < LANES // 2, after, before), REACH)
+            to = QUANTITIES * owned + row + base // SUB
+            message_ref[p, to : to + 1, :] = jnp.sum(jnp.where(mine, packed, 0.0), 0, keepdims=True)
 
 
 def resid_kernel(
     mine_ref, other_ref, band_ref, live_ref, design_ref, obs_ref, weight_ref, index_ref, phase_ref, axis_ref, knot_ref,
-    params_ref, resid_ref, message_ref, tiled, scaled_ref, moments, solved_ref, rhs_ref,
+    params_ref, resid_ref, message_ref, tiled, tiled_axis, splines_ref, moments, solved_ref, rhs_ref,
 ):
-    tiles, shards = obs_ref.shape[0], moments.shape[1]
+    tiles, shards = obs_ref.shape[0], rhs_ref.shape[0] // 3
     rep = tiles // shards
     by_tile(design_ref, tiled)
+    by_tile(axis_ref, tiled_axis)
     solved = solve_small([mine_ref[q] + other_ref[q] for q in range(SIGNALS)])
     blocks = SRC_DEV // LANES
     for m in range(5):
         solved_ref[m] = solved[m]
         for b in range(blocks):
             params_ref[m : m + 1, b * LANES : (b + 1) * LANES] = solved[m][b : b + 1, :]
-    rows = moments.shape[0]
+    rows = moments.shape[0] // shards
     axes_of = patterns([q % 3 for q in range(rows)])
-    weights_of = [
-        [per_sublane([CUBICS[min(q // 3, 3)][c] / 6.0 for q in range(i, i + SUB)], f32) for c in range(4)]
-        for i in range(0, rows, SUB)
-    ]
+    splines_of = patterns([min(q // 3, 3) for q in range(rows)])
 
     def left_of(t):
-        u = row_of(phase_ref, t)
-        r = 1.0 - u
-        u2, r2 = u * u, r * r
-        cubes = [r2 * r, r2 * u, r * u2, u2 * u]
-        axes = tile_of(axis_ref, t)
-        scaled = axes * row_of(scaled_ref, t)
-        return stacked_parts(
-            [pick_rows(scaled, x) * sum(c * m for c, m in zip(w, cubes)) for x, w in zip(axes_of, weights_of)]
-        )
+        axes = tile_of(tiled_axis, t)
+        splines = tile_of(splines_ref, t)
+        return stacked_parts([pick_rows(axes, x) * pick_rows(splines, j) for x, j in zip(axes_of, splines_of)], split3)
 
     def group(start, steps):
         for part in range(steps // SUB):
             at = pl.ds(start + part * SUB, SUB)
             live = live_ref[at, :]
-            index = index_ref[at, :]
-            block_of = index // LANES
-            lane_of = index - block_of * LANES
+            block_of, lane_of = low_bits(index_ref[at, :], LANES)
             hits = [block_of == b for b in range(blocks)]
-            fitted = jnp.zeros((SUB, LANES), f32)
+            left = obs_ref[at, :]
             for m in range(5):
-                picked = jnp.zeros((SUB, LANES), f32)
                 for b in range(blocks):
                     table = jnp.broadcast_to(solved_ref[m, b : b + 1, :], (SUB, LANES))
-                    picked = jnp.where(hits[b], jnp.take_along_axis(table, lane_of, axis=1), picked)
-                fitted = fitted + tiled[at, m, :] * picked
-            resid = live * (obs_ref[at, :] - fitted)
+                    found = jnp.take_along_axis(table, lane_of, axis=1)
+                    picked = jnp.where(hits[b], found, picked) if b else found
+                left = left - tiled[across(start + part * SUB, m), :] * picked
+            resid = live * left
             resid_ref[at, :] = resid
-            scaled_ref[at, :] = weight_ref[at, :] * live * resid
-        add_blocks(moments, start, steps, rep, rows, left_of, knot_ref)
+            scaled = weight_ref[at, :] * resid
+            for j, basis in enumerate(spline_basis(phase_ref[at, :])):
+                splines_ref[across(start + part * SUB, j), :] = basis * scaled
+        add_blocks(moments, start, steps, rep, rows, 3, left_of, knot_ref)
 
     if rep > math.gcd(tiles, 64):
         moments[...] = jnp.zeros_like(moments)
     over_steps(tiles, group)
-    parts = message_ref.shape[0]
-    packed = [jnp.zeros((SUB, LANES), f32)] * halo_rows()
     for x in range(3):
-        running = moments[9 + x]
+        running = moments[pl.ds(9 + x, shards, stride=rows), :]
         for j in reversed(range(3)):
-            running = moments[j * 3 + x] + shift_up(running, 1)
-        rhs_ref[x] = running
-        packed = pack(rhs_ref, x, x, message_ref, packed)
-    for q in range(band_ref.shape[0]):
-        packed = pack(band_ref, q, 3 + q, message_ref, packed)
-    first = QUANTITIES * (shards // parts)
-    for p in range(parts):
-        for i, row in enumerate(packed):
-            message_ref[p, first + i : first + i + 1, :] = row[p : p + 1]
-
-
-def solve_kernel(place_ref, sums_ref, out_ref):
+            running = moments[pl.ds(j * 3 + x, shards, stride=rows), :] + shift_up(running, 1)
+        rhs_ref[x * shards : (x + 1) * shards, :] = running
+    pack(rhs_ref, 0, 3, 0, message_ref)
+    pack(band_ref, 3, QUANTITIES - 3, 1, message_ref)
+
+
+def solve_kernel(place_ref, sums_ref, out_ref, edges_ref):
     owned = out_ref.shape[0] // 4
     ring = -(-(owned + 2) // SUB) * SUB
     order = {pair: n for n, pair in enumerate(PAIRS)}
@@ -428,11 +442,16 @@
     edge = (place_ref[0] == place_ref[1] - 1).astype(jnp.int32)
     known = jnp.where(after & (jnp.full((ring, LANES), edge, jnp.int32) == 1), 0.0, 1.0)
 
+    back = LANES - REACH - WINDOW * (SUB - 1)
+    for i in range(halo_rows()):
+        packed = sums_ref[QUANTITIES * owned + i : QUANTITIES * owned + i + 1, :]
+        edges_ref[i * SUB : (i + 1) * SUB, :] = slots_of(jnp.broadcast_to(packed, (SUB, LANES)), back)
+
     def load(q):
         rows = sums_ref[q * owned : (q + 1) * owned, :]
-        rest = sums_ref[pl.ds(QUANTITIES * owned + q // PER_ROW, 1), :]
-        rest = jnp.broadcast_to(rest, (ring - owned, LANES))
-        rest = pltpu.roll(rest, (-(REACH + 2 * REACH * (q % PER_ROW))) % LANES, 1)
+        place = q if q < 3 else q + SUB - 3
+        slot = place // SUB * SUB + SUB - 1 - place % SUB
+        rest = jnp.broadcast_to(edges_ref[slot : slot + 1, :], (ring - owned, LANES))
         return jnp.where(inside | after | before, jnp.concatenate([rows, rest], 0), 0.0)
 
     def turn(value, n):
@@ -475,7 +494,7 @@
             at = pl.ds(start + part * SUB, SUB)
             basis = [b * live_ref[at, :] for b in spline_basis(phase_ref[at, :])]
             for x in range(3):
-                along = tiled[at, x, :]
+                along = tiled[across(start + part * SUB, x), :]
                 for j in range(4):
                     out_ref[x * 4 + j, at, :] = along * basis[j]
 
@@ -564,7 +583,7 @@
     obs, w, phase, index, knots = (
         a.reshape(tiles, LANES) for a in (observed, weight, phase_frac, source_index, knot_index)
     )
-    tiled = pltpu.VMEM((tiles, SUB, LANES), f32)
+    tiled = pltpu.VMEM((tiles * SUB, LANES), f32)
     dense = pltpu.VMEM((tiles, LANES), f32)
     blocks = SRC_DEV // LANES
     moments, live = call(
@@ -574,14 +593,14 @@
         [
             pltpu.SMEM(counts.shape, jnp.int32), pltpu.VMEM(design.shape, f32), dense, dense,
             pltpu.VMEM((tiles, LANES), jnp.int32), pltpu.SemaphoreType.DMA((5,)), dense, dense,
-            pltpu.VMEM((SRC_DEV // LOW * 64, LOW), f32),
+            pltpu.VMEM((SRC_DEV // LOW * 64, LOW), f32), tiled,
         ],
         HBM,
     )
     band = call(
         band_kernel, "band_sums", [], [live, phase, axis_factors, w, knots],
-        jax.ShapeDtypeStruct((24, shards, KNOT_DEV), f32),
-        [dense, pltpu.VMEM((48, shards, KNOT_DEV), f32)],
+        jax.ShapeDtypeStruct((24 * shards, KNOT_DEV), f32),
+        [tiled, tiled, pltpu.VMEM((shards * 48, KNOT_DEV), f32)],
     )
     if lax.axis_size("ccd") == 2:
         other = swapped(moments, "ccd", 1)
@@ -600,8 +619,8 @@
             jax.ShapeDtypeStruct((tiles, LANES), f32),
             jax.ShapeDtypeStruct((parts, message_rows, LANES), f32),
         ),
-        [tiled, dense, pltpu.VMEM((16, shards, KNOT_DEV), f32), pltpu.VMEM((5, blocks, LANES), f32),
-         pltpu.VMEM((3, shards, KNOT_DEV), f32)],
+        [tiled, tiled, tiled, pltpu.VMEM((shards * 16, KNOT_DEV), f32), pltpu.VMEM((5, blocks, LANES), f32),
+         pltpu.VMEM((3 * shards, KNOT_DEV), f32)],
     )
     factors = call(
         prepare_kernel, "prepare", [], [message, live, phase, axis_factors],
@@ -624,7 +643,7 @@
         part = jnp.zeros_like(place)
     coefs = call(
         solve_kernel, "attitude", [jnp.stack([part, jnp.full_like(part, parts)])], [sums],
-        jax.ShapeDtypeStruct((owned * 4, LANES), f32), [],
+        jax.ShapeDtypeStruct((owned * 4, LANES), f32), [pltpu.VMEM((halo_rows() * SUB, LANES), f32)],
     )
     if fast:
         coefs = doubled(doubled(coefs, 3, lower), 1, upper)

time: 34.1 us -> 33.1 us (0.971)
  Pallas kernels: 8.09 us -> 7.02 us
    pallas_call x6, Pallas kernels: 8.09 us -> 7.02 us  [call(): pl.pallas_call(kernel, name=name, out_shape=outs, in_specs=[SMEM] * len(s...]
  transfers between devices with their start and end apart: 8 -> 8, of which waited for: 7 -> 7; matrix products, arithmetic and copies ran while one was open for 0% -> 0% of each run, Pallas kernels for 5% -> 4%
where the time goes in v5:
time: 33.1 us; the launch traced here: 32.9 us
  waiting for transfers between devices  15 us (45%)
  starting transfers between devices  9.89 us (30%)
  Pallas kernels  7.02 us (21%)
  between operations  0.8 us (2%)
    ppermute x8, waiting for transfers between devices, swapped(): return lax.ppermute(value, axis, [(i, i ^ bit) for i in range(size)])  15 us
    ppermute x8, starting transfers between devices, swapped(): return lax.ppermute(value, axis, [(i, i ^ bit) for i in range(size)])  9.89 us
    pallas_call x6, Pallas kernels, call(): pl.pallas_call(kernel, name=name, out_shape=outs, in_specs=[SMEM] * len(s...  7.02 us
  transfers between devices with their start and end apart: 8, of which 7 were waited for; matrix products, arithmetic and copies ran while one was open for 0% of the time, Pallas kernels for 4%

profile of v5, /device:TPU:0, one launch (start us, length us, event | category | flops | bytes accessed | tf_op | source)
XLA Modules:
  0.0 32.9 jit_solution(11233473117799180870)
XLA Ops:
  0.7 2.8 %source_sums.1 = (f32[20,8,128]{2,1,0:T(8,128)S(1)}, f32[64,128]{1,0:T(8,128)S(1)}) custom-call(s32[1,1,16]{2,1,0:T(1,128)} %counts_hbm.1, f32[5,8192]{1,0:T(8,128)} %design_ref.1, f32[64,128]{1,0:T(8,128)} %bitcast.28, f32[64,128]{1,0:T(8,128)} %bitcast.24, s32[64,128]{1,0:T(8,128)} %bitcast.30), custom_call_target="tpu_custom_call" | custom-call | tf_op jit(solution)/shard_map/source_sums/pallas_call | solution.py:538
  3.5 0.0 copy-start.1
  3.5 0.6 %collective-permute-start = (f32[20,8,128]{2,1,0:T(8,128)S(1)}, f32[20,8,128]{2,1,0:T(8,128)S(1)}, u32[]{:S(2)}, u32[]{:S(2)}) collective-permute-start(f32[20,8,128]{2,1,0:T(8,128)S(1)} %get-tuple-element.10.mine_ref), channel_id=1, source_target_pairs={{0,1},{1,0},{2,3},{3,2},{4,5},{5,4},{6,7},{7,6},{8,9},{9,8},{10,11... | collective-permute-start | bytes 245768 | tf_op jit(solution)/shard_map/ppermute | solution.py:551
  4.1 0.0 copy-start.5
  4.1 1.1 %band_sums.1.band_ref = f32[384,128]{1,0:T(8,128)S(1)} custom-call(f32[64,128]{1,0:T(8,128)S(1)} %get-tuple-element.11.live_ref, f32[64,128]{1,0:T(8,128)S(1)} %bitcast.18, f32[3,8192]{1,0:T(4,128)S(1)} %copy-done, f32[64,128]{1,0:T(8,128)S(1)} %bitcast.25, s32[64,128]{1,0:T(8,128)S(1)} %bitcast.21), custom_call_target="tpu_custom_call" | custom-call | tf_op jit(solution)/shard_map/band_sums/pallas_call | solution.py:538
  5.2 1.3 %residuals.1 = (f32[5,1024]{1,0:T(8,128)}, f32[64,128]{1,0:T(8,128)S(1)}, f32[4,112,128]{2,1,0:T(8,128)S(1)}) custom-call(f32[20,8,128]{2,1,0:T(8,128)S(1)} %get-tuple-element.10.mine_ref, f32[20,8,128]{2,1,0:T(8,128)S(1)} %collective-permute-done.other_ref, f32[384,128]{1,0:T(8,128)S(1)} %band_sums.1.band_ref, f32[64,128]{1,0:T(8,128)S(1)} %get-tuple-element.11.live_ref, ...), custom_call_target="tpu_custom_call" | custom-call | tf_op jit(solution)/shard_map/residuals/pallas_call | solution.py:538
  6.6 0.2 collective-permute-start.1
  6.8 1.2 %collective-permute-done.1 = f32[2,112,128]{2,1,0:T(8,128)S(1)} collective-permute-done((f32[2,112,128]{2,1,0:T(8,128)S(1)}, f32[2,112,128]{2,1,0:T(8,128)S(1)}, u32[]{:S(2)}, u32[]{:S(2)}) %collective-permute-start.1) | collective-permute-done | bytes 114720 | tf_op jit(solution)/shard_map/ppermute | solution.py:551
  8.0 2.7 %collective-permute-start.2 = (f32[1,112,128]{2,1,0:T(8,128)S(1)}, f32[1,112,128]{2,1,0:T(8,128)S(1)}, u32[]{:S(2)}, u32[]{:S(2)}) collective-permute-start(f32[1,112,128]{2,1,0:T(8,128)S(1)} %constant_dynamic-slice_fusion), channel_id=1, source_target_pairs={{0,3},{1,2},{2,1},{3,0},{4,7},{5,6},{6,5},{7,4},{8,11},{9,10},{10,... | collective-permute-start | bytes 172040 | tf_op jit(solution)/shard_map/ppermute | solution.py:551
  10.7 2.1 %collective-permute-done.2 = f32[1,112,128]{2,1,0:T(8,128)S(1)} collective-permute-done((f32[1,112,128]{2,1,0:T(8,128)S(1)}, f32[1,112,128]{2,1,0:T(8,128)S(1)}, u32[]{:S(2)}, u32[]{:S(2)}) %collective-permute-start.2) | collective-permute-done | bytes 57376 | tf_op jit(solution)/shard_map/ppermute | solution.py:551
  12.8 1.6 %collective-permute-start.3 = (f32[112,128]{1,0:T(8,128)S(1)}, f32[112,128]{1,0:T(8,128)S(1)}, u32[]{:S(2)}, u32[]{:S(2)}) collective-permute-start(f32[112,128]{1,0:T(8,128)S(1)} %add_bitcast_fusion), channel_id=1, source_target_pairs={{0,5},{1,4},{2,7},{3,6},{4,1},{5,0},{6,3},{7,2},{8,13},{9,12},{10,... | collective-permute-start | bytes 172040 | tf_op jit(solution)/shard_map/ppermute | solution.py:551
  14.4 2.3 %collective-permute-done.3 = f32[112,128]{1,0:T(8,128)S(1)} collective-permute-done((f32[112,128]{1,0:T(8,128)S(1)}, f32[112,128]{1,0:T(8,128)S(1)}, u32[]{:S(2)}, u32[]{:S(2)}) %collective-permute-start.3) | collective-permute-done | bytes 57376 | tf_op jit(solution)/shard_map/ppermute | solution.py:551
  16.8 1.5 %collective-permute-start.4 = (f32[112,128]{1,0:T(8,128)S(1)}, f32[112,128]{1,0:T(8,128)S(1)}, u32[]{:S(2)}, u32[]{:S(2)}) collective-permute-start(f32[112,128]{1,0:T(8,128)S(1)} %add.41), channel_id=1, source_target_pairs={{0,9},{1,8},{2,11},{3,10},{4,13},{5,12},{6,15},{7,14},{8,1},{9,0},... | collective-permute-start | bytes 172040 | tf_op jit(solution)/shard_map/ppermute | solution.py:551
  18.3 2.5 %collective-permute-done.4 = f32[112,128]{1,0:T(8,128)S(1)} collective-permute-done((f32[112,128]{1,0:T(8,128)S(1)}, f32[112,128]{1,0:T(8,128)S(1)}, u32[]{:S(2)}, u32[]{:S(2)}) %collective-permute-start.4) | collective-permute-done | bytes 57376 | tf_op jit(solution)/shard_map/ppermute | solution.py:551
  20.7 2.3 %collective-permute-start.5 = (f32[112,128]{1,0:T(8,128)S(1)}, f32[112,128]{1,0:T(8,128)S(1)}, u32[]{:S(2)}, u32[]{:S(2)}) collective-permute-start(f32[112,128]{1,0:T(8,128)S(1)} %add.42), channel_id=1, source_target_pairs={{0,17},{1,16},{2,19},{3,18},{4,21},{5,20},{6,23},{7,22},{8,25},{9,... | collective-permute-start | bytes 172040 | tf_op jit(solution)/shard_map/ppermute | solution.py:551
  23.0 0.1 pad_add_fusion.place_ref
  23.1 3.7 %collective-permute-done.5 = f32[112,128]{1,0:T(8,128)S(1)} collective-permute-done((f32[112,128]{1,0:T(8,128)S(1)}, f32[112,128]{1,0:T(8,128)S(1)}, u32[]{:S(2)}, u32[]{:S(2)}) %collective-permute-start.5) | collective-permute-done | bytes 57376 | tf_op jit(solution)/shard_map/ppermute | solution.py:551
  26.8 0.8 %attitude.1 = f32[16,128]{1,0:T(8,128)S(1)} custom-call(s32[2]{0:T(128)S(1)} %pad_add_fusion.place_ref, f32[112,128]{1,0:T(8,128)S(1)} %add.43.sums_ref), custom_call_target="tpu_custom_call" | custom-call | tf_op jit(solution)/shard_map/attitude/pallas_call | solution.py:538
  27.6 1.0 %collective-permute-start.6 = (f32[16,128]{1,0:T(8,128)S(1)}, f32[16,128]{1,0:T(8,128)S(1)}, u32[]{:S(2)}, u32[]{:S(2)}) collective-permute-start(f32[16,128]{1,0:T(8,128)S(1)} %attitude.1), channel_id=1, source_target_pairs={{0,3},{1,2},{2,1},{3,0},{4,7},{5,6},{6,5},{7,4},{8,11},{9,10},{10,... | collective-permute-start | bytes 24584 | tf_op jit(solution)/shard_map/ppermute | solution.py:551
  28.6 2.2 %collective-permute-done.6 = f32[16,128]{1,0:T(8,128)S(1)} collective-permute-done((f32[16,128]{1,0:T(8,128)S(1)}, f32[16,128]{1,0:T(8,128)S(1)}, u32[]{:S(2)}, u32[]{:S(2)}) %collective-permute-start.6) | collective-permute-done | bytes 8224 | tf_op jit(solution)/shard_map/ppermute | solution.py:551
  30.8 0.2 collective-permute-start.7
  30.9 0.1 prepare.1.factor_ref
  31.0 0.9 %collective-permute-done.7 = f32[32,128]{1,0:T(8,128)S(1)} collective-permute-done((f32[32,128]{1,0:T(8,128)S(1)}, f32[32,128]{1,0:T(8,128)S(1)}, u32[]{:S(2)}, u32[]{:S(2)}) %collective-permute-start.7) | collective-permute-done | bytes 16416 | tf_op jit(solution)/shard_map/ppermute | solution.py:551
  32.0 0.9 %predict.1 = (f32[3,128]{1,0:T(4,128)}, f32[64,128]{1,0:T(8,128)}) custom-call(s32[1]{0:T(128)} %bitcast.5.place_ref, f32[16,4,128]{2,1,0:T(4,128)S(1)} %bitcast.27, f32[12,64,128]{2,1,0:T(8,128)S(1)} %prepare.1.factor_ref, f32[64,128]{1,0:T(8,128)S(1)} %get-tuple-element.14.resid_ref, s32[64,128]{1,0:T(8,128)S(1)} %bitcast.23), custom_call_target="tpu_custom_call" | custom-call | tf_op jit(solution)/shard_map/predict/pallas_call | solution.py:538
  (24 shorter events, 0.1 us)
Async XLA Ops:
  0.6 3.4 %copy-start = (f32[3,8192]{1,0:T(4,128)S(1)}, f32[3,8192]{1,0:T(4,128)}, u32[]{:S(2)}) copy-start(f32[3,8192]{1,0:T(4,128)} %axis_ref.5) | copy-start | bytes 294916
  0.6 3.4 %copy-start.2 = (f32[8192]{0:T(1024)S(1)}, f32[8192]{0:T(1024)}, u32[]{:S(2)}) copy-start(f32[8192]{0:T(1024)} %param.11) | copy-start | bytes 98308
  0.7 3.4 %copy-start.3 = (s32[8192]{0:T(1024)S(1)}, s32[8192]{0:T(1024)}, u32[]{:S(2)}) copy-start(s32[8192]{0:T(1024)} %param.14) | copy-start | bytes 98308
  0.7 3.4 %copy-start.4 = (f32[8192]{0:T(1024)S(1)}, f32[8192]{0:T(1024)}, u32[]{:S(2)}) copy-start(f32[8192]{0:T(1024)} %param.10) | copy-start | bytes 98308
  3.5 1.7 %copy-start.1 = (f32[5,8192]{1,0:T(8,128)S(1)}, f32[5,8192]{1,0:T(8,128)}, u32[]{:S(2)}) copy-start(f32[5,8192]{1,0:T(8,128)} %design_ref.1) | copy-start | bytes 491524
  3.5 1.7 %collective-permute-start = (f32[20,8,128]{2,1,0:T(8,128)S(1)}, f32[20,8,128]{2,1,0:T(8,128)S(1)}, u32[]{:S(2)}, u32[]{:S(2)}) collective-permute-start(f32[20,8,128]{2,1,0:T(8,128)S(1)} %get-tuple-element.10.mine_ref), channel_id=1, source_target_pairs={{0,1},{1,0},{2,3},{3,2},{4,5},{5,4},{6,7},{7,6},{8,9},{9,8},{10,11... | collective-permute-start | bytes 245768 | tf_op jit(solution)/shard_map/ppermute | solution.py:551
  4.1 1.1 %copy-start.5 = (f32[8192]{0:T(1024)S(1)}, f32[8192]{0:T(1024)}, u32[]{:S(2)}) copy-start(f32[8192]{0:T(1024)} %param.9) | copy-start | bytes 98308
  4.1 1.1 %copy-start.6 = (s32[8192]{0:T(1024)S(1)}, s32[8192]{0:T(1024)}, u32[]{:S(2)}) copy-start(s32[8192]{0:T(1024)} %param.13) | copy-start | bytes 98308
  6.6 1.4 %collective-permute-start.1 = (f32[2,112,128]{2,1,0:T(8,128)S(1)}, f32[2,112,128]{2,1,0:T(8,128)S(1)}, u32[]{:S(2)}, u32[]{:S(2)}) collective-permute-start(f32[2,112,128]{2,1,0:T(8,128)S(1)} %dynamic-slice_bitcast_fusion), channel_id=1, source_target_pairs={{0,1},{1,0},{2,3},{3,2},{4,5},{5,4},{6,7},{7,6},{8,9},{9,8},{10,11... | collective-permute-start | bytes 344072 | tf_op jit(solution)/shard_map/ppermute | solution.py:551
  8.0 4.8 %collective-permute-start.2 = (f32[1,112,128]{2,1,0:T(8,128)S(1)}, f32[1,112,128]{2,1,0:T(8,128)S(1)}, u32[]{:S(2)}, u32[]{:S(2)}) collective-permute-start(f32[1,112,128]{2,1,0:T(8,128)S(1)} %constant_dynamic-slice_fusion), channel_id=1, source_target_pairs={{0,3},{1,2},{2,1},{3,0},{4,7},{5,6},{6,5},{7,4},{8,11},{9,10},{10,... | collective-permute-start | bytes 172040 | tf_op jit(solution)/shard_map/ppermute | solution.py:551
  12.8 3.9 %collective-permute-start.3 = (f32[112,128]{1,0:T(8,128)S(1)}, f32[112,128]{1,0:T(8,128)S(1)}, u32[]{:S(2)}, u32[]{:S(2)}) collective-permute-start(f32[112,128]{1,0:T(8,128)S(1)} %add_bitcast_fusion), channel_id=1, source_target_pairs={{0,5},{1,4},{2,7},{3,6},{4,1},{5,0},{6,3},{7,2},{8,13},{9,12},{10,... | collective-permute-start | bytes 172040 | tf_op jit(solution)/shard_map/ppermute | solution.py:551
  16.8 3.9 %collective-permute-start.4 = (f32[112,128]{1,0:T(8,128)S(1)}, f32[112,128]{1,0:T(8,128)S(1)}, u32[]{:S(2)}, u32[]{:S(2)}) collective-permute-start(f32[112,128]{1,0:T(8,128)S(1)} %add.41), channel_id=1, source_target_pairs={{0,9},{1,8},{2,11},{3,10},{4,13},{5,12},{6,15},{7,14},{8,1},{9,0},... | collective-permute-start | bytes 172040 | tf_op jit(solution)/shard_map/ppermute | solution.py:551
  20.7 6.1 %collective-permute-start.5 = (f32[112,128]{1,0:T(8,128)S(1)}, f32[112,128]{1,0:T(8,128)S(1)}, u32[]{:S(2)}, u32[]{:S(2)}) collective-permute-start(f32[112,128]{1,0:T(8,128)S(1)} %add.42), channel_id=1, source_target_pairs={{0,17},{1,16},{2,19},{3,18},{4,21},{5,20},{6,23},{7,22},{8,25},{9,... | collective-permute-start | bytes 172040 | tf_op jit(solution)/shard_map/ppermute | solution.py:551
  27.6 3.1 %collective-permute-start.6 = (f32[16,128]{1,0:T(8,128)S(1)}, f32[16,128]{1,0:T(8,128)S(1)}, u32[]{:S(2)}, u32[]{:S(2)}) collective-permute-start(f32[16,128]{1,0:T(8,128)S(1)} %attitude.1), channel_id=1, source_target_pairs={{0,3},{1,2},{2,1},{3,0},{4,7},{5,6},{6,5},{7,4},{8,11},{9,10},{10,... | collective-permute-start | bytes 24584 | tf_op jit(solution)/shard_map/ppermute | solution.py:551
  30.8 1.2 %collective-permute-start.7 = (f32[32,128]{1,0:T(8,128)S(1)}, f32[32,128]{1,0:T(8,128)S(1)}, u32[]{:S(2)}, u32[]{:S(2)}) collective-permute-start(f32[32,128]{1,0:T(8,128)S(1)} %pad_maximum_fusion.1), channel_id=1, source_target_pairs={{0,1},{1,0},{2,3},{3,2},{4,5},{5,4},{6,7},{7,6},{8,9},{9,8},{10,11... | collective-permute-start | bytes 49160 | tf_op jit(solution)/shard_map/ppermute | solution.py:551

commit v6 on v5

--- a/solution.py
+++ b/solution.py
@@ -1,3 +1,4 @@
+import functools
 import math
 
 import jax
@@ -431,7 +432,15 @@
     pack(band_ref, 3, QUANTITIES - 3, 1, message_ref)
 
 
-def solve_kernel(place_ref, sums_ref, out_ref, edges_ref):
+def part_bits():
+    place = lax.axis_index("src")
+    upper = lax.axis_index("ccd")
+    for shift in range(lax.axis_size("src").bit_length() - 1):
+        upper = upper ^ ((place >> shift) & 1)
+    return [upper, place & 1]
+
+
+def solve_kernel(parts, sums_ref, out_ref, edges_ref):
     owned = out_ref.shape[0] // 4
     ring = -(-(owned + 2) // SUB) * SUB
     order = {pair: n for n, pair in enumerate(PAIRS)}
@@ -439,7 +448,8 @@
     inside = row < owned
     after = (row == owned) & (lane < REACH)
     before = (row == ring - 1) & (lane >= LANES - REACH)
-    edge = (place_ref[0] == place_ref[1] - 1).astype(jnp.int32)
+    part = 0 if parts == 1 else sum(bit << i for i, bit in enumerate(reversed(part_bits())))
+    edge = (part == parts - 1) * jnp.ones((), jnp.int32)
     known = jnp.where(after & (jnp.full((ring, LANES), edge, jnp.int32) == 1), 0.0, 1.0)
 
     back = LANES - REACH - WINDOW * (SUB - 1)
@@ -501,14 +511,14 @@
     over_steps(phase_ref.shape[0], group)
 
 
-def predict_kernel(place_ref, coef_ref, factor_ref, resid_ref, knot_ref, att_ref, out_ref, windows):
+def predict_kernel(coef_ref, factor_ref, resid_ref, knot_ref, att_ref, out_ref, windows):
     tiles, shards = resid_ref.shape[0], coef_ref.shape[0]
     rep = tiles // shards
     for x in range(3):
         coefs = coef_ref[:, x, :]
         for j in range(4):
             windows[x * 4 + j] = coefs if j == 0 else shift_down(coefs, j)
-        att_ref[x : x + 1, :] = windows[x * 4, pl.ds(place_ref[0], 1), :]
+        att_ref[x : x + 1, :] = windows[x * 4, pl.ds(lax.axis_index("src"), 1), :]
     row = iota((SUB, LANES), 0)
 
     def group(start, steps):
@@ -626,29 +636,23 @@
         prepare_kernel, "prepare", [], [message, live, phase, axis_factors],
         jax.ShapeDtypeStruct((12, tiles, LANES), f32), [tiled],
     )
-    place = lax.axis_index("src")
     if fast:
-        upper = lax.axis_index("ccd")
-        for shift in range(shards.bit_length() - 1):
-            upper = upper ^ ((place >> shift) & 1)
-        lower = place & 1
+        upper, lower = part_bits()
         sums = halved(halved(message, 1, upper), 3, lower)[0]
         bit = 2
         while bit < shards:
             sums = sums + swapped(sums, BOTH, 2 * bit + 1)
             bit *= 2
-        part = 2 * upper + lower
     else:
         sums = summed_over(summed_over(message[0], "ccd"), "src")
-        part = jnp.zeros_like(place)
     coefs = call(
-        solve_kernel, "attitude", [jnp.stack([part, jnp.full_like(part, parts)])], [sums],
+        functools.partial(solve_kernel, parts), "attitude", [], [sums],
         jax.ShapeDtypeStruct((owned * 4, LANES), f32), [pltpu.VMEM((halo_rows() * SUB, LANES), f32)],
     )
     if fast:
         coefs = doubled(doubled(coefs, 3, lower), 1, upper)
     attitude, residual = call(
-        predict_kernel, "predict", [place.reshape(1)], [coefs.reshape(shards, 4, LANES), factors, resid, knots],
+        predict_kernel, "predict", [], [coefs.reshape(shards, 4, LANES), factors, resid, knots],
         (jax.ShapeDtypeStruct((3, KNOT_DEV), f32), jax.ShapeDtypeStruct((tiles, LANES), f32)),
         [pltpu.VMEM((12, shards, KNOT_DEV), f32)],
     )

time: 33.1 us -> 32.5 us (0.982)
  Pallas kernels: 7.02 us -> 6.48 us
    pallas_call x6, Pallas kernels: 7.02 us -> 6.48 us  [call(): pl.pallas_call(kernel, name=name, out_shape=outs, in_specs=[SMEM] * len(s...]
where the time goes in v6:
time: 32.5 us; the launch traced here: 32.4 us
  waiting for transfers between devices  15.1 us (46%)
  starting transfers between devices  9.89 us (30%)
  Pallas kernels  6.48 us (20%)
  between operations  0.8 us (2%)
    ppermute x8, waiting for transfers between devices, swapped(): return lax.ppermute(value, axis, [(i, i ^ bit) for i in range(size)])  15.1 us
    ppermute x8, starting transfers between devices, swapped(): return lax.ppermute(value, axis, [(i, i ^ bit) for i in range(size)])  9.89 us
    pallas_call x6, Pallas kernels, call(): pl.pallas_call(kernel, name=name, out_shape=outs, in_specs=[SMEM] * len(s...  6.48 us
  transfers between devices with their start and end apart: 8, of which 7 were waited for; matrix products, arithmetic and copies ran while one was open for 0% of the time, Pallas kernels for 4%

profile of v6, /device:TPU:0, one launch (start us, length us, event | category | flops | bytes accessed | tf_op | source)
XLA Modules:
  0.0 32.4 jit_solution(400539708032863731)
XLA Ops:
  0.7 2.8 %source_sums.1 = (f32[20,8,128]{2,1,0:T(8,128)S(1)}, f32[64,128]{1,0:T(8,128)S(1)}) custom-call(s32[1,1,16]{2,1,0:T(1,128)} %counts_hbm.1, f32[5,8192]{1,0:T(8,128)} %design_ref.1, f32[64,128]{1,0:T(8,128)} %bitcast.26, f32[64,128]{1,0:T(8,128)} %bitcast.19, s32[64,128]{1,0:T(8,128)} %bitcast.28), custom_call_target="tpu_custom_call" | custom-call | tf_op jit(solution)/shard_map/source_sums/pallas_call | solution.py:548
  3.5 0.0 copy-start.1
  3.5 0.6 %collective-permute-start = (f32[20,8,128]{2,1,0:T(8,128)S(1)}, f32[20,8,128]{2,1,0:T(8,128)S(1)}, u32[]{:S(2)}, u32[]{:S(2)}) collective-permute-start(f32[20,8,128]{2,1,0:T(8,128)S(1)} %get-tuple-element.10.mine_ref), channel_id=1, source_target_pairs={{0,1},{1,0},{2,3},{3,2},{4,5},{5,4},{6,7},{7,6},{8,9},{9,8},{10,11... | collective-permute-start | bytes 245768 | tf_op jit(solution)/shard_map/ppermute | solution.py:561
  4.1 0.0 copy-start.5
  4.1 0.0 copy-start.6
  4.1 1.1 %band_sums.1.band_ref = f32[384,128]{1,0:T(8,128)S(1)} custom-call(f32[64,128]{1,0:T(8,128)S(1)} %get-tuple-element.11.live_ref, f32[64,128]{1,0:T(8,128)S(1)} %bitcast.16, f32[3,8192]{1,0:T(4,128)S(1)} %copy-done, f32[64,128]{1,0:T(8,128)S(1)} %bitcast.20, s32[64,128]{1,0:T(8,128)S(1)} %bitcast.22), custom_call_target="tpu_custom_call" | custom-call | tf_op jit(solution)/shard_map/band_sums/pallas_call | solution.py:548
  5.2 1.3 %residuals.1 = (f32[5,1024]{1,0:T(8,128)}, f32[64,128]{1,0:T(8,128)S(1)}, f32[4,112,128]{2,1,0:T(8,128)S(1)}) custom-call(f32[20,8,128]{2,1,0:T(8,128)S(1)} %get-tuple-element.10.mine_ref, f32[20,8,128]{2,1,0:T(8,128)S(1)} %collective-permute-done.other_ref, f32[384,128]{1,0:T(8,128)S(1)} %band_sums.1.band_ref, f32[64,128]{1,0:T(8,128)S(1)} %get-tuple-element.11.live_ref, ...), custom_call_target="tpu_custom_call" | custom-call | tf_op jit(solution)/shard_map/residuals/pallas_call | solution.py:548
  6.6 0.2 collective-permute-start.1
  6.8 1.2 %collective-permute-done.1 = f32[2,112,128]{2,1,0:T(8,128)S(1)} collective-permute-done((f32[2,112,128]{2,1,0:T(8,128)S(1)}, f32[2,112,128]{2,1,0:T(8,128)S(1)}, u32[]{:S(2)}, u32[]{:S(2)}) %collective-permute-start.1) | collective-permute-done | bytes 114720 | tf_op jit(solution)/shard_map/ppermute | solution.py:561
  8.0 2.7 %collective-permute-start.2 = (f32[1,112,128]{2,1,0:T(8,128)S(1)}, f32[1,112,128]{2,1,0:T(8,128)S(1)}, u32[]{:S(2)}, u32[]{:S(2)}) collective-permute-start(f32[1,112,128]{2,1,0:T(8,128)S(1)} %constant_dynamic-slice_fusion), channel_id=1, source_target_pairs={{0,3},{1,2},{2,1},{3,0},{4,7},{5,6},{6,5},{7,4},{8,11},{9,10},{10,... | collective-permute-start | bytes 172040 | tf_op jit(solution)/shard_map/ppermute | solution.py:561
  10.7 2.1 %collective-permute-done.2 = f32[1,112,128]{2,1,0:T(8,128)S(1)} collective-permute-done((f32[1,112,128]{2,1,0:T(8,128)S(1)}, f32[1,112,128]{2,1,0:T(8,128)S(1)}, u32[]{:S(2)}, u32[]{:S(2)}) %collective-permute-start.2) | collective-permute-done | bytes 57376 | tf_op jit(solution)/shard_map/ppermute | solution.py:561
  12.8 1.6 %collective-permute-start.3 = (f32[112,128]{1,0:T(8,128)S(1)}, f32[112,128]{1,0:T(8,128)S(1)}, u32[]{:S(2)}, u32[]{:S(2)}) collective-permute-start(f32[112,128]{1,0:T(8,128)S(1)} %add_bitcast_fusion), channel_id=1, source_target_pairs={{0,5},{1,4},{2,7},{3,6},{4,1},{5,0},{6,3},{7,2},{8,13},{9,12},{10,... | collective-permute-start | bytes 172040 | tf_op jit(solution)/shard_map/ppermute | solution.py:561
  14.4 2.3 %collective-permute-done.3 = f32[112,128]{1,0:T(8,128)S(1)} collective-permute-done((f32[112,128]{1,0:T(8,128)S(1)}, f32[112,128]{1,0:T(8,128)S(1)}, u32[]{:S(2)}, u32[]{:S(2)}) %collective-permute-start.3) | collective-permute-done | bytes 57376 | tf_op jit(solution)/shard_map/ppermute | solution.py:561
  16.8 1.5 %collective-permute-start.4 = (f32[112,128]{1,0:T(8,128)S(1)}, f32[112,128]{1,0:T(8,128)S(1)}, u32[]{:S(2)}, u32[]{:S(2)}) collective-permute-start(f32[112,128]{1,0:T(8,128)S(1)} %add.37), channel_id=1, source_target_pairs={{0,9},{1,8},{2,11},{3,10},{4,13},{5,12},{6,15},{7,14},{8,1},{9,0},... | collective-permute-start | bytes 172040 | tf_op jit(solution)/shard_map/ppermute | solution.py:561
  18.3 2.5 %collective-permute-done.4 = f32[112,128]{1,0:T(8,128)S(1)} collective-permute-done((f32[112,128]{1,0:T(8,128)S(1)}, f32[112,128]{1,0:T(8,128)S(1)}, u32[]{:S(2)}, u32[]{:S(2)}) %collective-permute-start.4) | collective-permute-done | bytes 57376 | tf_op jit(solution)/shard_map/ppermute | solution.py:561
  20.7 2.3 %collective-permute-start.5 = (f32[112,128]{1,0:T(8,128)S(1)}, f32[112,128]{1,0:T(8,128)S(1)}, u32[]{:S(2)}, u32[]{:S(2)}) collective-permute-start(f32[112,128]{1,0:T(8,128)S(1)} %add.38), channel_id=1, source_target_pairs={{0,17},{1,16},{2,19},{3,18},{4,21},{5,20},{6,23},{7,22},{8,25},{9,... | collective-permute-start | bytes 172040 | tf_op jit(solution)/shard_map/ppermute | solution.py:561
  23.0 3.8 %collective-permute-done.5 = f32[112,128]{1,0:T(8,128)S(1)} collective-permute-done((f32[112,128]{1,0:T(8,128)S(1)}, f32[112,128]{1,0:T(8,128)S(1)}, u32[]{:S(2)}, u32[]{:S(2)}) %collective-permute-start.5) | collective-permute-done | bytes 57376 | tf_op jit(solution)/shard_map/ppermute | solution.py:561
  26.8 0.3 attitude.1
  27.1 1.0 %collective-permute-start.6 = (f32[16,128]{1,0:T(8,128)S(1)}, f32[16,128]{1,0:T(8,128)S(1)}, u32[]{:S(2)}, u32[]{:S(2)}) collective-permute-start(f32[16,128]{1,0:T(8,128)S(1)} %attitude.1), channel_id=1, source_target_pairs={{0,3},{1,2},{2,1},{3,0},{4,7},{5,6},{6,5},{7,4},{8,11},{9,10},{10,... | collective-permute-start | bytes 24584 | tf_op jit(solution)/shard_map/ppermute | solution.py:561
  28.1 2.2 %collective-permute-done.6 = f32[16,128]{1,0:T(8,128)S(1)} collective-permute-done((f32[16,128]{1,0:T(8,128)S(1)}, f32[16,128]{1,0:T(8,128)S(1)}, u32[]{:S(2)}, u32[]{:S(2)}) %collective-permute-start.6) | collective-permute-done | bytes 8224 | tf_op jit(solution)/shard_map/ppermute | solution.py:561
  30.2 0.2 collective-permute-start.7
  30.4 0.1 prepare.1.factor_ref
  30.5 0.9 %collective-permute-done.7 = f32[32,128]{1,0:T(8,128)S(1)} collective-permute-done((f32[32,128]{1,0:T(8,128)S(1)}, f32[32,128]{1,0:T(8,128)S(1)}, u32[]{:S(2)}, u32[]{:S(2)}) %collective-permute-start.7) | collective-permute-done | bytes 16416 | tf_op jit(solution)/shard_map/ppermute | solution.py:561
  31.4 0.9 %predict.1 = (f32[3,128]{1,0:T(4,128)}, f32[64,128]{1,0:T(8,128)}) custom-call(f32[16,4,128]{2,1,0:T(4,128)S(1)} %bitcast.25, f32[12,64,128]{2,1,0:T(8,128)S(1)} %prepare.1.factor_ref, f32[64,128]{1,0:T(8,128)S(1)} %get-tuple-element.14.resid_ref, s32[64,128]{1,0:T(8,128)S(1)} %bitcast.24), custom_call_target="tpu_custom_call" | custom-call | tf_op jit(solution)/shard_map/predict/pallas_call | solution.py:548
  (23 shorter events, 0.1 us)
Async XLA Ops:
  0.6 3.4 %copy-start = (f32[3,8192]{1,0:T(4,128)S(1)}, f32[3,8192]{1,0:T(4,128)}, u32[]{:S(2)}) copy-start(f32[3,8192]{1,0:T(4,128)} %axis_ref.5) | copy-start | bytes 294916
  0.6 3.4 %copy-start.2 = (f32[8192]{0:T(1024)S(1)}, f32[8192]{0:T(1024)}, u32[]{:S(2)}) copy-start(f32[8192]{0:T(1024)} %param.11) | copy-start | bytes 98308
  0.7 3.4 %copy-start.3 = (f32[8192]{0:T(1024)S(1)}, f32[8192]{0:T(1024)}, u32[]{:S(2)}) copy-start(f32[8192]{0:T(1024)} %param.10) | copy-start | bytes 98308
  0.7 3.4 %copy-start.4 = (s32[8192]{0:T(1024)S(1)}, s32[8192]{0:T(1024)}, u32[]{:S(2)}) copy-start(s32[8192]{0:T(1024)} %param.14) | copy-start | bytes 98308
  3.5 1.7 %copy-start.1 = (f32[5,8192]{1,0:T(8,128)S(1)}, f32[5,8192]{1,0:T(8,128)}, u32[]{:S(2)}) copy-start(f32[5,8192]{1,0:T(8,128)} %design_ref.1) | copy-start | bytes 491524
  3.5 1.7 %collective-permute-start = (f32[20,8,128]{2,1,0:T(8,128)S(1)}, f32[20,8,128]{2,1,0:T(8,128)S(1)}, u32[]{:S(2)}, u32[]{:S(2)}) collective-permute-start(f32[20,8,128]{2,1,0:T(8,128)S(1)} %get-tuple-element.10.mine_ref), channel_id=1, source_target_pairs={{0,1},{1,0},{2,3},{3,2},{4,5},{5,4},{6,7},{7,6},{8,9},{9,8},{10,11... | collective-permute-start | bytes 245768 | tf_op jit(solution)/shard_map/ppermute | solution.py:561
  4.1 1.1 %copy-start.5 = (f32[8192]{0:T(1024)S(1)}, f32[8192]{0:T(1024)}, u32[]{:S(2)}) copy-start(f32[8192]{0:T(1024)} %param.9) | copy-start | bytes 98308
  4.1 1.1 %copy-start.6 = (s32[8192]{0:T(1024)S(1)}, s32[8192]{0:T(1024)}, u32[]{:S(2)}) copy-start(s32[8192]{0:T(1024)} %param.13) | copy-start | bytes 98308
  6.6 1.4 %collective-permute-start.1 = (f32[2,112,128]{2,1,0:T(8,128)S(1)}, f32[2,112,128]{2,1,0:T(8,128)S(1)}, u32[]{:S(2)}, u32[]{:S(2)}) collective-permute-start(f32[2,112,128]{2,1,0:T(8,128)S(1)} %dynamic-slice_bitcast_fusion), channel_id=1, source_target_pairs={{0,1},{1,0},{2,3},{3,2},{4,5},{5,4},{6,7},{7,6},{8,9},{9,8},{10,11... | collective-permute-start | bytes 344072 | tf_op jit(solution)/shard_map/ppermute | solution.py:561
  8.0 4.8 %collective-permute-start.2 = (f32[1,112,128]{2,1,0:T(8,128)S(1)}, f32[1,112,128]{2,1,0:T(8,128)S(1)}, u32[]{:S(2)}, u32[]{:S(2)}) collective-permute-start(f32[1,112,128]{2,1,0:T(8,128)S(1)} %constant_dynamic-slice_fusion), channel_id=1, source_target_pairs={{0,3},{1,2},{2,1},{3,0},{4,7},{5,6},{6,5},{7,4},{8,11},{9,10},{10,... | collective-permute-start | bytes 172040 | tf_op jit(solution)/shard_map/ppermute | solution.py:561
  12.8 3.9 %collective-permute-start.3 = (f32[112,128]{1,0:T(8,128)S(1)}, f32[112,128]{1,0:T(8,128)S(1)}, u32[]{:S(2)}, u32[]{:S(2)}) collective-permute-start(f32[112,128]{1,0:T(8,128)S(1)} %add_bitcast_fusion), channel_id=1, source_target_pairs={{0,5},{1,4},{2,7},{3,6},{4,1},{5,0},{6,3},{7,2},{8,13},{9,12},{10,... | collective-permute-start | bytes 172040 | tf_op jit(solution)/shard_map/ppermute | solution.py:561
  16.8 3.9 %collective-permute-start.4 = (f32[112,128]{1,0:T(8,128)S(1)}, f32[112,128]{1,0:T(8,128)S(1)}, u32[]{:S(2)}, u32[]{:S(2)}) collective-permute-start(f32[112,128]{1,0:T(8,128)S(1)} %add.37), channel_id=1, source_target_pairs={{0,9},{1,8},{2,11},{3,10},{4,13},{5,12},{6,15},{7,14},{8,1},{9,0},... | collective-permute-start | bytes 172040 | tf_op jit(solution)/shard_map/ppermute | solution.py:561
  20.7 6.1 %collective-permute-start.5 = (f32[112,128]{1,0:T(8,128)S(1)}, f32[112,128]{1,0:T(8,128)S(1)}, u32[]{:S(2)}, u32[]{:S(2)}) collective-permute-start(f32[112,128]{1,0:T(8,128)S(1)} %add.38), channel_id=1, source_target_pairs={{0,17},{1,16},{2,19},{3,18},{4,21},{5,20},{6,23},{7,22},{8,25},{9,... | collective-permute-start | bytes 172040 | tf_op jit(solution)/shard_map/ppermute | solution.py:561
  27.1 3.1 %collective-permute-start.6 = (f32[16,128]{1,0:T(8,128)S(1)}, f32[16,128]{1,0:T(8,128)S(1)}, u32[]{:S(2)}, u32[]{:S(2)}) collective-permute-start(f32[16,128]{1,0:T(8,128)S(1)} %attitude.1), channel_id=1, source_target_pairs={{0,3},{1,2},{2,1},{3,0},{4,7},{5,6},{6,5},{7,4},{8,11},{9,10},{10,... | collective-permute-start | bytes 24584 | tf_op jit(solution)/shard_map/ppermute | solution.py:561
  30.2 1.2 %collective-permute-start.7 = (f32[32,128]{1,0:T(8,128)S(1)}, f32[32,128]{1,0:T(8,128)S(1)}, u32[]{:S(2)}, u32[]{:S(2)}) collective-permute-start(f32[32,128]{1,0:T(8,128)S(1)} %pad_maximum_fusion.1), channel_id=1, source_target_pairs={{0,1},{1,0},{2,3},{3,2},{4,5},{5,4},{6,7},{7,6},{8,9},{9,8},{10,11... | collective-permute-start | bytes 49160 | tf_op jit(solution)/shard_map/ppermute | solution.py:561

commit v7 on v6

--- a/solution.py
+++ b/solution.py
@@ -72,30 +72,28 @@
         for n in range(m, 5):
             matrix[m, n] = moments[position] + (src_ridge if m == n else 0.0)
             position += 1
-    factor = {}
-    inverse = {}
+    scaled, factor, inverse = {}, {}, {}
     for j in range(5):
         for i in range(j, 5):
             running = matrix[j, i]
             for k in range(j):
-                running = running - factor[i, k] * factor[j, k]
-            if i == j:
-                factor[j, j] = jnp.sqrt(running)
-                inverse[j] = 1.0 / factor[j, j]
-            else:
-                factor[i, j] = running * inverse[j]
+                running = running - scaled[i, k] * factor[j, k]
+            scaled[i, j] = running
+        inverse[j] = 1.0 / scaled[j, j]
+        for i in range(j + 1, 5):
+            factor[i, j] = scaled[i, j] * inverse[j]
     forward = []
     for i in range(5):
         running = moments[15 + i]
         for k in range(i):
             running = running - factor[i, k] * forward[k]
-        forward.append(running * inverse[i])
+        forward.append(running)
     solved = [None] * 5
     for i in reversed(range(5)):
-        running = forward[i]
+        running = forward[i] * inverse[i]
         for k in range(i + 1, 5):
             running = running - factor[k, i] * solved[k]
-        solved[i] = running * inverse[i]
+        solved[i] = running
     return solved
 
 
@@ -220,8 +218,9 @@
 
 
 def source_kernel(
-    counts_hbm, design_hbm, obs_hbm, weight_hbm, index_hbm, out_ref, live_ref,
-    counts_ref, design_ref, obs_ref, weight_ref, index_ref, sems, low_ref, high_ref, total, tiled,
+    counts_hbm, weight_hbm, index_hbm, obs_hbm, design_hbm, phase_hbm, axis_hbm, knot_hbm,
+    out_ref, live_ref, weight_ref, index_ref, obs_ref, design_ref, phase_ref, axis_ref, knot_ref,
+    counts_ref, sems, low_ref, high_ref, total, tiled,
 ):
     tiles = obs_ref.shape[0]
     shards = counts_ref.shape[2]
@@ -230,7 +229,7 @@
         pltpu.make_async_copy(src, dst, sems.at[i])
         for i, (src, dst) in enumerate(
             [(counts_hbm, counts_ref), (weight_hbm, weight_ref), (index_hbm, index_ref), (obs_hbm, obs_ref),
-             (design_hbm, design_ref)]
+             (design_hbm, design_ref), (phase_hbm, phase_ref), (axis_hbm, axis_ref), (knot_hbm, knot_ref)]
         )
     ]
     for copy in copies:
@@ -283,6 +282,8 @@
             total[...] += got
 
     over_steps(tiles, group)
+    for copy in copies[5:]:
+        copy.wait()
     height = total.shape[0] // highs
     wide, half_tile = 2 * SUB, SUB // 2
     for h in range(highs):
@@ -296,7 +297,7 @@
             out_ref[wide:SIGNALS, h * (LOW // LANES) + half, :] = rest[:, cols]
 
 
-def band_kernel(live_ref, phase_ref, axis_ref, weight_ref, knot_ref, out_ref, tiled, powers_ref, moments):
+def band_kernel(phase_ref, axis_ref, weight_ref, knot_ref, out_ref, tiled, powers_ref, moments):
     tiles, shards = phase_ref.shape[0], out_ref.shape[0] // 24
     rep = tiles // shards
     by_tile(axis_ref, tiled)
@@ -310,7 +311,7 @@
         r = 1.0 - u
         u2, r2 = u * u, r * r
         u3, r3 = u2 * u, r2 * r
-        w = weight_ref[at, :] * live_ref[at, :]
+        w = weight_ref[at, :]
         u3w, r3w = u3 * w, r3 * w
         powers = [r3w * r3, r3w * (r2 * u), r3w * (r * u2), r3w * u3, u3w * (r2 * u), u3w * (r * u2), u3w * u3]
         for p in range(7):
@@ -596,19 +597,20 @@
     tiled = pltpu.VMEM((tiles * SUB, LANES), f32)
     dense = pltpu.VMEM((tiles, LANES), f32)
     blocks = SRC_DEV // LANES
-    moments, live = call(
+    inputs = (w, index, obs, design, phase, axis_factors, knots)
+    moments, live, w, index, obs, design, phase, axis_factors, knots = call(
         source_kernel, "source_sums", [],
-        [pltpu.with_memory_space_constraint(a, pltpu.HBM) for a in (counts, design, obs, w, index)],
-        (jax.ShapeDtypeStruct((SIGNALS, blocks, LANES), f32), jax.ShapeDtypeStruct((tiles, LANES), f32)),
+        [pltpu.with_memory_space_constraint(a, pltpu.HBM) for a in (counts,) + inputs],
+        (jax.ShapeDtypeStruct((SIGNALS, blocks, LANES), f32), jax.ShapeDtypeStruct((tiles, LANES), f32))
+        + tuple(jax.ShapeDtypeStruct(a.shape, a.dtype) for a in inputs),
         [
-            pltpu.SMEM(counts.shape, jnp.int32), pltpu.VMEM(design.shape, f32), dense, dense,
-            pltpu.VMEM((tiles, LANES), jnp.int32), pltpu.SemaphoreType.DMA((5,)), dense, dense,
+            pltpu.SMEM(counts.shape, jnp.int32), pltpu.SemaphoreType.DMA((8,)), dense, dense,
             pltpu.VMEM((SRC_DEV // LOW * 64, LOW), f32), tiled,
         ],
         HBM,
     )
     band = call(
-        band_kernel, "band_sums", [], [live, phase, axis_factors, w, knots],
+        band_kernel, "band_sums", [], [phase, axis_factors, w, knots],
         jax.ShapeDtypeStruct((24 * shards, KNOT_DEV), f32),
         [tiled, tiled, pltpu.VMEM((shards * 48, KNOT_DEV), f32)],
     )

time: 32.5 us -> 32.2 us (level)
  waiting for transfers between devices: 15.1 us -> 12.5 us
  starting transfers between devices: 9.89 us -> 12.2 us
    ppermute x8, waiting for transfers between devices: 15.1 us -> 12.5 us  [swapped(): return lax.ppermute(value, axis, [(i, i ^ bit) for i in range(size)])]
    ppermute x8, starting transfers between devices: 9.89 us -> 12.2 us  [swapped(): return lax.ppermute(value, axis, [(i, i ^ bit) for i in range(size)])]
where the time goes in v7:
time: 32.2 us; the launch traced here: 32 us
  waiting for transfers between devices  12.5 us (39%)
  starting transfers between devices  12.2 us (38%)
  Pallas kernels  6.44 us (20%)
  between operations  0.72 us (2%)
    ppermute x8, waiting for transfers between devices, swapped(): return lax.ppermute(value, axis, [(i, i ^ bit) for i in range(size)])  12.5 us
    ppermute x8, starting transfers between devices, swapped(): return lax.ppermute(value, axis, [(i, i ^ bit) for i in range(size)])  12.2 us
    pallas_call x6, Pallas kernels, call(): pl.pallas_call(kernel, name=name, out_shape=outs, in_specs=[SMEM] * len(s...  6.44 us
  transfers between devices with their start and end apart: 8, of which 7 were waited for; matrix products, arithmetic and copies ran while one was open for 0% of the time, Pallas kernels for 4%

profile of v7, /device:TPU:0, one launch (start us, length us, event | category | flops | bytes accessed | tf_op | source)
XLA Modules:
  0.0 32.0 jit_solution(7918938280346537220)
XLA Ops:
  0.6 2.8 %source_sums.1 = (f32[20,8,128]{2,1,0:T(8,128)S(1)}, f32[64,128]{1,0:T(8,128)S(1)}, f32[64,128]{1,0:T(8,128)S(1)}, s32[64,128]{1,0:T(8,128)S(1)}, f32[64,128]{1,...) custom-call(s32[1,1,16]{2,1,0:T(1,128)} %counts_hbm.1, ...), custom_call_target="tpu_custom_call" | custom-call | tf_op jit(solution)/shard_map/source_sums/pallas_call | solution.py:549
  3.5 0.6 %collective-permute-start = (f32[20,8,128]{2,1,0:T(8,128)S(1)}, f32[20,8,128]{2,1,0:T(8,128)S(1)}, u32[]{:S(2)}, u32[]{:S(2)}) collective-permute-start(f32[20,8,128]{2,1,0:T(8,128)S(1)} %get-tuple-element.17.mine_ref), channel_id=1, source_target_pairs={{0,1},{1,0},{2,3},{3,2},{4,5},{5,4},{6,7},{7,6},{8,9},{9,8},{10,11... | collective-permute-start | bytes 245768 | tf_op jit(solution)/shard_map/ppermute | solution.py:562
  4.0 1.1 %band_sums.1.band_ref = f32[384,128]{1,0:T(8,128)S(1)} custom-call(f32[64,128]{1,0:T(8,128)S(1)} %get-tuple-element.18.phase_ref, f32[3,8192]{1,0:T(4,128)S(1)} %get-tuple-element.19.axis_ref, f32[64,128]{1,0:T(8,128)S(1)} %get-tuple-element.20.weight_ref, s32[64,128]{1,0:T(8,128)S(1)} %get-tuple-element.21.knot_ref), custom_call_target="tpu_custom_call" | custom-call | tf_op jit(solution)/shard_map/band_sums/pallas_call | solution.py:549
  5.1 0.0 collective-permute-done.other_ref
  5.1 1.2 %residuals.1 = (f32[5,1024]{1,0:T(8,128)}, f32[64,128]{1,0:T(8,128)S(1)}, f32[4,112,128]{2,1,0:T(8,128)S(1)}) custom-call(f32[20,8,128]{2,1,0:T(8,128)S(1)} %get-tuple-element.17.mine_ref, f32[20,8,128]{2,1,0:T(8,128)S(1)} %collective-permute-done.other_ref, f32[384,128]{1,0:T(8,128)S(1)} %band_sums.1.band_ref, f32[64,128]{1,0:T(8,128)S(1)} %get-tuple-element.22.live_ref, ...), custom_call_target="tpu_custom_call" | custom-call | tf_op jit(solution)/shard_map/residuals/pallas_call | solution.py:549
  6.4 0.2 collective-permute-start.1
  6.7 1.1 %collective-permute-done.1 = f32[2,112,128]{2,1,0:T(8,128)S(1)} collective-permute-done((f32[2,112,128]{2,1,0:T(8,128)S(1)}, f32[2,112,128]{2,1,0:T(8,128)S(1)}, u32[]{:S(2)}, u32[]{:S(2)}) %collective-permute-start.1) | collective-permute-done | bytes 114720 | tf_op jit(solution)/shard_map/ppermute | solution.py:562
  7.8 2.7 %collective-permute-start.2 = (f32[1,112,128]{2,1,0:T(8,128)S(1)}, f32[1,112,128]{2,1,0:T(8,128)S(1)}, u32[]{:S(2)}, u32[]{:S(2)}) collective-permute-start(f32[1,112,128]{2,1,0:T(8,128)S(1)} %constant_dynamic-slice_fusion), channel_id=1, source_target_pairs={{0,3},{1,2},{2,1},{3,0},{4,7},{5,6},{6,5},{7,4},{8,11},{9,10},{10,... | collective-permute-start | bytes 172040 | tf_op jit(solution)/shard_map/ppermute | solution.py:562
  10.5 2.1 %collective-permute-done.2 = f32[1,112,128]{2,1,0:T(8,128)S(1)} collective-permute-done((f32[1,112,128]{2,1,0:T(8,128)S(1)}, f32[1,112,128]{2,1,0:T(8,128)S(1)}, u32[]{:S(2)}, u32[]{:S(2)}) %collective-permute-start.2) | collective-permute-done | bytes 57376 | tf_op jit(solution)/shard_map/ppermute | solution.py:562
  12.6 1.7 %collective-permute-start.3 = (f32[112,128]{1,0:T(8,128)S(1)}, f32[112,128]{1,0:T(8,128)S(1)}, u32[]{:S(2)}, u32[]{:S(2)}) collective-permute-start(f32[112,128]{1,0:T(8,128)S(1)} %add_bitcast_fusion), channel_id=1, source_target_pairs={{0,5},{1,4},{2,7},{3,6},{4,1},{5,0},{6,3},{7,2},{8,13},{9,12},{10,... | collective-permute-start | bytes 172040 | tf_op jit(solution)/shard_map/ppermute | solution.py:562
  14.3 2.3 %collective-permute-done.3 = f32[112,128]{1,0:T(8,128)S(1)} collective-permute-done((f32[112,128]{1,0:T(8,128)S(1)}, f32[112,128]{1,0:T(8,128)S(1)}, u32[]{:S(2)}, u32[]{:S(2)}) %collective-permute-start.3) | collective-permute-done | bytes 57376 | tf_op jit(solution)/shard_map/ppermute | solution.py:562
  16.6 1.6 %collective-permute-start.4 = (f32[112,128]{1,0:T(8,128)S(1)}, f32[112,128]{1,0:T(8,128)S(1)}, u32[]{:S(2)}, u32[]{:S(2)}) collective-permute-start(f32[112,128]{1,0:T(8,128)S(1)} %add.37), channel_id=1, source_target_pairs={{0,9},{1,8},{2,11},{3,10},{4,13},{5,12},{6,15},{7,14},{8,1},{9,0},... | collective-permute-start | bytes 172040 | tf_op jit(solution)/shard_map/ppermute | solution.py:562
  18.1 2.4 %collective-permute-done.4 = f32[112,128]{1,0:T(8,128)S(1)} collective-permute-done((f32[112,128]{1,0:T(8,128)S(1)}, f32[112,128]{1,0:T(8,128)S(1)}, u32[]{:S(2)}, u32[]{:S(2)}) %collective-permute-start.4) | collective-permute-done | bytes 57376 | tf_op jit(solution)/shard_map/ppermute | solution.py:562
  20.5 2.4 %collective-permute-start.5 = (f32[112,128]{1,0:T(8,128)S(1)}, f32[112,128]{1,0:T(8,128)S(1)}, u32[]{:S(2)}, u32[]{:S(2)}) collective-permute-start(f32[112,128]{1,0:T(8,128)S(1)} %add.38), channel_id=1, source_target_pairs={{0,17},{1,16},{2,19},{3,18},{4,21},{5,20},{6,23},{7,22},{8,25},{9,... | collective-permute-start | bytes 172040 | tf_op jit(solution)/shard_map/ppermute | solution.py:562
  22.9 2.4 %collective-permute-done.5 = f32[112,128]{1,0:T(8,128)S(1)} collective-permute-done((f32[112,128]{1,0:T(8,128)S(1)}, f32[112,128]{1,0:T(8,128)S(1)}, u32[]{:S(2)}, u32[]{:S(2)}) %collective-permute-start.5) | collective-permute-done | bytes 57376 | tf_op jit(solution)/shard_map/ppermute | solution.py:562
  25.4 0.3 attitude.1
  25.7 2.3 %collective-permute-start.6 = (f32[16,128]{1,0:T(8,128)S(1)}, f32[16,128]{1,0:T(8,128)S(1)}, u32[]{:S(2)}, u32[]{:S(2)}) collective-permute-start(f32[16,128]{1,0:T(8,128)S(1)} %attitude.1), channel_id=1, source_target_pairs={{0,3},{1,2},{2,1},{3,0},{4,7},{5,6},{6,5},{7,4},{8,11},{9,10},{10,... | collective-permute-start | bytes 24584 | tf_op jit(solution)/shard_map/ppermute | solution.py:562
  28.0 1.4 %collective-permute-done.6 = f32[16,128]{1,0:T(8,128)S(1)} collective-permute-done((f32[16,128]{1,0:T(8,128)S(1)}, f32[16,128]{1,0:T(8,128)S(1)}, u32[]{:S(2)}, u32[]{:S(2)}) %collective-permute-start.6) | collective-permute-done | bytes 8224 | tf_op jit(solution)/shard_map/ppermute | solution.py:562
  29.4 0.8 %collective-permute-start.7 = (f32[32,128]{1,0:T(8,128)S(1)}, f32[32,128]{1,0:T(8,128)S(1)}, u32[]{:S(2)}, u32[]{:S(2)}) collective-permute-start(f32[32,128]{1,0:T(8,128)S(1)} %pad_maximum_fusion.1), channel_id=1, source_target_pairs={{0,1},{1,0},{2,3},{3,2},{4,5},{5,4},{6,7},{7,6},{8,9},{9,8},{10,11... | collective-permute-start | bytes 49160 | tf_op jit(solution)/shard_map/ppermute | solution.py:562
  30.2 0.1 prepare.1.factor_ref
  30.3 0.8 %collective-permute-done.7 = f32[32,128]{1,0:T(8,128)S(1)} collective-permute-done((f32[32,128]{1,0:T(8,128)S(1)}, f32[32,128]{1,0:T(8,128)S(1)}, u32[]{:S(2)}, u32[]{:S(2)}) %collective-permute-start.7) | collective-permute-done | bytes 16416 | tf_op jit(solution)/shard_map/ppermute | solution.py:562
  31.1 0.9 %predict.1 = (f32[3,128]{1,0:T(4,128)}, f32[64,128]{1,0:T(8,128)}) custom-call(f32[16,4,128]{2,1,0:T(4,128)S(1)} %bitcast.16, f32[12,64,128]{2,1,0:T(8,128)S(1)} %prepare.1.factor_ref, f32[64,128]{1,0:T(8,128)S(1)} %get-tuple-element.28.resid_ref, s32[64,128]{1,0:T(8,128)S(1)} %get-tuple-element.21.knot_ref), custom_call_target="tpu_custom_call" | custom-call | tf_op jit(solution)/shard_map/predict/pallas_call | solution.py:549
  (11 shorter events, 0.1 us)
Async XLA Ops:
  3.5 1.7 %collective-permute-start = (f32[20,8,128]{2,1,0:T(8,128)S(1)}, f32[20,8,128]{2,1,0:T(8,128)S(1)}, u32[]{:S(2)}, u32[]{:S(2)}) collective-permute-start(f32[20,8,128]{2,1,0:T(8,128)S(1)} %get-tuple-element.17.mine_ref), channel_id=1, source_target_pairs={{0,1},{1,0},{2,3},{3,2},{4,5},{5,4},{6,7},{7,6},{8,9},{9,8},{10,11... | collective-permute-start | bytes 245768 | tf_op jit(solution)/shard_map/ppermute | solution.py:562
  6.4 1.4 %collective-permute-start.1 = (f32[2,112,128]{2,1,0:T(8,128)S(1)}, f32[2,112,128]{2,1,0:T(8,128)S(1)}, u32[]{:S(2)}, u32[]{:S(2)}) collective-permute-start(f32[2,112,128]{2,1,0:T(8,128)S(1)} %dynamic-slice_bitcast_fusion), channel_id=1, source_target_pairs={{0,1},{1,0},{2,3},{3,2},{4,5},{5,4},{6,7},{7,6},{8,9},{9,8},{10,11... | collective-permute-start | bytes 344072 | tf_op jit(solution)/shard_map/ppermute | solution.py:562
  7.8 4.8 %collective-permute-start.2 = (f32[1,112,128]{2,1,0:T(8,128)S(1)}, f32[1,112,128]{2,1,0:T(8,128)S(1)}, u32[]{:S(2)}, u32[]{:S(2)}) collective-permute-start(f32[1,112,128]{2,1,0:T(8,128)S(1)} %constant_dynamic-slice_fusion), channel_id=1, source_target_pairs={{0,3},{1,2},{2,1},{3,0},{4,7},{5,6},{6,5},{7,4},{8,11},{9,10},{10,... | collective-permute-start | bytes 172040 | tf_op jit(solution)/shard_map/ppermute | solution.py:562
  12.6 3.9 %collective-permute-start.3 = (f32[112,128]{1,0:T(8,128)S(1)}, f32[112,128]{1,0:T(8,128)S(1)}, u32[]{:S(2)}, u32[]{:S(2)}) collective-permute-start(f32[112,128]{1,0:T(8,128)S(1)} %add_bitcast_fusion), channel_id=1, source_target_pairs={{0,5},{1,4},{2,7},{3,6},{4,1},{5,0},{6,3},{7,2},{8,13},{9,12},{10,... | collective-permute-start | bytes 172040 | tf_op jit(solution)/shard_map/ppermute | solution.py:562
  16.6 3.9 %collective-permute-start.4 = (f32[112,128]{1,0:T(8,128)S(1)}, f32[112,128]{1,0:T(8,128)S(1)}, u32[]{:S(2)}, u32[]{:S(2)}) collective-permute-start(f32[112,128]{1,0:T(8,128)S(1)} %add.37), channel_id=1, source_target_pairs={{0,9},{1,8},{2,11},{3,10},{4,13},{5,12},{6,15},{7,14},{8,1},{9,0},... | collective-permute-start | bytes 172040 | tf_op jit(solution)/shard_map/ppermute | solution.py:562
  20.5 4.8 %collective-permute-start.5 = (f32[112,128]{1,0:T(8,128)S(1)}, f32[112,128]{1,0:T(8,128)S(1)}, u32[]{:S(2)}, u32[]{:S(2)}) collective-permute-start(f32[112,128]{1,0:T(8,128)S(1)} %add.38), channel_id=1, source_target_pairs={{0,17},{1,16},{2,19},{3,18},{4,21},{5,20},{6,23},{7,22},{8,25},{9,... | collective-permute-start | bytes 172040 | tf_op jit(solution)/shard_map/ppermute | solution.py:562
  25.7 3.7 %collective-permute-start.6 = (f32[16,128]{1,0:T(8,128)S(1)}, f32[16,128]{1,0:T(8,128)S(1)}, u32[]{:S(2)}, u32[]{:S(2)}) collective-permute-start(f32[16,128]{1,0:T(8,128)S(1)} %attitude.1), channel_id=1, source_target_pairs={{0,3},{1,2},{2,1},{3,0},{4,7},{5,6},{6,5},{7,4},{8,11},{9,10},{10,... | collective-permute-start | bytes 24584 | tf_op jit(solution)/shard_map/ppermute | solution.py:562
  29.4 1.7 %collective-permute-start.7 = (f32[32,128]{1,0:T(8,128)S(1)}, f32[32,128]{1,0:T(8,128)S(1)}, u32[]{:S(2)}, u32[]{:S(2)}) collective-permute-start(f32[32,128]{1,0:T(8,128)S(1)} %pad_maximum_fusion.1), channel_id=1, source_target_pairs={{0,1},{1,0},{2,3},{3,2},{4,5},{5,4},{6,7},{7,6},{8,9},{9,8},{10,11... | collective-permute-start | bytes 49160 | tf_op jit(solution)/shard_map/ppermute | solution.py:562

commit v8 on v7

--- a/solution.py
+++ b/solution.py
@@ -641,10 +641,10 @@
     if fast:
         upper, lower = part_bits()
         sums = halved(halved(message, 1, upper), 3, lower)[0]
-        bit = 2
-        while bit < shards:
+        bit = shards // 2
+        while bit > 1:
             sums = sums + swapped(sums, BOTH, 2 * bit + 1)
-            bit *= 2
+            bit //= 2
     else:
         sums = summed_over(summed_over(message[0], "ccd"), "src")
     coefs = call(

time: 32.2 us -> 31.7 us (0.984)
  waiting for transfers between devices: 12.5 us -> 11.5 us
  starting transfers between devices: 12.2 us -> 12.8 us
    ppermute x8, waiting for transfers between devices: 12.5 us -> 11.5 us  [swapped(): return lax.ppermute(value, axis, [(i, i ^ bit) for i in range(size)])]
    ppermute x8, starting transfers between devices: 12.2 us -> 12.8 us  [swapped(): return lax.ppermute(value, axis, [(i, i ^ bit) for i in range(size)])]
where the time goes in v8:
time: 31.7 us; the launch traced here: 31.5 us
  starting transfers between devices  12.8 us (40%)
  waiting for transfers between devices  11.5 us (36%)
  Pallas kernels  6.44 us (20%)
  between operations  0.71 us (2%)
    ppermute x8, starting transfers between devices, swapped(): return lax.ppermute(value, axis, [(i, i ^ bit) for i in range(size)])  12.8 us
    ppermute x8, waiting for transfers between devices, swapped(): return lax.ppermute(value, axis, [(i, i ^ bit) for i in range(size)])  11.5 us
    pallas_call x6, Pallas kernels, call(): pl.pallas_call(kernel, name=name, out_shape=outs, in_specs=[SMEM] * len(s...  6.44 us
  transfers between devices with their start and end apart: 8, of which 7 were waited for; matrix products, arithmetic and copies ran while one was open for 0% of the time, Pallas kernels for 4%

profile of v8, /device:TPU:0, one launch (start us, length us, event | category | flops | bytes accessed | tf_op | source)
XLA Modules:
  0.0 31.5 jit_solution(1247097245968508929)
XLA Ops:
  0.6 2.8 %source_sums.1 = (f32[20,8,128]{2,1,0:T(8,128)S(1)}, f32[64,128]{1,0:T(8,128)S(1)}, f32[64,128]{1,0:T(8,128)S(1)}, s32[64,128]{1,0:T(8,128)S(1)}, f32[64,128]{1,...) custom-call(s32[1,1,16]{2,1,0:T(1,128)} %counts_hbm.1, ...), custom_call_target="tpu_custom_call" | custom-call | tf_op jit(solution)/shard_map/source_sums/pallas_call | solution.py:549
  3.5 0.6 %collective-permute-start = (f32[20,8,128]{2,1,0:T(8,128)S(1)}, f32[20,8,128]{2,1,0:T(8,128)S(1)}, u32[]{:S(2)}, u32[]{:S(2)}) collective-permute-start(f32[20,8,128]{2,1,0:T(8,128)S(1)} %get-tuple-element.17.mine_ref), channel_id=1, source_target_pairs={{0,1},{1,0},{2,3},{3,2},{4,5},{5,4},{6,7},{7,6},{8,9},{9,8},{10,11... | collective-permute-start | bytes 245768 | tf_op jit(solution)/shard_map/ppermute | solution.py:562
  4.0 1.1 %band_sums.1.band_ref = f32[384,128]{1,0:T(8,128)S(1)} custom-call(f32[64,128]{1,0:T(8,128)S(1)} %get-tuple-element.18.phase_ref, f32[3,8192]{1,0:T(4,128)S(1)} %get-tuple-element.19.axis_ref, f32[64,128]{1,0:T(8,128)S(1)} %get-tuple-element.20.weight_ref, s32[64,128]{1,0:T(8,128)S(1)} %get-tuple-element.21.knot_ref), custom_call_target="tpu_custom_call" | custom-call | tf_op jit(solution)/shard_map/band_sums/pallas_call | solution.py:549
  5.1 0.0 collective-permute-done.other_ref
  5.1 1.2 %residuals.1 = (f32[5,1024]{1,0:T(8,128)}, f32[64,128]{1,0:T(8,128)S(1)}, f32[4,112,128]{2,1,0:T(8,128)S(1)}) custom-call(f32[20,8,128]{2,1,0:T(8,128)S(1)} %get-tuple-element.17.mine_ref, f32[20,8,128]{2,1,0:T(8,128)S(1)} %collective-permute-done.other_ref, f32[384,128]{1,0:T(8,128)S(1)} %band_sums.1.band_ref, f32[64,128]{1,0:T(8,128)S(1)} %get-tuple-element.22.live_ref, ...), custom_call_target="tpu_custom_call" | custom-call | tf_op jit(solution)/shard_map/residuals/pallas_call | solution.py:549
  6.4 0.2 collective-permute-start.1
  6.7 1.1 %collective-permute-done.1 = f32[2,112,128]{2,1,0:T(8,128)S(1)} collective-permute-done((f32[2,112,128]{2,1,0:T(8,128)S(1)}, f32[2,112,128]{2,1,0:T(8,128)S(1)}, u32[]{:S(2)}, u32[]{:S(2)}) %collective-permute-start.1) | collective-permute-done | bytes 114720 | tf_op jit(solution)/shard_map/ppermute | solution.py:562
  7.8 2.7 %collective-permute-start.2 = (f32[1,112,128]{2,1,0:T(8,128)S(1)}, f32[1,112,128]{2,1,0:T(8,128)S(1)}, u32[]{:S(2)}, u32[]{:S(2)}) collective-permute-start(f32[1,112,128]{2,1,0:T(8,128)S(1)} %constant_dynamic-slice_fusion), channel_id=1, source_target_pairs={{0,3},{1,2},{2,1},{3,0},{4,7},{5,6},{6,5},{7,4},{8,11},{9,10},{10,... | collective-permute-start | bytes 172040 | tf_op jit(solution)/shard_map/ppermute | solution.py:562
  10.5 2.1 %collective-permute-done.2 = f32[1,112,128]{2,1,0:T(8,128)S(1)} collective-permute-done((f32[1,112,128]{2,1,0:T(8,128)S(1)}, f32[1,112,128]{2,1,0:T(8,128)S(1)}, u32[]{:S(2)}, u32[]{:S(2)}) %collective-permute-start.2) | collective-permute-done | bytes 57376 | tf_op jit(solution)/shard_map/ppermute | solution.py:562
  12.6 2.7 %collective-permute-start.3 = (f32[112,128]{1,0:T(8,128)S(1)}, f32[112,128]{1,0:T(8,128)S(1)}, u32[]{:S(2)}, u32[]{:S(2)}) collective-permute-start(f32[112,128]{1,0:T(8,128)S(1)} %add_bitcast_fusion), channel_id=1, source_target_pairs={{0,17},{1,16},{2,19},{3,18},{4,21},{5,20},{6,23},{7,22},{8,25},{9,... | collective-permute-start | bytes 172040 | tf_op jit(solution)/shard_map/ppermute | solution.py:562
  15.4 2.1 %collective-permute-done.3 = f32[112,128]{1,0:T(8,128)S(1)} collective-permute-done((f32[112,128]{1,0:T(8,128)S(1)}, f32[112,128]{1,0:T(8,128)S(1)}, u32[]{:S(2)}, u32[]{:S(2)}) %collective-permute-start.3) | collective-permute-done | bytes 57376 | tf_op jit(solution)/shard_map/ppermute | solution.py:562
  17.5 2.0 %collective-permute-start.4 = (f32[112,128]{1,0:T(8,128)S(1)}, f32[112,128]{1,0:T(8,128)S(1)}, u32[]{:S(2)}, u32[]{:S(2)}) collective-permute-start(f32[112,128]{1,0:T(8,128)S(1)} %add.37), channel_id=1, source_target_pairs={{0,9},{1,8},{2,11},{3,10},{4,13},{5,12},{6,15},{7,14},{8,1},{9,0},... | collective-permute-start | bytes 172040 | tf_op jit(solution)/shard_map/ppermute | solution.py:562
  19.5 2.1 %collective-permute-done.4 = f32[112,128]{1,0:T(8,128)S(1)} collective-permute-done((f32[112,128]{1,0:T(8,128)S(1)}, f32[112,128]{1,0:T(8,128)S(1)}, u32[]{:S(2)}, u32[]{:S(2)}) %collective-permute-start.4) | collective-permute-done | bytes 57376 | tf_op jit(solution)/shard_map/ppermute | solution.py:562
  21.6 2.3 %collective-permute-start.5 = (f32[112,128]{1,0:T(8,128)S(1)}, f32[112,128]{1,0:T(8,128)S(1)}, u32[]{:S(2)}, u32[]{:S(2)}) collective-permute-start(f32[112,128]{1,0:T(8,128)S(1)} %add.38), channel_id=1, source_target_pairs={{0,5},{1,4},{2,7},{3,6},{4,1},{5,0},{6,3},{7,2},{8,13},{9,12},{10,... | collective-permute-start | bytes 172040 | tf_op jit(solution)/shard_map/ppermute | solution.py:562
  23.9 1.9 %collective-permute-done.5 = f32[112,128]{1,0:T(8,128)S(1)} collective-permute-done((f32[112,128]{1,0:T(8,128)S(1)}, f32[112,128]{1,0:T(8,128)S(1)}, u32[]{:S(2)}, u32[]{:S(2)}) %collective-permute-start.5) | collective-permute-done | bytes 57376 | tf_op jit(solution)/shard_map/ppermute | solution.py:562
  25.8 0.3 attitude.1
  26.0 1.8 %collective-permute-start.6 = (f32[16,128]{1,0:T(8,128)S(1)}, f32[16,128]{1,0:T(8,128)S(1)}, u32[]{:S(2)}, u32[]{:S(2)}) collective-permute-start(f32[16,128]{1,0:T(8,128)S(1)} %attitude.1), channel_id=1, source_target_pairs={{0,3},{1,2},{2,1},{3,0},{4,7},{5,6},{6,5},{7,4},{8,11},{9,10},{10,... | collective-permute-start | bytes 24584 | tf_op jit(solution)/shard_map/ppermute | solution.py:562
  27.8 1.4 %collective-permute-done.6 = f32[16,128]{1,0:T(8,128)S(1)} collective-permute-done((f32[16,128]{1,0:T(8,128)S(1)}, f32[16,128]{1,0:T(8,128)S(1)}, u32[]{:S(2)}, u32[]{:S(2)}) %collective-permute-start.6) | collective-permute-done | bytes 8224 | tf_op jit(solution)/shard_map/ppermute | solution.py:562
  29.2 0.5 %collective-permute-start.7 = (f32[32,128]{1,0:T(8,128)S(1)}, f32[32,128]{1,0:T(8,128)S(1)}, u32[]{:S(2)}, u32[]{:S(2)}) collective-permute-start(f32[32,128]{1,0:T(8,128)S(1)} %pad_maximum_fusion.1), channel_id=1, source_target_pairs={{0,1},{1,0},{2,3},{3,2},{4,5},{5,4},{6,7},{7,6},{8,9},{9,8},{10,11... | collective-permute-start | bytes 49160 | tf_op jit(solution)/shard_map/ppermute | solution.py:562
  29.7 0.1 prepare.1.factor_ref
  29.8 0.8 %collective-permute-done.7 = f32[32,128]{1,0:T(8,128)S(1)} collective-permute-done((f32[32,128]{1,0:T(8,128)S(1)}, f32[32,128]{1,0:T(8,128)S(1)}, u32[]{:S(2)}, u32[]{:S(2)}) %collective-permute-start.7) | collective-permute-done | bytes 16416 | tf_op jit(solution)/shard_map/ppermute | solution.py:562
  30.6 0.9 %predict.1 = (f32[3,128]{1,0:T(4,128)}, f32[64,128]{1,0:T(8,128)}) custom-call(f32[16,4,128]{2,1,0:T(4,128)S(1)} %bitcast.16, f32[12,64,128]{2,1,0:T(8,128)S(1)} %prepare.1.factor_ref, f32[64,128]{1,0:T(8,128)S(1)} %get-tuple-element.28.resid_ref, s32[64,128]{1,0:T(8,128)S(1)} %get-tuple-element.21.knot_ref), custom_call_target="tpu_custom_call" | custom-call | tf_op jit(solution)/shard_map/predict/pallas_call | solution.py:549
  (11 shorter events, 0.1 us)
Async XLA Ops:
  3.5 1.7 %collective-permute-start = (f32[20,8,128]{2,1,0:T(8,128)S(1)}, f32[20,8,128]{2,1,0:T(8,128)S(1)}, u32[]{:S(2)}, u32[]{:S(2)}) collective-permute-start(f32[20,8,128]{2,1,0:T(8,128)S(1)} %get-tuple-element.17.mine_ref), channel_id=1, source_target_pairs={{0,1},{1,0},{2,3},{3,2},{4,5},{5,4},{6,7},{7,6},{8,9},{9,8},{10,11... | collective-permute-start | bytes 245768 | tf_op jit(solution)/shard_map/ppermute | solution.py:562
  6.4 1.4 %collective-permute-start.1 = (f32[2,112,128]{2,1,0:T(8,128)S(1)}, f32[2,112,128]{2,1,0:T(8,128)S(1)}, u32[]{:S(2)}, u32[]{:S(2)}) collective-permute-start(f32[2,112,128]{2,1,0:T(8,128)S(1)} %dynamic-slice_bitcast_fusion), channel_id=1, source_target_pairs={{0,1},{1,0},{2,3},{3,2},{4,5},{5,4},{6,7},{7,6},{8,9},{9,8},{10,11... | collective-permute-start | bytes 344072 | tf_op jit(solution)/shard_map/ppermute | solution.py:562
  7.8 4.8 %collective-permute-start.2 = (f32[1,112,128]{2,1,0:T(8,128)S(1)}, f32[1,112,128]{2,1,0:T(8,128)S(1)}, u32[]{:S(2)}, u32[]{:S(2)}) collective-permute-start(f32[1,112,128]{2,1,0:T(8,128)S(1)} %constant_dynamic-slice_fusion), channel_id=1, source_target_pairs={{0,3},{1,2},{2,1},{3,0},{4,7},{5,6},{6,5},{7,4},{8,11},{9,10},{10,... | collective-permute-start | bytes 172040 | tf_op jit(solution)/shard_map/ppermute | solution.py:562
  12.6 4.9 %collective-permute-start.3 = (f32[112,128]{1,0:T(8,128)S(1)}, f32[112,128]{1,0:T(8,128)S(1)}, u32[]{:S(2)}, u32[]{:S(2)}) collective-permute-start(f32[112,128]{1,0:T(8,128)S(1)} %add_bitcast_fusion), channel_id=1, source_target_pairs={{0,17},{1,16},{2,19},{3,18},{4,21},{5,20},{6,23},{7,22},{8,25},{9,... | collective-permute-start | bytes 172040 | tf_op jit(solution)/shard_map/ppermute | solution.py:562
  17.5 4.1 %collective-permute-start.4 = (f32[112,128]{1,0:T(8,128)S(1)}, f32[112,128]{1,0:T(8,128)S(1)}, u32[]{:S(2)}, u32[]{:S(2)}) collective-permute-start(f32[112,128]{1,0:T(8,128)S(1)} %add.37), channel_id=1, source_target_pairs={{0,9},{1,8},{2,11},{3,10},{4,13},{5,12},{6,15},{7,14},{8,1},{9,0},... | collective-permute-start | bytes 172040 | tf_op jit(solution)/shard_map/ppermute | solution.py:562
  21.6 4.1 %collective-permute-start.5 = (f32[112,128]{1,0:T(8,128)S(1)}, f32[112,128]{1,0:T(8,128)S(1)}, u32[]{:S(2)}, u32[]{:S(2)}) collective-permute-start(f32[112,128]{1,0:T(8,128)S(1)} %add.38), channel_id=1, source_target_pairs={{0,5},{1,4},{2,7},{3,6},{4,1},{5,0},{6,3},{7,2},{8,13},{9,12},{10,... | collective-permute-start | bytes 172040 | tf_op jit(solution)/shard_map/ppermute | solution.py:562
  26.0 3.1 %collective-permute-start.6 = (f32[16,128]{1,0:T(8,128)S(1)}, f32[16,128]{1,0:T(8,128)S(1)}, u32[]{:S(2)}, u32[]{:S(2)}) collective-permute-start(f32[16,128]{1,0:T(8,128)S(1)} %attitude.1), channel_id=1, source_target_pairs={{0,3},{1,2},{2,1},{3,0},{4,7},{5,6},{6,5},{7,4},{8,11},{9,10},{10,... | collective-permute-start | bytes 24584 | tf_op jit(solution)/shard_map/ppermute | solution.py:562
  29.2 1.4 %collective-permute-start.7 = (f32[32,128]{1,0:T(8,128)S(1)}, f32[32,128]{1,0:T(8,128)S(1)}, u32[]{:S(2)}, u32[]{:S(2)}) collective-permute-start(f32[32,128]{1,0:T(8,128)S(1)} %pad_maximum_fusion.1), channel_id=1, source_target_pairs={{0,1},{1,0},{2,3},{3,2},{4,5},{5,4},{6,7},{7,6},{8,9},{9,8},{10,11... | collective-permute-start | bytes 49160 | tf_op jit(solution)/shard_map/ppermute | solution.py:562

commit v9 on v8

--- a/solution.py
+++ b/solution.py
@@ -42,8 +42,8 @@
 
 
 def split2(value):
-    high = value.astype(bf16).astype(f32)
-    return [high, value - high]
+    high = value.astype(bf16)
+    return [high, (value - high.astype(f32)).astype(bf16)]
 
 
 def split3(value):
@@ -173,6 +173,8 @@
 
 def stacked_parts(values, split):
     parts = split(jnp.concatenate(values, 0))
+    if split is split2:
+        return jnp.concatenate(parts, 0)
     if len(parts) * parts[0].shape[0] % (2 * SUB):
         parts.append(jnp.zeros((SUB, LANES), f32))
     return jnp.concatenate(parts, 0).astype(bf16)
@@ -285,16 +287,17 @@
     for copy in copies[5:]:
         copy.wait()
     height = total.shape[0] // highs
-    wide, half_tile = 2 * SUB, SUB // 2
+    wide, half_tile, blocks = 2 * SUB, SUB // 2, SRC_DEV // LANES
     for h in range(highs):
-        block = total[h * height : (h + 1) * height, :]
-        tail = block[3 * wide :]
-        summed = sum_parts(block, wide, 3)
+        sums = total[h * height : (h + 1) * height, :]
+        tail = sums[3 * wide :]
+        summed = sum_parts(sums, wide, 3)
         rest = tail[0:half_tile] + tail[half_tile : 2 * half_tile] + tail[2 * half_tile : 3 * half_tile]
         for half in range(LOW // LANES):
             cols = slice(half * LANES, (half + 1) * LANES)
-            out_ref[0:wide, h * (LOW // LANES) + half, :] = summed[:, cols]
-            out_ref[wide:SIGNALS, h * (LOW // LANES) + half, :] = rest[:, cols]
+            block = h * (LOW // LANES) + half
+            out_ref[pl.ds(block, wide, stride=blocks), :] = summed[:, cols]
+            out_ref[pl.ds(wide * blocks + block, SIGNALS - wide, stride=blocks), :] = rest[:, cols]
 
 
 def band_kernel(phase_ref, axis_ref, weight_ref, knot_ref, out_ref, tiled, powers_ref, moments):
@@ -305,7 +308,7 @@
     lefts_of = patterns([PAIRS[q % 6][0] for q in range(24)])
     rights_of = patterns([PAIRS[q % 6][1] for q in range(24)])
     powers_of = patterns([q // 6 if q < 42 else 0 for q in range(rows)])
-    for start in by_group(tiles):
+    def dense(start):
         at = pl.ds(start, SUB)
         u = phase_ref[at, :]
         r = 1.0 - u
@@ -324,9 +327,11 @@
         return stacked_parts([products[i % 3] * pick_rows(powers, p) for i, p in enumerate(powers_of)], split2)
 
     def group(start, steps):
-        add_blocks(moments, start, steps, rep, rows, 2, left_of, knot_ref)
-
-    if rep > math.gcd(tiles, 64):
+        for part in range(steps // SUB):
+            dense(start + part * SUB)
+            add_blocks(moments, start + part * SUB, SUB, rep, rows, 2, left_of, knot_ref)
+
+    if rep > SUB:
         moments[...] = jnp.zeros_like(moments)
     over_steps(tiles, group)
     table = bernstein_products()
@@ -386,8 +391,9 @@
     rep = tiles // shards
     by_tile(design_ref, tiled)
     by_tile(axis_ref, tiled_axis)
-    solved = solve_small([mine_ref[q] + other_ref[q] for q in range(SIGNALS)])
     blocks = SRC_DEV // LANES
+    at = [slice(q * blocks, (q + 1) * blocks) for q in range(SIGNALS)]
+    solved = solve_small([mine_ref[rows, :] + other_ref[rows, :] for rows in at])
     for m in range(5):
         solved_ref[m] = solved[m]
         for b in range(blocks):
@@ -419,9 +425,9 @@
             scaled = weight_ref[at, :] * resid
             for j, basis in enumerate(spline_basis(phase_ref[at, :])):
                 splines_ref[across(start + part * SUB, j), :] = basis * scaled
-        add_blocks(moments, start, steps, rep, rows, 3, left_of, knot_ref)
-
-    if rep > math.gcd(tiles, 64):
+            add_blocks(moments, start + part * SUB, SUB, rep, rows, 3, left_of, knot_ref)
+
+    if rep > SUB:
         moments[...] = jnp.zeros_like(moments)
     over_steps(tiles, group)
     for x in range(3):
@@ -513,10 +519,10 @@
 
 
 def predict_kernel(coef_ref, factor_ref, resid_ref, knot_ref, att_ref, out_ref, windows):
-    tiles, shards = resid_ref.shape[0], coef_ref.shape[0]
+    tiles, shards = resid_ref.shape[0], coef_ref.shape[0] // 4
     rep = tiles // shards
     for x in range(3):
-        coefs = coef_ref[:, x, :]
+        coefs = coef_ref[pl.ds(x, shards, stride=4), :]
         for j in range(4):
             windows[x * 4 + j] = coefs if j == 0 else shift_down(coefs, j)
         att_ref[x : x + 1, :] = windows[x * 4, pl.ds(lax.axis_index("src"), 1), :]
@@ -601,7 +607,7 @@
     moments, live, w, index, obs, design, phase, axis_factors, knots = call(
         source_kernel, "source_sums", [],
         [pltpu.with_memory_space_constraint(a, pltpu.HBM) for a in (counts,) + inputs],
-        (jax.ShapeDtypeStruct((SIGNALS, blocks, LANES), f32), jax.ShapeDtypeStruct((tiles, LANES), f32))
+        (jax.ShapeDtypeStruct((SIGNALS * blocks, LANES), f32), jax.ShapeDtypeStruct((tiles, LANES), f32))
         + tuple(jax.ShapeDtypeStruct(a.shape, a.dtype) for a in inputs),
         [
             pltpu.SMEM(counts.shape, jnp.int32), pltpu.SemaphoreType.DMA((8,)), dense, dense,
@@ -654,7 +660,7 @@
     if fast:
         coefs = doubled(doubled(coefs, 3, lower), 1, upper)
     attitude, residual = call(
-        predict_kernel, "predict", [], [coefs.reshape(shards, 4, LANES), factors, resid, knots],
+        predict_kernel, "predict", [], [coefs, factors, resid, knots],
         (jax.ShapeDtypeStruct((3, KNOT_DEV), f32), jax.ShapeDtypeStruct((tiles, LANES), f32)),
         [pltpu.VMEM((12, shards, KNOT_DEV), f32)],
     )

time: 31.7 us -> 31.6 us (level)
  no operation moved by 1% of the time
where the time goes in v9:
time: 31.6 us; the launch traced here: 31.5 us
  starting transfers between devices  12.8 us (41%)
  waiting for transfers between devices  11.5 us (36%)
  Pallas kernels  6.41 us (20%)
  between operations  0.72 us (2%)
    ppermute x8, starting transfers between devices, swapped(): return lax.ppermute(value, axis, [(i, i ^ bit) for i in range(size)])  12.8 us
    ppermute x8, waiting for transfers between devices, swapped(): return lax.ppermute(value, axis, [(i, i ^ bit) for i in range(size)])  11.5 us
    pallas_call x6, Pallas kernels, call(): pl.pallas_call(kernel, name=name, out_shape=outs, in_specs=[SMEM] * len(s...  6.41 us
  transfers between devices with their start and end apart: 8, of which 7 were waited for; matrix products, arithmetic and copies ran while one was open for 0% of the time, Pallas kernels for 4%

profile of v9, /device:TPU:0, one launch (start us, length us, event | category | flops | bytes accessed | tf_op | source)
XLA Modules:
  0.0 31.5 jit_solution(8354283418013303049)
XLA Ops:
  0.6 2.8 %source_sums.1 = (f32[160,128]{1,0:T(8,128)S(1)}, f32[64,128]{1,0:T(8,128)S(1)}, f32[64,128]{1,0:T(8,128)S(1)}, s32[64,128]{1,0:T(8,128)S(1)}, f32[64,128]{1,0:T...) custom-call(s32[1,1,16]{2,1,0:T(1,128)} %counts_hbm.1, ...), custom_call_target="tpu_custom_call" | custom-call | tf_op jit(solution)/shard_map/source_sums/pallas_call | solution.py:555
  3.4 0.6 %collective-permute-start = (f32[160,128]{1,0:T(8,128)S(1)}, f32[160,128]{1,0:T(8,128)S(1)}, u32[]{:S(2)}, u32[]{:S(2)}) collective-permute-start(f32[160,128]{1,0:T(8,128)S(1)} %get-tuple-element.17.mine_ref), channel_id=1, source_target_pairs={{0,1},{1,0},{2,3},{3,2},{4,5},{5,4},{6,7},{7,6},{8,9},{9,8},{10,11... | collective-permute-start | bytes 245768 | tf_op jit(solution)/shard_map/ppermute | solution.py:568
  4.0 1.1 %band_sums.1.band_ref = f32[384,128]{1,0:T(8,128)S(1)} custom-call(f32[64,128]{1,0:T(8,128)S(1)} %get-tuple-element.18.phase_ref, f32[3,8192]{1,0:T(4,128)S(1)} %get-tuple-element.19.axis_ref, f32[64,128]{1,0:T(8,128)S(1)} %get-tuple-element.20.weight_ref, s32[64,128]{1,0:T(8,128)S(1)} %get-tuple-element.21.knot_ref), custom_call_target="tpu_custom_call" | custom-call | tf_op jit(solution)/shard_map/band_sums/pallas_call | solution.py:555
  5.1 0.0 collective-permute-done.other_ref
  5.1 1.3 %residuals.1 = (f32[5,1024]{1,0:T(8,128)}, f32[64,128]{1,0:T(8,128)S(1)}, f32[4,112,128]{2,1,0:T(8,128)S(1)}) custom-call(f32[160,128]{1,0:T(8,128)S(1)} %get-tuple-element.17.mine_ref, f32[160,128]{1,0:T(8,128)S(1)} %collective-permute-done.other_ref, f32[384,128]{1,0:T(8,128)S(1)} %band_sums.1.band_ref, f32[64,128]{1,0:T(8,128)S(1)} %get-tuple-element.22.live_ref, ...), custom_call_target="tpu_custom_call" | custom-call | tf_op jit(solution)/shard_map/residuals/pallas_call | solution.py:555
  6.4 0.2 collective-permute-start.1
  6.6 1.2 %collective-permute-done.1 = f32[2,112,128]{2,1,0:T(8,128)S(1)} collective-permute-done((f32[2,112,128]{2,1,0:T(8,128)S(1)}, f32[2,112,128]{2,1,0:T(8,128)S(1)}, u32[]{:S(2)}, u32[]{:S(2)}) %collective-permute-start.1) | collective-permute-done | bytes 114720 | tf_op jit(solution)/shard_map/ppermute | solution.py:568
  7.8 2.6 %collective-permute-start.2 = (f32[1,112,128]{2,1,0:T(8,128)S(1)}, f32[1,112,128]{2,1,0:T(8,128)S(1)}, u32[]{:S(2)}, u32[]{:S(2)}) collective-permute-start(f32[1,112,128]{2,1,0:T(8,128)S(1)} %constant_dynamic-slice_fusion), channel_id=1, source_target_pairs={{0,3},{1,2},{2,1},{3,0},{4,7},{5,6},{6,5},{7,4},{8,11},{9,10},{10,... | collective-permute-start | bytes 172040 | tf_op jit(solution)/shard_map/ppermute | solution.py:568
  10.5 2.1 %collective-permute-done.2 = f32[1,112,128]{2,1,0:T(8,128)S(1)} collective-permute-done((f32[1,112,128]{2,1,0:T(8,128)S(1)}, f32[1,112,128]{2,1,0:T(8,128)S(1)}, u32[]{:S(2)}, u32[]{:S(2)}) %collective-permute-start.2) | collective-permute-done | bytes 57376 | tf_op jit(solution)/shard_map/ppermute | solution.py:568
  12.6 2.8 %collective-permute-start.3 = (f32[112,128]{1,0:T(8,128)S(1)}, f32[112,128]{1,0:T(8,128)S(1)}, u32[]{:S(2)}, u32[]{:S(2)}) collective-permute-start(f32[112,128]{1,0:T(8,128)S(1)} %add_bitcast_fusion), channel_id=1, source_target_pairs={{0,17},{1,16},{2,19},{3,18},{4,21},{5,20},{6,23},{7,22},{8,25},{9,... | collective-permute-start | bytes 172040 | tf_op jit(solution)/shard_map/ppermute | solution.py:568
  15.4 2.1 %collective-permute-done.3 = f32[112,128]{1,0:T(8,128)S(1)} collective-permute-done((f32[112,128]{1,0:T(8,128)S(1)}, f32[112,128]{1,0:T(8,128)S(1)}, u32[]{:S(2)}, u32[]{:S(2)}) %collective-permute-start.3) | collective-permute-done | bytes 57376 | tf_op jit(solution)/shard_map/ppermute | solution.py:568
  17.5 2.0 %collective-permute-start.4 = (f32[112,128]{1,0:T(8,128)S(1)}, f32[112,128]{1,0:T(8,128)S(1)}, u32[]{:S(2)}, u32[]{:S(2)}) collective-permute-start(f32[112,128]{1,0:T(8,128)S(1)} %add.37), channel_id=1, source_target_pairs={{0,9},{1,8},{2,11},{3,10},{4,13},{5,12},{6,15},{7,14},{8,1},{9,0},... | collective-permute-start | bytes 172040 | tf_op jit(solution)/shard_map/ppermute | solution.py:568
  19.5 2.1 %collective-permute-done.4 = f32[112,128]{1,0:T(8,128)S(1)} collective-permute-done((f32[112,128]{1,0:T(8,128)S(1)}, f32[112,128]{1,0:T(8,128)S(1)}, u32[]{:S(2)}, u32[]{:S(2)}) %collective-permute-start.4) | collective-permute-done | bytes 57376 | tf_op jit(solution)/shard_map/ppermute | solution.py:568
  21.6 2.3 %collective-permute-start.5 = (f32[112,128]{1,0:T(8,128)S(1)}, f32[112,128]{1,0:T(8,128)S(1)}, u32[]{:S(2)}, u32[]{:S(2)}) collective-permute-start(f32[112,128]{1,0:T(8,128)S(1)} %add.38), channel_id=1, source_target_pairs={{0,5},{1,4},{2,7},{3,6},{4,1},{5,0},{6,3},{7,2},{8,13},{9,12},{10,... | collective-permute-start | bytes 172040 | tf_op jit(solution)/shard_map/ppermute | solution.py:568
  23.9 1.9 %collective-permute-done.5 = f32[112,128]{1,0:T(8,128)S(1)} collective-permute-done((f32[112,128]{1,0:T(8,128)S(1)}, f32[112,128]{1,0:T(8,128)S(1)}, u32[]{:S(2)}, u32[]{:S(2)}) %collective-permute-start.5) | collective-permute-done | bytes 57376 | tf_op jit(solution)/shard_map/ppermute | solution.py:568
  25.7 0.3 attitude.1
  26.0 1.8 %collective-permute-start.6 = (f32[16,128]{1,0:T(8,128)S(1)}, f32[16,128]{1,0:T(8,128)S(1)}, u32[]{:S(2)}, u32[]{:S(2)}) collective-permute-start(f32[16,128]{1,0:T(8,128)S(1)} %attitude.1), channel_id=1, source_target_pairs={{0,3},{1,2},{2,1},{3,0},{4,7},{5,6},{6,5},{7,4},{8,11},{9,10},{10,... | collective-permute-start | bytes 24584 | tf_op jit(solution)/shard_map/ppermute | solution.py:568
  27.8 1.4 %collective-permute-done.6 = f32[16,128]{1,0:T(8,128)S(1)} collective-permute-done((f32[16,128]{1,0:T(8,128)S(1)}, f32[16,128]{1,0:T(8,128)S(1)}, u32[]{:S(2)}, u32[]{:S(2)}) %collective-permute-start.6) | collective-permute-done | bytes 8224 | tf_op jit(solution)/shard_map/ppermute | solution.py:568
  29.2 0.5 %collective-permute-start.7 = (f32[32,128]{1,0:T(8,128)S(1)}, f32[32,128]{1,0:T(8,128)S(1)}, u32[]{:S(2)}, u32[]{:S(2)}) collective-permute-start(f32[32,128]{1,0:T(8,128)S(1)} %pad_maximum_fusion.1), channel_id=1, source_target_pairs={{0,1},{1,0},{2,3},{3,2},{4,5},{5,4},{6,7},{7,6},{8,9},{9,8},{10,11... | collective-permute-start | bytes 49160 | tf_op jit(solution)/shard_map/ppermute | solution.py:568
  29.7 0.1 prepare.1.factor_ref
  29.8 0.8 %collective-permute-done.7 = f32[32,128]{1,0:T(8,128)S(1)} collective-permute-done((f32[32,128]{1,0:T(8,128)S(1)}, f32[32,128]{1,0:T(8,128)S(1)}, u32[]{:S(2)}, u32[]{:S(2)}) %collective-permute-start.7) | collective-permute-done | bytes 16416 | tf_op jit(solution)/shard_map/ppermute | solution.py:568
  30.5 0.9 %predict.1 = (f32[3,128]{1,0:T(4,128)}, f32[64,128]{1,0:T(8,128)}) custom-call(f32[64,128]{1,0:T(8,128)S(1)} %pad_maximum_fusion.coef_ref, f32[12,64,128]{2,1,0:T(8,128)S(1)} %prepare.1.factor_ref, f32[64,128]{1,0:T(8,128)S(1)} %get-tuple-element.28.resid_ref, s32[64,128]{1,0:T(8,128)S(1)} %get-tuple-element.21.knot_ref), custom_call_target="tpu_custom_call" | custom-call | tf_op jit(solution)/shard_map/predict/pallas_call | solution.py:555
  (11 shorter events, 0.1 us)
Async XLA Ops:
  3.4 1.6 %collective-permute-start = (f32[160,128]{1,0:T(8,128)S(1)}, f32[160,128]{1,0:T(8,128)S(1)}, u32[]{:S(2)}, u32[]{:S(2)}) collective-permute-start(f32[160,128]{1,0:T(8,128)S(1)} %get-tuple-element.17.mine_ref), channel_id=1, source_target_pairs={{0,1},{1,0},{2,3},{3,2},{4,5},{5,4},{6,7},{7,6},{8,9},{9,8},{10,11... | collective-permute-start | bytes 245768 | tf_op jit(solution)/shard_map/ppermute | solution.py:568
  6.4 1.4 %collective-permute-start.1 = (f32[2,112,128]{2,1,0:T(8,128)S(1)}, f32[2,112,128]{2,1,0:T(8,128)S(1)}, u32[]{:S(2)}, u32[]{:S(2)}) collective-permute-start(f32[2,112,128]{2,1,0:T(8,128)S(1)} %dynamic-slice_bitcast_fusion), channel_id=1, source_target_pairs={{0,1},{1,0},{2,3},{3,2},{4,5},{5,4},{6,7},{7,6},{8,9},{9,8},{10,11... | collective-permute-start | bytes 344072 | tf_op jit(solution)/shard_map/ppermute | solution.py:568
  7.8 4.8 %collective-permute-start.2 = (f32[1,112,128]{2,1,0:T(8,128)S(1)}, f32[1,112,128]{2,1,0:T(8,128)S(1)}, u32[]{:S(2)}, u32[]{:S(2)}) collective-permute-start(f32[1,112,128]{2,1,0:T(8,128)S(1)} %constant_dynamic-slice_fusion), channel_id=1, source_target_pairs={{0,3},{1,2},{2,1},{3,0},{4,7},{5,6},{6,5},{7,4},{8,11},{9,10},{10,... | collective-permute-start | bytes 172040 | tf_op jit(solution)/shard_map/ppermute | solution.py:568
  12.6 4.9 %collective-permute-start.3 = (f32[112,128]{1,0:T(8,128)S(1)}, f32[112,128]{1,0:T(8,128)S(1)}, u32[]{:S(2)}, u32[]{:S(2)}) collective-permute-start(f32[112,128]{1,0:T(8,128)S(1)} %add_bitcast_fusion), channel_id=1, source_target_pairs={{0,17},{1,16},{2,19},{3,18},{4,21},{5,20},{6,23},{7,22},{8,25},{9,... | collective-permute-start | bytes 172040 | tf_op jit(solution)/shard_map/ppermute | solution.py:568
  17.5 4.1 %collective-permute-start.4 = (f32[112,128]{1,0:T(8,128)S(1)}, f32[112,128]{1,0:T(8,128)S(1)}, u32[]{:S(2)}, u32[]{:S(2)}) collective-permute-start(f32[112,128]{1,0:T(8,128)S(1)} %add.37), channel_id=1, source_target_pairs={{0,9},{1,8},{2,11},{3,10},{4,13},{5,12},{6,15},{7,14},{8,1},{9,0},... | collective-permute-start | bytes 172040 | tf_op jit(solution)/shard_map/ppermute | solution.py:568
  21.6 4.1 %collective-permute-start.5 = (f32[112,128]{1,0:T(8,128)S(1)}, f32[112,128]{1,0:T(8,128)S(1)}, u32[]{:S(2)}, u32[]{:S(2)}) collective-permute-start(f32[112,128]{1,0:T(8,128)S(1)} %add.38), channel_id=1, source_target_pairs={{0,5},{1,4},{2,7},{3,6},{4,1},{5,0},{6,3},{7,2},{8,13},{9,12},{10,... | collective-permute-start | bytes 172040 | tf_op jit(solution)/shard_map/ppermute | solution.py:568
  26.0 3.1 %collective-permute-start.6 = (f32[16,128]{1,0:T(8,128)S(1)}, f32[16,128]{1,0:T(8,128)S(1)}, u32[]{:S(2)}, u32[]{:S(2)}) collective-permute-start(f32[16,128]{1,0:T(8,128)S(1)} %attitude.1), channel_id=1, source_target_pairs={{0,3},{1,2},{2,1},{3,0},{4,7},{5,6},{6,5},{7,4},{8,11},{9,10},{10,... | collective-permute-start | bytes 24584 | tf_op jit(solution)/shard_map/ppermute | solution.py:568
  29.2 1.3 %collective-permute-start.7 = (f32[32,128]{1,0:T(8,128)S(1)}, f32[32,128]{1,0:T(8,128)S(1)}, u32[]{:S(2)}, u32[]{:S(2)}) collective-permute-start(f32[32,128]{1,0:T(8,128)S(1)} %pad_maximum_fusion.1), channel_id=1, source_target_pairs={{0,1},{1,0},{2,3},{3,2},{4,5},{5,4},{6,7},{7,6},{8,9},{9,8},{10,11... | collective-permute-start | bytes 49160 | tf_op jit(solution)/shard_map/ppermute | solution.py:568

commit v10 on v8

--- a/solution.py
+++ b/solution.py
@@ -399,7 +399,7 @@
     def left_of(t):
         axes = tile_of(tiled_axis, t)
         splines = tile_of(splines_ref, t)
-        return stacked_parts([pick_rows(axes, x) * pick_rows(splines, j) for x, j in zip(axes_of, splines_of)], split3)
+        return stacked_parts([pick_rows(axes, x) * pick_rows(splines, j) for x, j in zip(axes_of, splines_of)], split2)
 
     def group(start, steps):
         for part in range(steps // SUB):
@@ -419,7 +419,7 @@
             scaled = weight_ref[at, :] * resid
             for j, basis in enumerate(spline_basis(phase_ref[at, :])):
                 splines_ref[across(start + part * SUB, j), :] = basis * scaled
-        add_blocks(moments, start, steps, rep, rows, 3, left_of, knot_ref)
+        add_blocks(moments, start, steps, rep, rows, 2, left_of, knot_ref)
 
     if rep > math.gcd(tiles, 64):
         moments[...] = jnp.zeros_like(moments)

time: 31.7 us -> 31.7 us (level)
  no operation moved by 1% of the time
where the time goes in v10:
time: 31.7 us; the launch traced here: 31.5 us
  starting transfers between devices  12.8 us (40%)
  waiting for transfers between devices  11.5 us (36%)
  Pallas kernels  6.45 us (20%)
  between operations  0.72 us (2%)
    ppermute x8, starting transfers between devices, swapped(): return lax.ppermute(value, axis, [(i, i ^ bit) for i in range(size)])  12.8 us
    ppermute x8, waiting for transfers between devices, swapped(): return lax.ppermute(value, axis, [(i, i ^ bit) for i in range(size)])  11.5 us
    pallas_call x6, Pallas kernels, call(): pl.pallas_call(kernel, name=name, out_shape=outs, in_specs=[SMEM] * len(s...  6.45 us
  transfers between devices with their start and end apart: 8, of which 7 were waited for; matrix products, arithmetic and copies ran while one was open for 0% of the time, Pallas kernels for 4%

profile of v10, /device:TPU:0, one launch (start us, length us, event | category | flops | bytes accessed | tf_op | source)
XLA Modules:
  0.0 31.5 jit_solution(1632259692365004756)
XLA Ops:
  0.6 2.8 %source_sums.1 = (f32[20,8,128]{2,1,0:T(8,128)S(1)}, f32[64,128]{1,0:T(8,128)S(1)}, f32[64,128]{1,0:T(8,128)S(1)}, s32[64,128]{1,0:T(8,128)S(1)}, f32[64,128]{1,...) custom-call(s32[1,1,16]{2,1,0:T(1,128)} %counts_hbm.1, ...), custom_call_target="tpu_custom_call" | custom-call | tf_op jit(solution)/shard_map/source_sums/pallas_call | solution.py:549
  3.5 0.6 %collective-permute-start = (f32[20,8,128]{2,1,0:T(8,128)S(1)}, f32[20,8,128]{2,1,0:T(8,128)S(1)}, u32[]{:S(2)}, u32[]{:S(2)}) collective-permute-start(f32[20,8,128]{2,1,0:T(8,128)S(1)} %get-tuple-element.17.mine_ref), channel_id=1, source_target_pairs={{0,1},{1,0},{2,3},{3,2},{4,5},{5,4},{6,7},{7,6},{8,9},{9,8},{10,11... | collective-permute-start | bytes 245768 | tf_op jit(solution)/shard_map/ppermute | solution.py:562
  4.0 1.1 %band_sums.1.band_ref = f32[384,128]{1,0:T(8,128)S(1)} custom-call(f32[64,128]{1,0:T(8,128)S(1)} %get-tuple-element.18.phase_ref, f32[3,8192]{1,0:T(4,128)S(1)} %get-tuple-element.19.axis_ref, f32[64,128]{1,0:T(8,128)S(1)} %get-tuple-element.20.weight_ref, s32[64,128]{1,0:T(8,128)S(1)} %get-tuple-element.21.knot_ref), custom_call_target="tpu_custom_call" | custom-call | tf_op jit(solution)/shard_map/band_sums/pallas_call | solution.py:549
  5.1 0.0 collective-permute-done.other_ref
  5.1 1.2 %residuals.1 = (f32[5,1024]{1,0:T(8,128)}, f32[64,128]{1,0:T(8,128)S(1)}, f32[4,112,128]{2,1,0:T(8,128)S(1)}) custom-call(f32[20,8,128]{2,1,0:T(8,128)S(1)} %get-tuple-element.17.mine_ref, f32[20,8,128]{2,1,0:T(8,128)S(1)} %collective-permute-done.other_ref, f32[384,128]{1,0:T(8,128)S(1)} %band_sums.1.band_ref, f32[64,128]{1,0:T(8,128)S(1)} %get-tuple-element.22.live_ref, ...), custom_call_target="tpu_custom_call" | custom-call | tf_op jit(solution)/shard_map/residuals/pallas_call | solution.py:549
  6.4 0.2 collective-permute-start.1
  6.7 1.2 %collective-permute-done.1 = f32[2,112,128]{2,1,0:T(8,128)S(1)} collective-permute-done((f32[2,112,128]{2,1,0:T(8,128)S(1)}, f32[2,112,128]{2,1,0:T(8,128)S(1)}, u32[]{:S(2)}, u32[]{:S(2)}) %collective-permute-start.1) | collective-permute-done | bytes 114720 | tf_op jit(solution)/shard_map/ppermute | solution.py:562
  7.9 2.7 %collective-permute-start.2 = (f32[1,112,128]{2,1,0:T(8,128)S(1)}, f32[1,112,128]{2,1,0:T(8,128)S(1)}, u32[]{:S(2)}, u32[]{:S(2)}) collective-permute-start(f32[1,112,128]{2,1,0:T(8,128)S(1)} %constant_dynamic-slice_fusion), channel_id=1, source_target_pairs={{0,3},{1,2},{2,1},{3,0},{4,7},{5,6},{6,5},{7,4},{8,11},{9,10},{10,... | collective-permute-start | bytes 172040 | tf_op jit(solution)/shard_map/ppermute | solution.py:562
  10.5 2.1 %collective-permute-done.2 = f32[1,112,128]{2,1,0:T(8,128)S(1)} collective-permute-done((f32[1,112,128]{2,1,0:T(8,128)S(1)}, f32[1,112,128]{2,1,0:T(8,128)S(1)}, u32[]{:S(2)}, u32[]{:S(2)}) %collective-permute-start.2) | collective-permute-done | bytes 57376 | tf_op jit(solution)/shard_map/ppermute | solution.py:562
  12.7 2.7 %collective-permute-start.3 = (f32[112,128]{1,0:T(8,128)S(1)}, f32[112,128]{1,0:T(8,128)S(1)}, u32[]{:S(2)}, u32[]{:S(2)}) collective-permute-start(f32[112,128]{1,0:T(8,128)S(1)} %add_bitcast_fusion), channel_id=1, source_target_pairs={{0,17},{1,16},{2,19},{3,18},{4,21},{5,20},{6,23},{7,22},{8,25},{9,... | collective-permute-start | bytes 172040 | tf_op jit(solution)/shard_map/ppermute | solution.py:562
  15.4 2.1 %collective-permute-done.3 = f32[112,128]{1,0:T(8,128)S(1)} collective-permute-done((f32[112,128]{1,0:T(8,128)S(1)}, f32[112,128]{1,0:T(8,128)S(1)}, u32[]{:S(2)}, u32[]{:S(2)}) %collective-permute-start.3) | collective-permute-done | bytes 57376 | tf_op jit(solution)/shard_map/ppermute | solution.py:562
  17.5 2.0 %collective-permute-start.4 = (f32[112,128]{1,0:T(8,128)S(1)}, f32[112,128]{1,0:T(8,128)S(1)}, u32[]{:S(2)}, u32[]{:S(2)}) collective-permute-start(f32[112,128]{1,0:T(8,128)S(1)} %add.37), channel_id=1, source_target_pairs={{0,9},{1,8},{2,11},{3,10},{4,13},{5,12},{6,15},{7,14},{8,1},{9,0},... | collective-permute-start | bytes 172040 | tf_op jit(solution)/shard_map/ppermute | solution.py:562
  19.6 2.1 %collective-permute-done.4 = f32[112,128]{1,0:T(8,128)S(1)} collective-permute-done((f32[112,128]{1,0:T(8,128)S(1)}, f32[112,128]{1,0:T(8,128)S(1)}, u32[]{:S(2)}, u32[]{:S(2)}) %collective-permute-start.4) | collective-permute-done | bytes 57376 | tf_op jit(solution)/shard_map/ppermute | solution.py:562
  21.6 2.3 %collective-permute-start.5 = (f32[112,128]{1,0:T(8,128)S(1)}, f32[112,128]{1,0:T(8,128)S(1)}, u32[]{:S(2)}, u32[]{:S(2)}) collective-permute-start(f32[112,128]{1,0:T(8,128)S(1)} %add.38), channel_id=1, source_target_pairs={{0,5},{1,4},{2,7},{3,6},{4,1},{5,0},{6,3},{7,2},{8,13},{9,12},{10,... | collective-permute-start | bytes 172040 | tf_op jit(solution)/shard_map/ppermute | solution.py:562
  23.9 1.9 %collective-permute-done.5 = f32[112,128]{1,0:T(8,128)S(1)} collective-permute-done((f32[112,128]{1,0:T(8,128)S(1)}, f32[112,128]{1,0:T(8,128)S(1)}, u32[]{:S(2)}, u32[]{:S(2)}) %collective-permute-start.5) | collective-permute-done | bytes 57376 | tf_op jit(solution)/shard_map/ppermute | solution.py:562
  25.8 0.3 attitude.1
  26.0 1.8 %collective-permute-start.6 = (f32[16,128]{1,0:T(8,128)S(1)}, f32[16,128]{1,0:T(8,128)S(1)}, u32[]{:S(2)}, u32[]{:S(2)}) collective-permute-start(f32[16,128]{1,0:T(8,128)S(1)} %attitude.1), channel_id=1, source_target_pairs={{0,3},{1,2},{2,1},{3,0},{4,7},{5,6},{6,5},{7,4},{8,11},{9,10},{10,... | collective-permute-start | bytes 24584 | tf_op jit(solution)/shard_map/ppermute | solution.py:562
  27.8 1.4 %collective-permute-done.6 = f32[16,128]{1,0:T(8,128)S(1)} collective-permute-done((f32[16,128]{1,0:T(8,128)S(1)}, f32[16,128]{1,0:T(8,128)S(1)}, u32[]{:S(2)}, u32[]{:S(2)}) %collective-permute-start.6) | collective-permute-done | bytes 8224 | tf_op jit(solution)/shard_map/ppermute | solution.py:562
  29.2 0.5 %collective-permute-start.7 = (f32[32,128]{1,0:T(8,128)S(1)}, f32[32,128]{1,0:T(8,128)S(1)}, u32[]{:S(2)}, u32[]{:S(2)}) collective-permute-start(f32[32,128]{1,0:T(8,128)S(1)} %pad_maximum_fusion.1), channel_id=1, source_target_pairs={{0,1},{1,0},{2,3},{3,2},{4,5},{5,4},{6,7},{7,6},{8,9},{9,8},{10,11... | collective-permute-start | bytes 49160 | tf_op jit(solution)/shard_map/ppermute | solution.py:562
  29.7 0.1 prepare.1.factor_ref
  29.8 0.8 %collective-permute-done.7 = f32[32,128]{1,0:T(8,128)S(1)} collective-permute-done((f32[32,128]{1,0:T(8,128)S(1)}, f32[32,128]{1,0:T(8,128)S(1)}, u32[]{:S(2)}, u32[]{:S(2)}) %collective-permute-start.7) | collective-permute-done | bytes 16416 | tf_op jit(solution)/shard_map/ppermute | solution.py:562
  30.6 0.9 %predict.1 = (f32[3,128]{1,0:T(4,128)}, f32[64,128]{1,0:T(8,128)}) custom-call(f32[16,4,128]{2,1,0:T(4,128)S(1)} %bitcast.16, f32[12,64,128]{2,1,0:T(8,128)S(1)} %prepare.1.factor_ref, f32[64,128]{1,0:T(8,128)S(1)} %get-tuple-element.28.resid_ref, s32[64,128]{1,0:T(8,128)S(1)} %get-tuple-element.21.knot_ref), custom_call_target="tpu_custom_call" | custom-call | tf_op jit(solution)/shard_map/predict/pallas_call | solution.py:549
  (11 shorter events, 0.1 us)
Async XLA Ops:
  3.5 1.7 %collective-permute-start = (f32[20,8,128]{2,1,0:T(8,128)S(1)}, f32[20,8,128]{2,1,0:T(8,128)S(1)}, u32[]{:S(2)}, u32[]{:S(2)}) collective-permute-start(f32[20,8,128]{2,1,0:T(8,128)S(1)} %get-tuple-element.17.mine_ref), channel_id=1, source_target_pairs={{0,1},{1,0},{2,3},{3,2},{4,5},{5,4},{6,7},{7,6},{8,9},{9,8},{10,11... | collective-permute-start | bytes 245768 | tf_op jit(solution)/shard_map/ppermute | solution.py:562
  6.4 1.4 %collective-permute-start.1 = (f32[2,112,128]{2,1,0:T(8,128)S(1)}, f32[2,112,128]{2,1,0:T(8,128)S(1)}, u32[]{:S(2)}, u32[]{:S(2)}) collective-permute-start(f32[2,112,128]{2,1,0:T(8,128)S(1)} %dynamic-slice_bitcast_fusion), channel_id=1, source_target_pairs={{0,1},{1,0},{2,3},{3,2},{4,5},{5,4},{6,7},{7,6},{8,9},{9,8},{10,11... | collective-permute-start | bytes 344072 | tf_op jit(solution)/shard_map/ppermute | solution.py:562
  7.9 4.8 %collective-permute-start.2 = (f32[1,112,128]{2,1,0:T(8,128)S(1)}, f32[1,112,128]{2,1,0:T(8,128)S(1)}, u32[]{:S(2)}, u32[]{:S(2)}) collective-permute-start(f32[1,112,128]{2,1,0:T(8,128)S(1)} %constant_dynamic-slice_fusion), channel_id=1, source_target_pairs={{0,3},{1,2},{2,1},{3,0},{4,7},{5,6},{6,5},{7,4},{8,11},{9,10},{10,... | collective-permute-start | bytes 172040 | tf_op jit(solution)/shard_map/ppermute | solution.py:562
  12.7 4.9 %collective-permute-start.3 = (f32[112,128]{1,0:T(8,128)S(1)}, f32[112,128]{1,0:T(8,128)S(1)}, u32[]{:S(2)}, u32[]{:S(2)}) collective-permute-start(f32[112,128]{1,0:T(8,128)S(1)} %add_bitcast_fusion), channel_id=1, source_target_pairs={{0,17},{1,16},{2,19},{3,18},{4,21},{5,20},{6,23},{7,22},{8,25},{9,... | collective-permute-start | bytes 172040 | tf_op jit(solution)/shard_map/ppermute | solution.py:562
  17.5 4.1 %collective-permute-start.4 = (f32[112,128]{1,0:T(8,128)S(1)}, f32[112,128]{1,0:T(8,128)S(1)}, u32[]{:S(2)}, u32[]{:S(2)}) collective-permute-start(f32[112,128]{1,0:T(8,128)S(1)} %add.37), channel_id=1, source_target_pairs={{0,9},{1,8},{2,11},{3,10},{4,13},{5,12},{6,15},{7,14},{8,1},{9,0},... | collective-permute-start | bytes 172040 | tf_op jit(solution)/shard_map/ppermute | solution.py:562
  21.6 4.1 %collective-permute-start.5 = (f32[112,128]{1,0:T(8,128)S(1)}, f32[112,128]{1,0:T(8,128)S(1)}, u32[]{:S(2)}, u32[]{:S(2)}) collective-permute-start(f32[112,128]{1,0:T(8,128)S(1)} %add.38), channel_id=1, source_target_pairs={{0,5},{1,4},{2,7},{3,6},{4,1},{5,0},{6,3},{7,2},{8,13},{9,12},{10,... | collective-permute-start | bytes 172040 | tf_op jit(solution)/shard_map/ppermute | solution.py:562
  26.0 3.1 %collective-permute-start.6 = (f32[16,128]{1,0:T(8,128)S(1)}, f32[16,128]{1,0:T(8,128)S(1)}, u32[]{:S(2)}, u32[]{:S(2)}) collective-permute-start(f32[16,128]{1,0:T(8,128)S(1)} %attitude.1), channel_id=1, source_target_pairs={{0,3},{1,2},{2,1},{3,0},{4,7},{5,6},{6,5},{7,4},{8,11},{9,10},{10,... | collective-permute-start | bytes 24584 | tf_op jit(solution)/shard_map/ppermute | solution.py:562
  29.2 1.4 %collective-permute-start.7 = (f32[32,128]{1,0:T(8,128)S(1)}, f32[32,128]{1,0:T(8,128)S(1)}, u32[]{:S(2)}, u32[]{:S(2)}) collective-permute-start(f32[32,128]{1,0:T(8,128)S(1)} %pad_maximum_fusion.1), channel_id=1, source_target_pairs={{0,1},{1,0},{2,3},{3,2},{4,5},{5,4},{6,7},{7,6},{8,9},{9,8},{10,11... | collective-permute-start | bytes 49160 | tf_op jit(solution)/shard_map/ppermute | solution.py:562
